TPU v7x, 256 devices: a whole 4x4x8 slice. The times are simulated.
256 devices in a mesh: tm: 4 (over z_lo, core), vocab: 64 (over x, y, z_hi).
Axes of the slice: x: 4, y: 4, z: 8 (z_hi: 4, z_lo: 2; z = z_hi * 2 + z_lo), core: 2. Of those that a mesh axis runs over, the one named last changes fastest.
Arguments:
- frames: bfloat16 [6144, 1024], P(('tm', 'vocab')), may hold values from -6 to 6
- qkv_weight: bfloat16 [1024, 3072], replicated, may hold values from -0.375 to 0.375
- attn_out_weight: bfloat16 [1024, 1024], replicated, may hold values from -0.1875 to 0.1875
- head_weight: bfloat16 [1024, 131072], P('tm', 'vocab'), may hold values from -0.5 to 0.5
- back_weight: bfloat16 [131072, 1024], P('vocab', 'tm'), may hold values from -6 to 6
Outputs:
- conditioned: bfloat16 [6144, 1024], P(('tm', 'vocab'))
- log_norm: float32 [6144], P(('tm', 'vocab'))
All inputs are finite; a program needn't handle non-finite values.
Results may differ from a plain program's by a relative error of at most 0.017.
The roundings to bfloat16 on the way count: a program that leaves them out, or rounds other values in their place, can miss the bound.
Values may be sent and summed in bfloat16 or wider, within the bound.
No kernel may reach another device: no remote copies, remote signals or barrier semaphores. Data moves between devices by JAX's collectives and lax.ppermute only.
A program may use at most 128 MiB of HBM per device.

v0:
```python
import math

import jax
import jax.numpy as jnp
from jax import lax
from jax.sharding import PartitionSpec as P

HEADS = 16
HEAD_DIM = 64
WIN = 128


def passed_along(block, axis, distance):
    devices = range(lax.axis_size(axis))
    route = [(i - distance, i) for i in devices if i - distance in devices]
    return lax.ppermute(block, axis, route)


def root_norm(values):
    return values * lax.rsqrt(jnp.mean(values * values, axis=-1, keepdims=True) + 1e-06)


def body(frames, qkv_weight, attn_out_weight, head_weight, back_weight):
    frame_rows = frames.shape[0]
    model_width = frames.shape[1]
    full_head = lax.all_gather(head_weight, "tm", axis=0, tiled=True)
    normed = root_norm(frames.astype(jnp.float32)).astype(jnp.bfloat16)
    project = jnp.dot(normed, qkv_weight, preferred_element_type=jnp.float32).astype(jnp.bfloat16)
    query = project[:, :model_width].reshape(frame_rows, HEADS, HEAD_DIM)
    own_pairs = project[:, model_width:]
    hop_count = (WIN + frame_rows - 1) // frame_rows
    past_blocks = []
    for hop_step in range(1, hop_count + 1):
        past_blocks.append(passed_along(own_pairs, ("tm", "vocab"), hop_step))
    key_rows = jnp.concatenate(past_blocks[::-1] + [own_pairs], axis=0)
    key_count = key_rows.shape[0]
    key_part = key_rows[:, :model_width].reshape(key_count, HEADS, HEAD_DIM)
    value_part = key_rows[:, model_width:].reshape(key_count, HEADS, HEAD_DIM)
    device_pos = lax.axis_index(("tm", "vocab"))
    query_pos = device_pos * frame_rows + jnp.arange(frame_rows, dtype=jnp.int32)
    key_pos = (device_pos - hop_count) * frame_rows + jnp.arange(key_count, dtype=jnp.int32)
    scores = jnp.einsum(
        "qhd,khd->hqk", query, key_part, preferred_element_type=jnp.float32
    ) / math.sqrt(HEAD_DIM)
    scores = 50.0 * jnp.tanh(scores / 50.0)
    allowed = (
        (key_pos[None, :] <= query_pos[:, None])
        & (key_pos[None, :] > query_pos[:, None] - WIN)
        & (key_pos[None, :] >= 0)
    )
    expo = jnp.where(allowed[None], jnp.exp(scores), 0.0)
    weights = (expo / jnp.sum(expo, axis=-1, keepdims=True)).astype(jnp.bfloat16)
    context = jnp.einsum("hqk,khd->qhd", weights, value_part, preferred_element_type=jnp.float32)
    context = context.astype(jnp.bfloat16).reshape(frame_rows, model_width)
    hidden = (
        frames.astype(jnp.float32)
        + jnp.dot(context, attn_out_weight, preferred_element_type=jnp.float32)
    ).astype(jnp.bfloat16)
    unit = root_norm(hidden.astype(jnp.float32)).astype(jnp.bfloat16)
    logits = jnp.dot(
        lax.all_gather(unit, "vocab", axis=0, tiled=True),
        full_head,
        preferred_element_type=jnp.float32,
    )
    label_probs = jnp.exp(30.0 * jnp.tanh(logits / 30.0)).astype(jnp.bfloat16)
    local_totals = jnp.sum(label_probs.astype(jnp.float32), axis=-1)
    partial_value = jnp.dot(
        label_probs,
        lax.all_gather(back_weight, "tm", axis=1, tiled=True),
        preferred_element_type=jnp.float32,
    )
    totals = lax.psum(local_totals, "vocab")
    summed = lax.psum(partial_value / totals[:, None], "vocab")
    offset = lax.axis_index("vocab") * frame_rows
    back_proj = lax.dynamic_slice_in_dim(summed, offset, frame_rows, 0)
    owned_totals = lax.dynamic_slice_in_dim(totals, offset, frame_rows, 0)
    center = back_proj - jnp.mean(back_proj, axis=-1, keepdims=True)
    spread = jnp.mean(center * center, axis=-1, keepdims=True)
    conditioned = (hidden.astype(jnp.float32) + center * lax.rsqrt(spread + 1e-05)).astype(
        jnp.bfloat16
    )
    return (conditioned, jnp.log(owned_totals))


def solution(mesh):
    return jax.shard_map(
        body,
        mesh=mesh,
        in_specs=(P(("tm", "vocab"), None), P(), P(), P("tm", "vocab"), P("vocab", "tm")),
        out_specs=(P(("tm", "vocab"), None), P(("tm", "vocab"))),
        check_vma=False,
    )
```

profile of v0, /device:TPU:32, one launch (start us, length us, event | category | flops | bytes accessed | tf_op | source)
XLA Modules:
  0.0 1142.8 jit_solution(6416594148082275547)
XLA Ops:
  8.0 0.9 fusion.9
  8.9 3.8 convolution_convert_fusion
  12.7 9.2 collective-permute-start
  21.9 4.4 collective-permute-start.1
  26.3 3.2 collective-permute-start.2
  29.5 5.2 collective-permute-start.3
  34.7 2.6 collective-permute-start.4
  37.4 0.8 reshape.133
  38.2 4.0 collective-permute-start.5
  42.3 8.4 collective-permute-done.4
  50.6 4.6 collective-permute-done.5
  55.7 1.9 fusion.3
  57.6 1.4 fusion.4
  59.7 0.7 multiply_convert_fusion
  60.5 0.7 all-gather.8.cloned.1.call-update
  61.3 12.6 %all-gather.6.cloned.1.call-done = bf16[1024,2048]{1,0:T(8,128)(2,1)} async-done(((bf16[256,2048]{1,0:T(8,128)(2,1)}), bf16[1024,2048]{1,0:T(8,128)(2,1)}) %all-gather.6.cloned.1.call-update) | async-done | bytes 4194320 | tf_op jit(solution)/shard_map/all_gather | solution.py:26
  73.8 84.2 %all-gather.4.cloned.1.call-done = bf16[1536,1024]{1,0:T(8,128)(2,1)} async-done(((bf16[24,1024]{1,0:T(8,128)(2,1)}), bf16[1536,1024]{1,0:T(8,128)(2,1)}) %all-gather.4.cloned.1.call-update) | async-done | bytes 3145744 | tf_op jit(solution)/shard_map/all_gather | solution.py:61
  158.0 12.5 %convert_reduce_fusion = (f32[1536]{0:T(1024)S(1)}, bf16[1536,2048]{1,0:T(8,128)(2,1)}) fusion(bf16[1536,1024]{1,0:T(8,128)(2,1)} %all-gather.4.cloned.1.call-done, bf16[1024,2048]{1,0:T(8,128)(2,1)} %all-gather.6.cloned.1.call-done), kind=kOutput, calls=%fused_computation | convolution fusion | flops 6458178048 | bytes 13637632 | tf_op jit(solution)/shard_map/dot_general | solution.py:60
  170.5 195.5 %psum.14 = f32[1536]{0:T(1024)S(1)} all-reduce(f32[1536]{0:T(1024)S(1)} %get-tuple-element.6), channel_id=1, replica_groups=mesh['tm'=4,'vocab'=64] {'vocab'}, use_global_device_ids=true, to_apply=%region_4.5 | all-reduce | flops 1536 | bytes 12288 | tf_op jit(solution)/shard_map/psum | solution.py:72
  366.0 11.6 %convolution_divide_fusion = f32[1536,1024]{1,0:T(8,128)} fusion(bf16[1536,2048]{1,0:T(8,128)(2,1)} %get-tuple-element.7, bf16[2048,1024]{1,0:T(8,128)(2,1)} %all-gather.8.cloned.1.call-done, f32[1536]{0:T(1024)S(1)} %psum.14), kind=kOutput, calls=%fused_computation.2 | convolution fusion | flops 6444023808 | bytes 16783360 | tf_op jit(solution)/shard_map/dot_general | solution.py:67
  378.3 754.3 %all-reduce.2.cloned.1.call-done = f32[1536,1024]{1,0:T(8,128)} async-done(((f32[1536,1024]{1,0:T(8,128)}), f32[1536,1024]{1,0:T(8,128)}) %all-reduce.2.cloned.1.call-update) | async-done | bytes 6291472 | tf_op jit(solution)/shard_map/psum | solution.py:73
  1132.6 1.0 dynamic-slice_reduce_fusion
  1133.6 1.1 multiply_reduce_fusion
  1134.7 1.6 add_convert_fusion
  (40 shorter events, 2.8 us)
Async XLA Ops:
  7.2 52.0 %copy-start = (bf16[1024,1024]{1,0:T(8,128)(2,1)S(1)}, bf16[1024,1024]{1,0:T(8,128)(2,1)}, u32[]{:S(2)}) copy-start(bf16[1024,1024]{1,0:T(8,128)(2,1)} %param.7) | copy-start | bytes 6291460
  7.2 66.6 %all-gather.6.cloned.1.call-start = ((), (), s32[]{:S(2)}) async-start(), calls=%async_computation.1 | async-start | bytes 5242880 | tf_op jit(solution)/shard_map/all_gather | solution.py:26
  7.9 150.1 %all-gather.4.cloned.1.call-start = ((), (), s32[]{:S(2)}) async-start(), calls=%async_computation | async-start | bytes 3194880 | tf_op jit(solution)/shard_map/all_gather | solution.py:61
  8.9 50.3 %copy-start.1 = (bf16[24,1024]{1,0:T(8,128)(2,1)S(1)}, bf16[24,1024]{1,0:T(8,128)(2,1)}, u32[]{:S(2)}) copy-start(bf16[24,1024]{1,0:T(8,128)(2,1)} %param.5) | copy-start | bytes 147460
  12.7 25.5 %collective-permute-start = (bf16[24,2048]{1,0:T(8,128)(2,1)S(1)}, bf16[24,2048]{1,0:T(8,128)(2,1)S(1)}, u32[]{:S(2)}, u32[]{:S(2)}) collective-permute-start(bf16[24,2048]{1,0:T(8,128)(2,1)S(1)} %slice.16), channel_id=1, source_target_pairs={{0,6},{1,7},{2,8},{3,9},{4,10},{5,11},{6,12},{7,13},{8,14},{9,15},... | collective-permute-start | bytes 294920 | tf_op jit(solution)/shard_map/ppermute | solution.py:16
  21.9 20.2 %collective-permute-start.1 = (bf16[24,2048]{1,0:T(8,128)(2,1)S(1)}, bf16[24,2048]{1,0:T(8,128)(2,1)S(1)}, u32[]{:S(2)}, u32[]{:S(2)}) collective-permute-start(bf16[24,2048]{1,0:T(8,128)(2,1)S(1)} %slice.16), channel_id=1, source_target_pairs={{0,5},{1,6},{2,7},{3,8},{4,9},{5,10},{6,11},{7,12},{8,13},{9,14},{... | collective-permute-start | bytes 294920 | tf_op jit(solution)/shard_map/ppermute | solution.py:16
  26.3 15.9 %collective-permute-start.2 = (bf16[24,2048]{1,0:T(8,128)(2,1)S(1)}, bf16[24,2048]{1,0:T(8,128)(2,1)S(1)}, u32[]{:S(2)}, u32[]{:S(2)}) collective-permute-start(bf16[24,2048]{1,0:T(8,128)(2,1)S(1)} %slice.16), channel_id=1, source_target_pairs={{0,4},{1,5},{2,6},{3,7},{4,8},{5,9},{6,10},{7,11},{8,12},{9,13},{1... | collective-permute-start | bytes 294920 | tf_op jit(solution)/shard_map/ppermute | solution.py:16
  29.5 12.7 %collective-permute-start.3 = (bf16[24,2048]{1,0:T(8,128)(2,1)S(1)}, bf16[24,2048]{1,0:T(8,128)(2,1)S(1)}, u32[]{:S(2)}, u32[]{:S(2)}) collective-permute-start(bf16[24,2048]{1,0:T(8,128)(2,1)S(1)} %slice.16), channel_id=1, source_target_pairs={{0,3},{1,4},{2,5},{3,6},{4,7},{5,8},{6,9},{7,10},{8,11},{9,12},{10... | collective-permute-start | bytes 294920 | tf_op jit(solution)/shard_map/ppermute | solution.py:16
  34.7 15.9 %collective-permute-start.4 = (bf16[24,2048]{1,0:T(8,128)(2,1)S(1)}, bf16[24,2048]{1,0:T(8,128)(2,1)S(1)}, u32[]{:S(2)}, u32[]{:S(2)}) collective-permute-start(bf16[24,2048]{1,0:T(8,128)(2,1)S(1)} %slice.16), channel_id=1, source_target_pairs={{0,2},{1,3},{2,4},{3,5},{4,6},{5,7},{6,8},{7,9},{8,10},{9,11},{10,... | collective-permute-start | bytes 294920 | tf_op jit(solution)/shard_map/ppermute | solution.py:16
  38.2 17.0 %collective-permute-start.5 = (bf16[24,2048]{1,0:T(8,128)(2,1)S(1)}, bf16[24,2048]{1,0:T(8,128)(2,1)S(1)}, u32[]{:S(2)}, u32[]{:S(2)}) collective-permute-start(bf16[24,2048]{1,0:T(8,128)(2,1)S(1)} %slice.16), channel_id=1, source_target_pairs={{0,1},{1,2},{2,3},{3,4},{4,5},{5,6},{6,7},{7,8},{8,9},{9,10},{10,1... | collective-permute-start | bytes 294920 | tf_op jit(solution)/shard_map/ppermute | solution.py:16
  60.5 305.5 %all-gather.8.cloned.1.call-start = ((), (), s32[]{:S(2)}) async-start(), calls=%async_computation.2 | async-start | bytes 5242880 | tf_op jit(solution)/shard_map/all_gather | solution.py:69
  61.2 1071.3 %all-reduce.2.cloned.1.call-start = ((), (), s32[]{:S(2)}) async-start(), calls=%async_computation.3 | async-start | bytes 12582912 | tf_op jit(solution)/shard_map/psum | solution.py:73
Sparse Core Ops, SparseCore 0:
  9.8 63.9 all-gather.5
  77.7 80.2 all-gather.3
  159.8 48.5 all-gather.7
  377.8 754.7 all-reduce.1
where the time goes:
time: 1140 us
  waiting for transfers between devices  865 us (76%)
  blocking collectives  195 us (17%)
  matrix products  31.8 us (3%)
  starting transfers between devices  28.6 us (3%)
  between operations  14 us (1%)
    psum x1, waiting for transfers between devices, body(): summed = lax.psum(partial_value / totals[:, None], 'vocab')  754 us
    psum x1, blocking collectives, body(): totals = lax.psum(local_totals, 'vocab')  195 us
    all_gather x1, waiting for transfers between devices, body(): lax.all_gather(unit, 'vocab', axis=0, tiled=True)  84.2 us
    ppermute x6, starting transfers between devices, passed_along(): return lax.ppermute(block, axis, route)  28.5 us
  transfers between devices with their start and end apart: 10, of which 5 were waited for; matrix products, arithmetic and copies ran while one was open for 2% of the time, Pallas kernels for 0%

commit v1 on v0

v1 whole, which is shorter than its diff:
```python
import math

import jax
import jax.numpy as jnp
from jax import lax
from jax.sharding import Mesh, PartitionSpec as P

HEADS = 16
HEAD_DIM = 64
WIN = 128
BF = jnp.bfloat16
F32 = jnp.float32
TIME = ("zl", "c")
PLANE = ("x", "y")
COL = "zh"
BLOCKS = TIME + PLANE
EVERY = BLOCKS + (COL,)


def gathered(block, axes):
    size = lax.axis_size(axes)
    copies = lax.optimization_barrier(jnp.broadcast_to(block[None], (size,) + block.shape))
    parts = lax.all_to_all(copies, axes, 0, 0)
    return parts.reshape((size * block.shape[0],) + block.shape[1:])


def passed_along(block, axes, distance):
    devices = range(lax.axis_size(axes))
    route = [(i, i + distance) for i in devices if i + distance in devices]
    return lax.ppermute(block, axes, route)


def root_norm(values):
    return values * lax.rsqrt(jnp.mean(values * values, axis=-1, keepdims=True) + 1e-06)


def body(frames, qkv_weight, attn_out_weight, head_weight, back_weight):
    rows = frames.shape[0]
    width = frames.shape[1]
    planes = lax.axis_size(PLANE)
    cols = lax.axis_size(COL)
    block = rows * cols
    far = WIN - block
    full_head = lax.all_gather(head_weight, TIME, axis=0, tiled=True)
    full_back = lax.all_gather(back_weight, TIME, axis=1, tiled=True)

    own = gathered(frames, COL)
    prev = passed_along(own, BLOCKS, 1)
    prev2 = passed_along(own[block - far :], BLOCKS, 2)
    keys = WIN + block
    normed = root_norm(jnp.concatenate([prev2, prev, own], axis=0).astype(F32)).astype(BF)
    project = jnp.dot(normed, qkv_weight, preferred_element_type=F32).astype(BF)
    query = project[WIN:, :width].reshape(block, HEADS, HEAD_DIM)
    key_part = project[:, width : 2 * width].reshape(keys, HEADS, HEAD_DIM)
    value_part = project[:, 2 * width :].reshape(keys, HEADS, HEAD_DIM)
    first = lax.axis_index(BLOCKS) * block
    query_pos = first + jnp.arange(block, dtype=jnp.int32)
    key_pos = first - WIN + jnp.arange(keys, dtype=jnp.int32)
    scores = jnp.einsum(
        "qhd,khd->hqk", query, key_part, preferred_element_type=F32
    ) / math.sqrt(HEAD_DIM)
    scores = 50.0 * jnp.tanh(scores / 50.0)
    allowed = (
        (key_pos[None, :] <= query_pos[:, None])
        & (key_pos[None, :] > query_pos[:, None] - WIN)
        & (key_pos[None, :] >= 0)
    )
    expo = jnp.where(allowed[None], jnp.exp(scores), 0.0)
    weights = (expo / jnp.sum(expo, axis=-1, keepdims=True)).astype(BF)
    context = jnp.einsum("hqk,khd->qhd", weights, value_part, preferred_element_type=F32)
    context = context.astype(BF).reshape(block, width)
    hidden = (
        own.astype(F32) + jnp.dot(context, attn_out_weight, preferred_element_type=F32)
    ).astype(BF)
    unit = root_norm(hidden.astype(F32)).astype(BF)

    logits = jnp.dot(gathered(unit, PLANE), full_head, preferred_element_type=F32)
    label_probs = jnp.exp(30.0 * jnp.tanh(logits / 30.0)).astype(BF)
    totals = jnp.sum(label_probs.astype(F32), axis=-1)
    partial = jnp.dot(label_probs, full_back, preferred_element_type=F32)

    high = lax.reduce_precision(totals, 8, 7)
    mid = lax.reduce_precision(totals - high, 8, 7)
    low = totals - high - mid
    split = jnp.stack([high, mid, low]).astype(BF).reshape(3, planes, block)
    split = jnp.pad(split.transpose(1, 0, 2), ((0, 0), (0, 5), (0, width - block)))
    sent = jnp.concatenate([partial.astype(BF).reshape(planes, block, width), split], axis=1)
    summed = jnp.sum(lax.all_to_all(sent, PLANE, 0, 0).astype(F32), axis=0)
    block_totals = jnp.sum(summed[block : block + 3, :block], axis=0)
    high = lax.reduce_precision(block_totals, 8, 7)
    mid = lax.reduce_precision(block_totals - high, 8, 7)
    low = block_totals - high - mid
    split = jnp.stack([high, mid, low]).astype(BF).reshape(3, cols, rows)
    split = jnp.pad(split.transpose(1, 0, 2), ((0, 0), (0, 5), (0, width - rows)))
    sent = jnp.concatenate([summed[:block].astype(BF).reshape(cols, rows, width), split], axis=1)
    summed = jnp.sum(lax.all_to_all(sent, COL, 0, 0).astype(F32), axis=0)
    owned_totals = jnp.sum(summed[rows : rows + 3, :rows], axis=0)
    back_proj = summed[:rows] / owned_totals[:, None]

    own_hidden = lax.dynamic_slice_in_dim(hidden, lax.axis_index(COL) * rows, rows, 0)
    center = back_proj - jnp.mean(back_proj, axis=-1, keepdims=True)
    spread = jnp.mean(center * center, axis=-1, keepdims=True)
    conditioned = (own_hidden.astype(F32) + center * lax.rsqrt(spread + 1e-05)).astype(BF)
    return (conditioned, jnp.log(owned_totals))


def solution(mesh):
    cube = Mesh(mesh.devices.reshape(2, 2, 4, 4, 4), EVERY)
    return jax.shard_map(
        body,
        mesh=cube,
        in_specs=(P(EVERY, None), P(), P(), P(TIME, PLANE + (COL,)), P(PLANE + (COL,), TIME)),
        out_specs=(P(EVERY, None), P(EVERY)),
        check_vma=False,
    )
```

time: 1140 us -> 203 us (0.18)
  waiting for transfers between devices: 865 us -> 33.4 us
  blocking collectives: 195 us -> 90.5 us
    psum x1 -> x0, waiting for transfers between devices: 754 us -> none  [body(): summed = lax.psum(partial_value / totals[:, None], 'vocab')]
    psum x1 -> x0, blocking collectives: 195 us -> none  [body(): totals = lax.psum(local_totals, 'vocab')]
    all_gather x3 -> x2, waiting for transfers between devices: 96.7 us -> 4.73 us  [the longest x1 4.73 us: body(): full_back = lax.all_gather(back_weight, TIME, axis=1, tiled=True)]
    all_to_all x0 -> x2, blocking collectives: none -> 90.5 us  [the longest x1 49.7 us: body(): summed = jnp.sum(lax.all_to_all(sent, PLANE, 0, 0).astype(F32), axis=0)]
    ppermute x6 -> x2, starting transfers between devices: 28.5 us -> 8.28 us  [passed_along(): return lax.ppermute(block, axes, route)]
    all_to_all x0 -> x2, waiting for transfers between devices: none -> 20.1 us  [the longest x1 11.3 us: body(): summed = jnp.sum(lax.all_to_all(sent, COL, 0, 0).astype(F32), axis=0)]
    all_to_all x0 -> x2, starting transfers between devices: none -> 14.5 us  [the longest x1 7.56 us: gathered(): parts = lax.all_to_all(copies, axes, 0, 0)]
  transfers between devices with their start and end apart: 10 -> 6, of which waited for: 5 -> 5; matrix products, arithmetic and copies ran while one was open for 2% -> 14% of each run, Pallas kernels for 0% -> 0%
where the time goes in v1:
time: 203 us; the launch traced here: 202 us
  blocking collectives  90.5 us (45%)
  waiting for transfers between devices  33.4 us (16%)
  matrix products  32.9 us (16%)
  starting transfers between devices  22.9 us (11%)
  between operations  14.2 us (7%)
  local copies, waits for them, and re-layouts  4.77 us (2%)
  other arithmetic  3.55 us (2%)
    all_to_all x1, blocking collectives, body(): summed = jnp.sum(lax.all_to_all(sent, PLANE, 0, 0).astype(F32), axis=0)  49.7 us
    all_to_all x1, blocking collectives, gathered(): parts = lax.all_to_all(copies, axes, 0, 0)  40.7 us
    dot_general x1, matrix products, body(): jnp.dot(gathered(unit, PLANE), full_head, preferred_element_type=F32)  12.5 us
    all_to_all x1, waiting for transfers between devices, body(): summed = jnp.sum(lax.all_to_all(sent, COL, 0, 0).astype(F32), axis=0)  11.3 us
    dot_general x1, matrix products, body(): partial = jnp.dot(label_probs, full_back, preferred_element_type=F32)  10 us
    all_to_all x1, waiting for transfers between devices, gathered(): parts = lax.all_to_all(copies, axes, 0, 0)  8.83 us
    ppermute x2, starting transfers between devices, passed_along(): return lax.ppermute(block, axes, route)  8.28 us
    all_to_all x1, starting transfers between devices, gathered(): parts = lax.all_to_all(copies, axes, 0, 0)  7.56 us
  transfers between devices with their start and end apart: 6, of which 5 were waited for; matrix products, arithmetic and copies ran while one was open for 14% of the time, Pallas kernels for 0%

profile of v1, /device:TPU:32, one launch (start us, length us, event | category | flops | bytes accessed | tf_op | source)
XLA Modules:
  0.0 202.1 jit_solution(7945279568523426241)
XLA Ops:
  7.2 0.7 all-gather.3.cloned.1.call-update
  7.9 1.5 broadcast_in_dim.12
  9.4 7.6 %all-to-all-start = ((bf16[4,24,1024]{2,1,0:T(8,128)(2,1)}), bf16[4,24,1024]{2,1,0:T(8,128)(2,1)S(1)}, u32[]{:S(2)}, u32[]{:S(2)}) async-start(bf16[4,24,1024]{2,1,0:T(8,128)(2,1)} %broadcast_in_dim.12), calls=%async_computation | async-start | bytes 393216 | tf_op jit(solution)/shard_map/all_to_all | solution.py:23
  17.0 0.7 all-gather.5.cloned.1.call-update
  17.7 8.8 %all-to-all-done = bf16[4,24,1024]{2,1,0:T(8,128)(2,1)S(1)} async-done(((bf16[4,24,1024]{2,1,0:T(8,128)(2,1)}), bf16[4,24,1024]{2,1,0:T(8,128)(2,1)S(1)}, u32[]{:S(2)}, u32[]{:S(2)}) %all-to-all-start) | async-done | bytes 196640 | tf_op jit(solution)/shard_map/all_to_all | solution.py:23
  26.6 3.5 %collective-permute-start.1 = (bf16[96,1024]{1,0:T(8,128)(2,1)S(1)}, bf16[96,1024]{1,0:T(8,128)(2,1)S(1)}, u32[]{:S(2)}, u32[]{:S(2)}) collective-permute-start(bf16[96,1024]{1,0:T(8,128)(2,1)S(1)} %bitcast.27), channel_id=1, source_target_pairs={{0,4},{4,8},{8,12},{12,16},{16,20},{20,24},{24,28},{28,32},{32,36}... | collective-permute-start | bytes 589832 | tf_op jit(solution)/shard_map/ppermute | solution.py:30
  30.1 4.8 %collective-permute-start = (bf16[32,1024]{1,0:T(8,128)(2,1)S(1)}, bf16[32,1024]{1,0:T(8,128)(2,1)S(1)}, u32[]{:S(2)}, u32[]{:S(2)}) collective-permute-start(bf16[32,1024]{1,0:T(8,128)(2,1)S(1)} %slice.33), channel_id=1, source_target_pairs={{0,8},{4,12},{8,16},{12,20},{16,24},{20,28},{24,32},{28,36},{32,40... | collective-permute-start | bytes 196616 | tf_op jit(solution)/shard_map/ppermute | solution.py:30
  35.0 6.7 %collective-permute-done = bf16[32,1024]{1,0:T(8,128)(2,1)S(1)} collective-permute-done((bf16[32,1024]{1,0:T(8,128)(2,1)S(1)}, bf16[32,1024]{1,0:T(8,128)(2,1)S(1)}, u32[]{:S(2)}, u32[]{:S(2)}) %collective-permute-start) | collective-permute-done | bytes 65568 | tf_op jit(solution)/shard_map/ppermute | solution.py:30
  42.3 4.5 %convolution_convert_fusion = bf16[224,3072]{1,0:T(8,128)(2,1)S(1)} fusion(bf16[1024,3072]{1,0:T(8,128)(2,1)} %param.6, f32[224]{0:T(256)S(1)} %add_rsqrt_fusion, bf16[96,1024]{1,0:T(8,128)(2,1)S(1)} %bitcast.30, bf16[96,1024]{1,0:T(8,128)(2,1)S(1)} %collective-permute-done.1, bf16[32,1024]{1,0:T(8,128)(2,1)S(1)} %collective-permute-done), kind=kOutput, calls=%fused_computation.5 | convolution fusion | flops 1411809280 | bytes 8127360 | tf_op jit(solution)/shard_map/dot_general | solution.py:52
  46.9 1.0 copy.21
  47.9 0.9 copy.20
  49.0 2.9 %exponential_select_fusion = f32[16,96,224]{2,1,0:T(8,128)} fusion(bf16[96,16,64]{0,2,1:T(8,128)(2,1)} %bitcast.36, bf16[224,16,64]{0,2,1:T(8,128)(2,1)} %bitcast.33, pred[96,224]{1,0:T(8,128)(4,1)S(1)} %and_and_fusion), kind=kOutput, calls=%fused_computation.9 | convolution fusion | flops 45072384 | bytes 2053120 | tf_op jit(solution)/shard_map/qhd,khd->hqk/dot_general | solution.py:59
  51.9 2.4 %convolution_convert_fusion.2 = bf16[16,64,96]{2,1,0:T(8,128)(2,1)S(1)} fusion(bf16[224,16,64]{0,2,1:T(8,128)(2,1)S(1)} %bitcast.34, f32[16,96,224]{2,1,0:T(8,128)} %exponential_select_fusion), kind=kOutput, calls=%fused_computation.11 | convolution fusion | flops 44828384 | bytes 2031616 | tf_op jit(solution)/shard_map/hqk,khd->qhd/dot_general | solution.py:70
  54.3 0.6 fusion.9
  55.4 40.7 %all_to_all.20 = bf16[16,96,1024]{2,1,0:T(8,128)(2,1)} all-to-all(bf16[16,96,1024]{2,1,0:T(8,128)(2,1)S(1)} %broadcast_in_dim.19), channel_id=1, replica_groups=mesh['zl'=2,'c'=2,'x'=4,'y'=4,'zh'=4] {'x','y'}, dimensions={0} | all-to-all | bytes 6291456 | tf_op jit(solution)/shard_map/all_to_all | solution.py:23
  96.2 12.5 %convert_reduce_fusion = (f32[1536]{0:T(1024)S(1)}, bf16[1536,2048]{1,0:T(8,128)(2,1)}) fusion(bf16[1536,1024]{1,0:T(8,128)(2,1)} %bitcast.25, bf16[1024,2048]{1,0:T(8,128)(2,1)} %all-gather.3.cloned.1.call-done), kind=kOutput, calls=%fused_computation | convolution fusion | flops 6458178048 | bytes 13637632 | tf_op jit(solution)/shard_map/dot_general | solution.py:77
  108.8 4.7 %all-gather.5.cloned.1.call-done = bf16[2048,1024]{1,0:T(8,128)(2,1)} async-done(((bf16[2048,256]{1,0:T(8,128)(2,1)}), bf16[2048,1024]{1,0:T(8,128)(2,1)}) %all-gather.5.cloned.1.call-update) | async-done | bytes 4194320 | tf_op jit(solution)/shard_map/all_gather | solution.py:45
  113.5 10.0 %convolution_convert_fusion.1 = bf16[1536,1024]{1,0:T(8,128)(2,1)S(1)} fusion(bf16[1536,2048]{1,0:T(8,128)(2,1)} %get-tuple-element.13, bf16[2048,1024]{1,0:T(8,128)(2,1)} %all-gather.5.cloned.1.call-done), kind=kOutput, calls=%fused_computation.6 | convolution fusion | flops 6444023808 | bytes 13631488 | tf_op jit(solution)/shard_map/dot_general | solution.py:80
  124.0 49.7 %all_to_all.21 = bf16[16,104,1024]{2,1,0:T(8,128)(2,1)S(1)} all-to-all(bf16[16,104,1024]{2,1,0:T(8,128)(2,1)S(1)} %fusion.1), channel_id=1, replica_groups=mesh['zl'=2,'c'=2,'x'=4,'y'=4,'zh'=4] {'x','y'}, dimensions={0} | all-to-all | bytes 6815744 | tf_op jit(solution)/shard_map/all_to_all | solution.py:88
  173.7 0.7 convert_reduce_fusion.1
  174.6 0.7 fusion.11
  175.3 7.0 %all-to-all-start.3 = ((bf16[4,32,1024]{2,1,0:T(8,128)(2,1)}), bf16[4,32,1024]{2,1,0:T(8,128)(2,1)S(1)}, u32[]{:S(2)}, u32[]{:S(2)}) async-start(bf16[4,32,1024]{2,1,0:T(8,128)(2,1)} %fusion.11), calls=%async_computation.3 | async-start | bytes 524288 | tf_op jit(solution)/shard_map/all_to_all | solution.py:96
  182.3 11.3 %all-to-all-done.3 = bf16[4,32,1024]{2,1,0:T(8,128)(2,1)S(1)} async-done(((bf16[4,32,1024]{2,1,0:T(8,128)(2,1)}), bf16[4,32,1024]{2,1,0:T(8,128)(2,1)S(1)}, u32[]{:S(2)}, u32[]{:S(2)}) %all-to-all-start.3) | async-done | bytes 262176 | tf_op jit(solution)/shard_map/all_to_all | solution.py:96
  194.6 0.7 add_convert_fusion
  (37 shorter events, 3.3 us)
Async XLA Ops:
  7.2 47.1 %copy-start = (bf16[1024,1024]{1,0:T(8,128)(2,1)S(1)}, bf16[1024,1024]{1,0:T(8,128)(2,1)}, u32[]{:S(2)}) copy-start(bf16[1024,1024]{1,0:T(8,128)(2,1)} %param.7) | copy-start | bytes 6291460
  7.2 89.0 %all-gather.3.cloned.1.call-start = ((), (), s32[]{:S(2)}) async-start(), calls=%async_computation.4 | async-start | bytes 5242880 | tf_op jit(solution)/shard_map/all_gather | solution.py:44
  9.4 17.2 %all-to-all-start = ((bf16[4,24,1024]{2,1,0:T(8,128)(2,1)}), bf16[4,24,1024]{2,1,0:T(8,128)(2,1)S(1)}, u32[]{:S(2)}, u32[]{:S(2)}) async-start(bf16[4,24,1024]{2,1,0:T(8,128)(2,1)} %broadcast_in_dim.12), calls=%async_computation | async-start | bytes 393216 | tf_op jit(solution)/shard_map/all_to_all | solution.py:23
  17.0 96.5 %all-gather.5.cloned.1.call-start = ((), (), s32[]{:S(2)}) async-start(), calls=%async_computation.5 | async-start | bytes 5242880 | tf_op jit(solution)/shard_map/all_gather | solution.py:45
  26.6 15.5 %collective-permute-start.1 = (bf16[96,1024]{1,0:T(8,128)(2,1)S(1)}, bf16[96,1024]{1,0:T(8,128)(2,1)S(1)}, u32[]{:S(2)}, u32[]{:S(2)}) collective-permute-start(bf16[96,1024]{1,0:T(8,128)(2,1)S(1)} %bitcast.27), channel_id=1, source_target_pairs={{0,4},{4,8},{8,12},{12,16},{16,20},{20,24},{24,28},{28,32},{32,36}... | collective-permute-start | bytes 589832 | tf_op jit(solution)/shard_map/ppermute | solution.py:30
  30.1 11.6 %collective-permute-start = (bf16[32,1024]{1,0:T(8,128)(2,1)S(1)}, bf16[32,1024]{1,0:T(8,128)(2,1)S(1)}, u32[]{:S(2)}, u32[]{:S(2)}) collective-permute-start(bf16[32,1024]{1,0:T(8,128)(2,1)S(1)} %slice.33), channel_id=1, source_target_pairs={{0,8},{4,12},{8,16},{12,20},{16,24},{20,28},{24,32},{28,36},{32,40... | collective-permute-start | bytes 196616 | tf_op jit(solution)/shard_map/ppermute | solution.py:30
  175.3 18.3 %all-to-all-start.3 = ((bf16[4,32,1024]{2,1,0:T(8,128)(2,1)}), bf16[4,32,1024]{2,1,0:T(8,128)(2,1)S(1)}, u32[]{:S(2)}, u32[]{:S(2)}) async-start(bf16[4,32,1024]{2,1,0:T(8,128)(2,1)} %fusion.11), calls=%async_computation.3 | async-start | bytes 524288 | tf_op jit(solution)/shard_map/all_to_all | solution.py:96
Sparse Core Ops, SparseCore 0:
  9.8 49.9 all-gather.2
  61.6 51.8 all-gather.4

commit v2 on v1

--- a/solution.py
+++ b/solution.py
@@ -4,6 +4,7 @@
 import jax.numpy as jnp
 from jax import lax
 from jax.sharding import Mesh, PartitionSpec as P
+
 
 HEADS = 16
 HEAD_DIM = 64
@@ -15,6 +16,7 @@
 COL = "zh"
 BLOCKS = TIME + PLANE
 EVERY = BLOCKS + (COL,)
+CHUNKS = ((0, 16), (16, 24))
 
 
 def gathered(block, axes):
@@ -30,6 +32,34 @@
     return lax.ppermute(block, axes, route)
 
 
+def swapped(block, axis):
+    return lax.ppermute(block, axis, [(0, 1), (1, 0)])
+
+
+def over_time(block, axis):
+    beside = swapped(block, "c")
+    across = swapped(block, "zl")
+    corner = swapped(across, "c")
+    return jnp.concatenate([block, beside, across, corner], axis=axis)
+
+
+def from_own(values):
+    quarter = values.shape[1] // 4
+    q = [values[:, i * quarter : (i + 1) * quarter] for i in range(4)]
+    odd = lax.axis_index("c") == 1
+    q = [jnp.where(odd, q[i ^ 1], q[i]) for i in range(4)]
+    late = lax.axis_index("zl") == 1
+    return jnp.concatenate([jnp.where(late, q[i ^ 2], q[i]) for i in range(4)], axis=1)
+
+
+def three_rows(totals, width):
+    high = lax.reduce_precision(totals, 8, 7)
+    mid = lax.reduce_precision(totals - high, 8, 7)
+    low = totals - high - mid
+    split = jnp.stack([high, mid, low], axis=1).astype(BF)
+    return jnp.pad(split, ((0, 0), (0, 5), (0, width - totals.shape[1])))
+
+
 def root_norm(values):
     return values * lax.rsqrt(jnp.mean(values * values, axis=-1, keepdims=True) + 1e-06)
 
@@ -41,8 +71,8 @@
     cols = lax.axis_size(COL)
     block = rows * cols
     far = WIN - block
-    full_head = lax.all_gather(head_weight, TIME, axis=0, tiled=True)
-    full_back = lax.all_gather(back_weight, TIME, axis=1, tiled=True)
+    full_head = over_time(head_weight, 0)
+    full_back = over_time(back_weight, 1)
 
     own = gathered(frames, COL)
     prev = passed_along(own, BLOCKS, 1)
@@ -74,28 +104,33 @@
     ).astype(BF)
     unit = root_norm(hidden.astype(F32)).astype(BF)
 
-    logits = jnp.dot(gathered(unit, PLANE), full_head, preferred_element_type=F32)
-    label_probs = jnp.exp(30.0 * jnp.tanh(logits / 30.0)).astype(BF)
-    totals = jnp.sum(label_probs.astype(F32), axis=-1)
-    partial = jnp.dot(label_probs, full_back, preferred_element_type=F32)
-
-    high = lax.reduce_precision(totals, 8, 7)
-    mid = lax.reduce_precision(totals - high, 8, 7)
-    low = totals - high - mid
-    split = jnp.stack([high, mid, low]).astype(BF).reshape(3, planes, block)
-    split = jnp.pad(split.transpose(1, 0, 2), ((0, 0), (0, 5), (0, width - block)))
-    sent = jnp.concatenate([partial.astype(BF).reshape(planes, block, width), split], axis=1)
+    unit = from_own(unit).reshape(cols, rows, width)
+    totals = []
+    partials = []
+    for first_row, last_row in CHUNKS:
+        count = last_row - first_row
+        piece = unit[:, first_row:last_row].reshape(cols * count, width)
+        piece = gathered(piece, PLANE)
+        logits = jnp.dot(piece, full_head, preferred_element_type=F32)
+        label_probs = jnp.exp(30.0 * jnp.tanh(logits / 30.0)).astype(BF)
+        total = jnp.sum(label_probs.astype(F32), axis=-1)
+        totals.append(total.reshape(planes, cols * count))
+        partial = jnp.dot(label_probs, full_back, preferred_element_type=F32).astype(BF)
+        partials.append(partial.reshape(planes, cols * count, width))
+    sent = jnp.concatenate(partials + [three_rows(jnp.concatenate(totals, axis=1), width)], axis=1)
     summed = jnp.sum(lax.all_to_all(sent, PLANE, 0, 0).astype(F32), axis=0)
     block_totals = jnp.sum(summed[block : block + 3, :block], axis=0)
-    high = lax.reduce_precision(block_totals, 8, 7)
-    mid = lax.reduce_precision(block_totals - high, 8, 7)
-    low = block_totals - high - mid
-    split = jnp.stack([high, mid, low]).astype(BF).reshape(3, cols, rows)
-    split = jnp.pad(split.transpose(1, 0, 2), ((0, 0), (0, 5), (0, width - rows)))
-    sent = jnp.concatenate([summed[:block].astype(BF).reshape(cols, rows, width), split], axis=1)
+    sums = []
+    ordered = []
+    for first_row, last_row in CHUNKS:
+        part = slice(cols * first_row, cols * last_row)
+        sums.append(summed[part].astype(BF).reshape(cols, last_row - first_row, width))
+        ordered.append(block_totals[part].reshape(cols, last_row - first_row))
+    split = three_rows(jnp.concatenate(ordered, axis=1), width)
+    sent = jnp.concatenate(sums + [split], axis=1)
     summed = jnp.sum(lax.all_to_all(sent, COL, 0, 0).astype(F32), axis=0)
     owned_totals = jnp.sum(summed[rows : rows + 3, :rows], axis=0)
-    back_proj = summed[:rows] / owned_totals[:, None]
+    back_proj = from_own(summed[:rows]) / owned_totals[:, None]
 
     own_hidden = lax.dynamic_slice_in_dim(hidden, lax.axis_index(COL) * rows, rows, 0)
     center = back_proj - jnp.mean(back_proj, axis=-1, keepdims=True)

time: 203 us -> 199 us (0.980)
  blocking collectives: 90.5 us -> 43.7 us
  waiting for transfers between devices: 33.4 us -> 53.5 us
  local copies, waits for them, and re-layouts: 4.77 us -> 23.6 us
  between operations: 14.2 us -> 0.92 us
  matrix products: 32.9 us -> 41.8 us
  starting transfers between devices: 22.9 us -> 30.8 us
    all_to_all x1 -> x0, blocking collectives: 40.7 us -> none  [gathered(): parts = lax.all_to_all(copies, axes, 0, 0)]
    all_to_all x1 -> x3, waiting for transfers between devices: 8.83 us -> 37.5 us  [gathered(): parts = lax.all_to_all(copies, axes, 0, 0)]
    unnamed x4 -> x12, local copies, waits for them, and re-layouts: 0.03 us -> 12.8 us
    all_to_all x1 -> x3, starting transfers between devices: 7.56 us -> 16.6 us  [gathered(): parts = lax.all_to_all(copies, axes, 0, 0)]
    dot_general x2 -> x4, matrix products: 22.5 us -> 29.7 us  [the longest x2 16.6 us: body(): logits = jnp.dot(piece, full_head, preferred_element_type=F32)]
    all_to_all x1, blocking collectives: 49.7 us -> 43.7 us  [body(): summed = jnp.sum(lax.all_to_all(sent, PLANE, 0, 0).astype(F32), axis=0)]
    all_gather x2 -> x0, waiting for transfers between devices: 4.73 us -> none  [the longest x1 4.73 us: body(): full_back = lax.all_gather(back_weight, TIME, axis=1, tiled=True)]
    concatenate x0 -> x6, local copies, waits for them, and re-layouts: none -> 3.79 us  [the longest x2 3.47 us: over_time(): return jnp.concatenate([block, beside, across, corner], axis=axis)]
  transfers between devices with their start and end apart: 6 -> 12, of which waited for: 5 -> 6; matrix products, arithmetic and copies ran while one was open for 14% -> 24% of each run, Pallas kernels for 0% -> 0%
where the time goes in v2:
time: 199 us; the launch traced here: 198 us
  waiting for transfers between devices  53.5 us (27%)
  blocking collectives  43.7 us (22%)
  matrix products  41.8 us (21%)
  starting transfers between devices  30.8 us (15%)
  local copies, waits for them, and re-layouts  23.6 us (12%)
  other arithmetic  3.59 us (2%)
    all_to_all x1, blocking collectives, body(): summed = jnp.sum(lax.all_to_all(sent, PLANE, 0, 0).astype(F32), axis=0)  43.7 us
    all_to_all x3, waiting for transfers between devices, gathered(): parts = lax.all_to_all(copies, axes, 0, 0)  37.5 us
    dot_general x2, matrix products, body(): logits = jnp.dot(piece, full_head, preferred_element_type=F32)  16.6 us
    all_to_all x3, starting transfers between devices, gathered(): parts = lax.all_to_all(copies, axes, 0, 0)  16.6 us
    dot_general x2, matrix products, body(): jnp.dot(label_probs, full_back, preferred_element_type=F32).astype(BF)  13.1 us
    unnamed x12, local copies, waits for them, and re-layouts  12.8 us
    all_to_all x1, waiting for transfers between devices, body(): summed = jnp.sum(lax.all_to_all(sent, COL, 0, 0).astype(F32), axis=0)  9.6 us
    ppermute x2, starting transfers between devices, passed_along(): return lax.ppermute(block, axes, route)  8.28 us
  transfers between devices with their start and end apart: 12, of which 6 were waited for; matrix products, arithmetic and copies ran while one was open for 24% of the time, Pallas kernels for 0%

profile of v2, /device:TPU:32, one launch (start us, length us, event | category | flops | bytes accessed | tf_op | source)
XLA Modules:
  0.0 197.8 jit_solution(7310711532683108722)
XLA Ops:
  4.1 6.8 %all-to-all-start = ((bf16[4,24,1024]{2,1,0:T(8,128)(2,1)}), bf16[4,24,1024]{2,1,0:T(8,128)(2,1)S(1)}, u32[]{:S(2)}, u32[]{:S(2)}) async-start(bf16[4,24,1024]{2,1,0:T(8,128)(2,1)} %broadcast_in_dim.22), calls=%async_computation | async-start | bytes 393216 | tf_op jit(solution)/shard_map/all_to_all | solution.py:25
  10.9 2.3 %constant_dynamic-update-slice_fusion.3 = bf16[1024,2048]{1,0:T(8,128)(2,1)} fusion(bf16[256,2048]{1,0:T(8,128)(2,1)} %param.8), kind=kLoop, calls=%fused_computation.53 | loop fusion | bytes 2097152
  13.3 21.7 %all-to-all-done = bf16[4,24,1024]{2,1,0:T(8,128)(2,1)S(1)} async-done(((bf16[4,24,1024]{2,1,0:T(8,128)(2,1)}), bf16[4,24,1024]{2,1,0:T(8,128)(2,1)S(1)}, u32[]{:S(2)}, u32[]{:S(2)}) %all-to-all-start) | async-done | bytes 196640 | tf_op jit(solution)/shard_map/all_to_all | solution.py:25
  34.9 3.5 %collective-permute-start.1 = (bf16[96,1024]{1,0:T(8,128)(2,1)S(1)}, bf16[96,1024]{1,0:T(8,128)(2,1)S(1)}, u32[]{:S(2)}, u32[]{:S(2)}) collective-permute-start(bf16[96,1024]{1,0:T(8,128)(2,1)S(1)} %bitcast.34), channel_id=1, source_target_pairs={{0,4},{4,8},{8,12},{12,16},{16,20},{20,24},{24,28},{28,32},{32,36}... | collective-permute-start | bytes 589832 | tf_op jit(solution)/shard_map/ppermute | solution.py:32
  38.4 4.8 %collective-permute-start = (bf16[32,1024]{1,0:T(8,128)(2,1)S(1)}, bf16[32,1024]{1,0:T(8,128)(2,1)S(1)}, u32[]{:S(2)}, u32[]{:S(2)}) collective-permute-start(bf16[32,1024]{1,0:T(8,128)(2,1)S(1)} %slice.103), channel_id=1, source_target_pairs={{0,8},{4,12},{8,16},{12,20},{16,24},{20,28},{24,32},{28,36},{32,40... | collective-permute-start | bytes 196616 | tf_op jit(solution)/shard_map/ppermute | solution.py:32
  43.4 5.8 %collective-permute-done = bf16[32,1024]{1,0:T(8,128)(2,1)S(1)} collective-permute-done((bf16[32,1024]{1,0:T(8,128)(2,1)S(1)}, bf16[32,1024]{1,0:T(8,128)(2,1)S(1)}, u32[]{:S(2)}, u32[]{:S(2)}) %collective-permute-start) | collective-permute-done | bytes 65568 | tf_op jit(solution)/shard_map/ppermute | solution.py:32
  49.4 4.4 %convolution_convert_fusion = bf16[224,3072]{1,0:T(8,128)(2,1)S(1)} fusion(bf16[1024,3072]{1,0:T(8,128)(2,1)} %param.6, f32[224]{0:T(256)S(1)} %add_rsqrt_fusion, bf16[96,1024]{1,0:T(8,128)(2,1)S(1)} %bitcast.37, bf16[96,1024]{1,0:T(8,128)(2,1)S(1)} %collective-permute-done.1, bf16[32,1024]{1,0:T(8,128)(2,1)S(1)} %collective-permute-done), kind=kOutput, calls=%fused_computation.7 | convolution fusion | flops 1411809280 | bytes 8127360 | tf_op jit(solution)/shard_map/dot_general | solution.py:82
  56.0 2.8 %exponential_select_fusion = f32[16,96,224]{2,1,0:T(8,128)} fusion(bf16[96,16,64]{0,2,1:T(8,128)(2,1)} %bitcast.48, bf16[224,16,64]{0,2,1:T(8,128)(2,1)S(1)} %bitcast.46, pred[96,224]{1,0:T(8,128)(4,1)S(1)} %and_and_fusion), kind=kOutput, calls=%fused_computation.11 | convolution fusion | flops 45072384 | bytes 2053120 | tf_op jit(solution)/shard_map/qhd,khd->hqk/dot_general | solution.py:89
  58.7 3.2 %convolution_convert_fusion.3 = bf16[16,64,96]{2,1,0:T(8,128)(2,1)} fusion(bf16[224,16,64]{0,2,1:T(8,128)(2,1)} %bitcast.45, f32[16,96,224]{2,1,0:T(8,128)} %exponential_select_fusion), kind=kOutput, calls=%fused_computation.14 | convolution fusion | flops 44828384 | bytes 2031616 | tf_op jit(solution)/shard_map/hqk,khd->qhd/dot_general | solution.py:100
  64.9 5.2 %all-to-all-start.2 = ((bf16[16,32,1024]{2,1,0:T(8,128)(2,1)}), bf16[16,32,1024]{2,1,0:T(8,128)(2,1)}, u32[]{:S(2)}, u32[]{:S(2)}) async-start(bf16[16,32,1024]{2,1,0:T(8,128)(2,1)} %broadcast_in_dim.28), calls=%async_computation.2 | async-start | bytes 2097152 | tf_op jit(solution)/shard_map/all_to_all | solution.py:25
  73.6 2.4 %constant_dynamic-update-slice_fusion.2 = bf16[1024,2048]{1,0:T(8,128)(2,1)} fusion(bf16[1024,2048]{1,0:T(8,128)(2,1)} %constant_dynamic-update-slice_fusion.3, bf16[256,2048]{1,0:T(8,128)(2,1)} %collective-permute-done.2), kind=kLoop, calls=%fused_computation.52 | loop fusion | bytes 2097152
  76.0 2.3 %constant_dynamic-update-slice_fusion.1 = bf16[1024,2048]{1,0:T(8,128)(2,1)} fusion(bf16[1024,2048]{1,0:T(8,128)(2,1)} %constant_dynamic-update-slice_fusion.2, bf16[256,2048]{1,0:T(8,128)(2,1)} %collective-permute-done.3), kind=kLoop, calls=%fused_computation.51 | loop fusion | bytes 2097152
  78.3 2.3 %constant_dynamic-update-slice_fusion.6 = bf16[2048,1024]{1,0:T(8,128)(2,1)} fusion(bf16[2048,1024]{1,0:T(8,128)(2,1)} %constant_dynamic-update-slice_fusion.7, bf16[2048,256]{1,0:T(8,128)(2,1)} %collective-permute-done.5), kind=kLoop, calls=%fused_computation.56 | loop fusion | bytes 2097152
  80.6 5.8 %all-to-all-done.2 = bf16[16,32,1024]{2,1,0:T(8,128)(2,1)} async-done(((bf16[16,32,1024]{2,1,0:T(8,128)(2,1)}), bf16[16,32,1024]{2,1,0:T(8,128)(2,1)}, u32[]{:S(2)}, u32[]{:S(2)}) %all-to-all-start.2) | async-done | bytes 1048608 | tf_op jit(solution)/shard_map/all_to_all | solution.py:25
  86.4 4.6 %all-to-all-start.1 = ((bf16[16,64,1024]{2,1,0:T(8,128)(2,1)}), bf16[16,64,1024]{2,1,0:T(8,128)(2,1)}, u32[]{:S(2)}, u32[]{:S(2)}) async-start(bf16[16,64,1024]{2,1,0:T(8,128)(2,1)} %broadcast_in_dim.26), calls=%async_computation.1 | async-start | bytes 4194304 | tf_op jit(solution)/shard_map/all_to_all | solution.py:25
  91.0 2.4 %constant_dynamic-update-slice_fusion.5 = bf16[2048,1024]{1,0:T(8,128)(2,1)} fusion(bf16[2048,1024]{1,0:T(8,128)(2,1)} %constant_dynamic-update-slice_fusion.6, bf16[2048,256]{1,0:T(8,128)(2,1)} %collective-permute-done.6), kind=kLoop, calls=%fused_computation.55 | loop fusion | bytes 2097152
  95.7 6.6 %convert_reduce_fusion.2 = (f32[512]{0:T(512)S(1)}, bf16[512,2048]{1,0:T(8,128)(2,1)}) fusion(bf16[512,1024]{1,0:T(8,128)(2,1)} %bitcast.11, bf16[1024,2048]{1,0:T(8,128)(2,1)} %constant_dynamic-update-slice_fusion), kind=kOutput, calls=%fused_computation.5 | convolution fusion | flops 2152726016 | bytes 7342080 | tf_op jit(solution)/shard_map/dot_general | solution.py:114
  103.6 5.1 %convolution_convert_fusion.2 = bf16[512,1024]{1,0:T(8,128)(2,1)S(1)} fusion(bf16[512,2048]{1,0:T(8,128)(2,1)} %get-tuple-element.23, bf16[2048,1024]{1,0:T(8,128)(2,1)} %constant_dynamic-update-slice_fusion.4), kind=kOutput, calls=%fused_computation.12 | convolution fusion | flops 2148007936 | bytes 7340032 | tf_op jit(solution)/shard_map/dot_general | solution.py:118
  108.7 10.0 %all-to-all-done.1 = bf16[16,64,1024]{2,1,0:T(8,128)(2,1)} async-done(((bf16[16,64,1024]{2,1,0:T(8,128)(2,1)}), bf16[16,64,1024]{2,1,0:T(8,128)(2,1)}, u32[]{:S(2)}, u32[]{:S(2)}) %all-to-all-start.1) | async-done | bytes 2097184 | tf_op jit(solution)/shard_map/all_to_all | solution.py:25
  118.7 10.0 %convert_reduce_fusion = (f32[1024]{0:T(1024)S(1)}, bf16[1024,2048]{1,0:T(8,128)(2,1)}) fusion(bf16[1024,1024]{1,0:T(8,128)(2,1)} %bitcast.8, bf16[1024,2048]{1,0:T(8,128)(2,1)} %constant_dynamic-update-slice_fusion), kind=kOutput, calls=%fused_computation | convolution fusion | flops 4305452032 | bytes 10489856 | tf_op jit(solution)/shard_map/dot_general | solution.py:114
  128.9 8.0 %convolution_convert_fusion.1 = bf16[1024,1024]{1,0:T(8,128)(2,1)S(1)} fusion(bf16[1024,2048]{1,0:T(8,128)(2,1)} %get-tuple-element.25, bf16[2048,1024]{1,0:T(8,128)(2,1)} %constant_dynamic-update-slice_fusion.4), kind=kOutput, calls=%fused_computation.9 | convolution fusion | flops 4296015872 | bytes 10485760 | tf_op jit(solution)/shard_map/dot_general | solution.py:118
  137.2 43.7 %all_to_all.25 = bf16[16,104,1024]{2,1,0:T(8,128)(2,1)S(1)} all-to-all(bf16[16,104,1024]{2,1,0:T(8,128)(2,1)S(1)} %fusion.1), channel_id=1, replica_groups=mesh['zl'=2,'c'=2,'x'=4,'y'=4,'zh'=4] {'x','y'}, dimensions={0} | all-to-all | bytes 6815744 | tf_op jit(solution)/shard_map/all_to_all | solution.py:121
  182.7 3.8 %all-to-all-start.4 = ((bf16[4,32,1024]{2,1,0:T(8,128)(2,1)}), bf16[4,32,1024]{2,1,0:T(8,128)(2,1)S(1)}, u32[]{:S(2)}, u32[]{:S(2)}) async-start(bf16[4,32,1024]{2,1,0:T(8,128)(2,1)} %fusion.11), calls=%async_computation.4 | async-start | bytes 524288 | tf_op jit(solution)/shard_map/all_to_all | solution.py:131
  186.5 9.6 %all-to-all-done.4 = bf16[4,32,1024]{2,1,0:T(8,128)(2,1)S(1)} async-done(((bf16[4,32,1024]{2,1,0:T(8,128)(2,1)}), bf16[4,32,1024]{2,1,0:T(8,128)(2,1)S(1)}, u32[]{:S(2)}, u32[]{:S(2)}) %all-to-all-start.4) | async-done | bytes 262176 | tf_op jit(solution)/shard_map/all_to_all | solution.py:131
  (69 shorter events, 19.8 us)
Async XLA Ops:
  0.6 61.3 %copy-start = (bf16[1024,1024]{1,0:T(8,128)(2,1)S(1)}, bf16[1024,1024]{1,0:T(8,128)(2,1)}, u32[]{:S(2)}) copy-start(bf16[1024,1024]{1,0:T(8,128)(2,1)} %param.7) | copy-start | bytes 6291460
  0.6 72.9 %collective-permute-start.2 = (bf16[256,2048]{1,0:T(8,128)(2,1)}, bf16[256,2048]{1,0:T(8,128)(2,1)}, u32[]{:S(2)}, u32[]{:S(2)}) collective-permute-start(bf16[256,2048]{1,0:T(8,128)(2,1)} %param.8), channel_id=1, source_target_pairs={{0,64},{64,0},{1,65},{65,1},{2,66},{66,2},{3,67},{67,3},{4,68},{68... | collective-permute-start | bytes 3145736 | tf_op jit(solution)/shard_map/ppermute | solution.py:36
  0.7 69.4 %collective-permute-start.3 = (bf16[256,2048]{1,0:T(8,128)(2,1)}, bf16[256,2048]{1,0:T(8,128)(2,1)}, u32[]{:S(2)}, u32[]{:S(2)}) collective-permute-start(bf16[256,2048]{1,0:T(8,128)(2,1)} %param.8), channel_id=1, source_target_pairs={{0,128},{128,0},{1,129},{129,1},{2,130},{130,2},{3,131},{131,3},{4... | collective-permute-start | bytes 3145736 | tf_op jit(solution)/shard_map/ppermute | solution.py:36
  4.1 30.8 %all-to-all-start = ((bf16[4,24,1024]{2,1,0:T(8,128)(2,1)}), bf16[4,24,1024]{2,1,0:T(8,128)(2,1)S(1)}, u32[]{:S(2)}, u32[]{:S(2)}) async-start(bf16[4,24,1024]{2,1,0:T(8,128)(2,1)} %broadcast_in_dim.22), calls=%async_computation | async-start | bytes 393216 | tf_op jit(solution)/shard_map/all_to_all | solution.py:25
  10.9 67.4 %collective-permute-start.5 = (bf16[2048,256]{1,0:T(8,128)(2,1)}, bf16[2048,256]{1,0:T(8,128)(2,1)}, u32[]{:S(2)}, u32[]{:S(2)}) collective-permute-start(bf16[2048,256]{1,0:T(8,128)(2,1)} %param.9), channel_id=1, source_target_pairs={{0,64},{64,0},{1,65},{65,1},{2,66},{66,2},{3,67},{67,3},{4,68},{68... | collective-permute-start | bytes 3145736 | tf_op jit(solution)/shard_map/ppermute | solution.py:36
  34.9 14.3 %collective-permute-start.1 = (bf16[96,1024]{1,0:T(8,128)(2,1)S(1)}, bf16[96,1024]{1,0:T(8,128)(2,1)S(1)}, u32[]{:S(2)}, u32[]{:S(2)}) collective-permute-start(bf16[96,1024]{1,0:T(8,128)(2,1)S(1)} %bitcast.34), channel_id=1, source_target_pairs={{0,4},{4,8},{8,12},{12,16},{16,20},{20,24},{24,28},{28,32},{32,36}... | collective-permute-start | bytes 589832 | tf_op jit(solution)/shard_map/ppermute | solution.py:32
  38.4 10.8 %collective-permute-start = (bf16[32,1024]{1,0:T(8,128)(2,1)S(1)}, bf16[32,1024]{1,0:T(8,128)(2,1)S(1)}, u32[]{:S(2)}, u32[]{:S(2)}) collective-permute-start(bf16[32,1024]{1,0:T(8,128)(2,1)S(1)} %slice.103), channel_id=1, source_target_pairs={{0,8},{4,12},{8,16},{12,20},{16,24},{20,28},{24,32},{28,36},{32,40... | collective-permute-start | bytes 196616 | tf_op jit(solution)/shard_map/ppermute | solution.py:32
  49.2 24.4 %collective-permute-start.6 = (bf16[2048,256]{1,0:T(8,128)(2,1)}, bf16[2048,256]{1,0:T(8,128)(2,1)}, u32[]{:S(2)}, u32[]{:S(2)}) collective-permute-start(bf16[2048,256]{1,0:T(8,128)(2,1)} %param.9), channel_id=1, source_target_pairs={{0,128},{128,0},{1,129},{129,1},{2,130},{130,2},{3,131},{131,3},{4... | collective-permute-start | bytes 3145736 | tf_op jit(solution)/shard_map/ppermute | solution.py:36
  61.9 8.3 %copy-start.1 = (bf16[2048,256]{1,0:T(8,128)(2,1)S(1)}, bf16[2048,256]{1,0:T(8,128)(2,1)}, u32[]{:S(2)}) copy-start(bf16[2048,256]{1,0:T(8,128)(2,1)} %param.9) | copy-start | bytes 3145732
  64.9 21.5 %all-to-all-start.2 = ((bf16[16,32,1024]{2,1,0:T(8,128)(2,1)}), bf16[16,32,1024]{2,1,0:T(8,128)(2,1)}, u32[]{:S(2)}, u32[]{:S(2)}) async-start(bf16[16,32,1024]{2,1,0:T(8,128)(2,1)} %broadcast_in_dim.28), calls=%async_computation.2 | async-start | bytes 2097152 | tf_op jit(solution)/shard_map/all_to_all | solution.py:25
  70.2 23.2 %collective-permute-start.4 = (bf16[256,2048]{1,0:T(8,128)(2,1)}, bf16[256,2048]{1,0:T(8,128)(2,1)}, u32[]{:S(2)}, u32[]{:S(2)}) collective-permute-start(bf16[256,2048]{1,0:T(8,128)(2,1)} %collective-permute-done.3), channel_id=1, source_target_pairs={{0,64},{64,0},{1,65},{65,1},{2,66},{66,2},{3,67},{67,3},{4,68},{68... | collective-permute-start | bytes 3145736 | tf_op jit(solution)/shard_map/ppermute | solution.py:36
  73.6 28.8 %collective-permute-start.7 = (bf16[2048,256]{1,0:T(8,128)(2,1)}, bf16[2048,256]{1,0:T(8,128)(2,1)S(1)}, u32[]{:S(2)}, u32[]{:S(2)}) collective-permute-start(bf16[2048,256]{1,0:T(8,128)(2,1)} %collective-permute-done.6), channel_id=1, source_target_pairs={{0,64},{64,0},{1,65},{65,1},{2,66},{66,2},{3,67},{67,3},{4,68},{68... | collective-permute-start | bytes 3145736 | tf_op jit(solution)/shard_map/ppermute | solution.py:36
  86.4 32.3 %all-to-all-start.1 = ((bf16[16,64,1024]{2,1,0:T(8,128)(2,1)}), bf16[16,64,1024]{2,1,0:T(8,128)(2,1)}, u32[]{:S(2)}, u32[]{:S(2)}) async-start(bf16[16,64,1024]{2,1,0:T(8,128)(2,1)} %broadcast_in_dim.26), calls=%async_computation.1 | async-start | bytes 4194304 | tf_op jit(solution)/shard_map/all_to_all | solution.py:25
  182.7 13.4 %all-to-all-start.4 = ((bf16[4,32,1024]{2,1,0:T(8,128)(2,1)}), bf16[4,32,1024]{2,1,0:T(8,128)(2,1)S(1)}, u32[]{:S(2)}, u32[]{:S(2)}) async-start(bf16[4,32,1024]{2,1,0:T(8,128)(2,1)} %fusion.11), calls=%async_computation.4 | async-start | bytes 524288 | tf_op jit(solution)/shard_map/all_to_all | solution.py:131

commit v3 on v2

--- a/solution.py
+++ b/solution.py
@@ -16,7 +16,6 @@
 COL = "zh"
 BLOCKS = TIME + PLANE
 EVERY = BLOCKS + (COL,)
-CHUNKS = ((0, 16), (16, 24))
 
 
 def gathered(block, axes):
@@ -52,6 +51,29 @@
     return jnp.concatenate([jnp.where(late, q[i ^ 2], q[i]) for i in range(4)], axis=1)
 
 
+def turned(block, distance):
+    size = lax.axis_size(COL)
+    return lax.ppermute(block, COL, [(i, (i + distance) % size) for i in range(size)])
+
+
+def column_rows(block):
+    after = [block, turned(block, -1), turned(block, -2), turned(block, 1)]
+    place = lax.axis_index(COL)
+    odd = place % 2 == 1
+    after = [jnp.where(odd, after[i - 1], after[i]) for i in range(4)]
+    late = place >= 2
+    return jnp.concatenate([jnp.where(late, after[i - 2], after[i]) for i in range(4)], axis=0)
+
+
+def column_sum(blocks):
+    place = lax.axis_index(COL)
+    total = lax.dynamic_index_in_dim(blocks, place, 0, False).astype(F32)
+    for distance in (1, -1, 2):
+        block = lax.dynamic_index_in_dim(blocks, (place + distance) % 4, 0, False)
+        total = total + turned(block, distance).astype(F32)
+    return total
+
+
 def three_rows(totals, width):
     high = lax.reduce_precision(totals, 8, 7)
     mid = lax.reduce_precision(totals - high, 8, 7)
@@ -74,7 +96,7 @@
     full_head = over_time(head_weight, 0)
     full_back = over_time(back_weight, 1)
 
-    own = gathered(frames, COL)
+    own = column_rows(frames)
     prev = passed_along(own, BLOCKS, 1)
     prev2 = passed_along(own[block - far :], BLOCKS, 2)
     keys = WIN + block
@@ -104,31 +126,18 @@
     ).astype(BF)
     unit = root_norm(hidden.astype(F32)).astype(BF)
 
-    unit = from_own(unit).reshape(cols, rows, width)
-    totals = []
-    partials = []
-    for first_row, last_row in CHUNKS:
-        count = last_row - first_row
-        piece = unit[:, first_row:last_row].reshape(cols * count, width)
-        piece = gathered(piece, PLANE)
-        logits = jnp.dot(piece, full_head, preferred_element_type=F32)
-        label_probs = jnp.exp(30.0 * jnp.tanh(logits / 30.0)).astype(BF)
-        total = jnp.sum(label_probs.astype(F32), axis=-1)
-        totals.append(total.reshape(planes, cols * count))
-        partial = jnp.dot(label_probs, full_back, preferred_element_type=F32).astype(BF)
-        partials.append(partial.reshape(planes, cols * count, width))
-    sent = jnp.concatenate(partials + [three_rows(jnp.concatenate(totals, axis=1), width)], axis=1)
+    every = gathered(from_own(unit), PLANE)
+    logits = jnp.dot(every, full_head, preferred_element_type=F32)
+    label_probs = jnp.exp(30.0 * jnp.tanh(logits / 30.0)).astype(BF)
+    totals = jnp.sum(label_probs.astype(F32), axis=-1)
+    partial = jnp.dot(label_probs, full_back, preferred_element_type=F32).astype(BF)
+    split = three_rows(totals.reshape(planes, block), width)
+    sent = jnp.concatenate([partial.reshape(planes, block, width), split], axis=1)
     summed = jnp.sum(lax.all_to_all(sent, PLANE, 0, 0).astype(F32), axis=0)
     block_totals = jnp.sum(summed[block : block + 3, :block], axis=0)
-    sums = []
-    ordered = []
-    for first_row, last_row in CHUNKS:
-        part = slice(cols * first_row, cols * last_row)
-        sums.append(summed[part].astype(BF).reshape(cols, last_row - first_row, width))
-        ordered.append(block_totals[part].reshape(cols, last_row - first_row))
-    split = three_rows(jnp.concatenate(ordered, axis=1), width)
-    sent = jnp.concatenate(sums + [split], axis=1)
-    summed = jnp.sum(lax.all_to_all(sent, COL, 0, 0).astype(F32), axis=0)
+    split = three_rows(block_totals.reshape(cols, rows), width)
+    sent = jnp.concatenate([summed[:block].astype(BF).reshape(cols, rows, width), split], axis=1)
+    summed = column_sum(sent)
     owned_totals = jnp.sum(summed[rows : rows + 3, :rows], axis=0)
     back_proj = from_own(summed[:rows]) / owned_totals[:, None]
 

time: 199 us -> 200 us (level)
  the two profiles are of different devices: /device:TPU:32 before, /device:TPU:20 now
where the time goes in v3:
time: 200 us
  waiting for transfers between devices  109 us (54%)
  starting transfers between devices  42.2 us (21%)
  matrix products  33.9 us (17%)
  other arithmetic  7.52 us (4%)
  local copies, waits for them, and re-layouts  5.97 us (3%)
    all_to_all x1, waiting for transfers between devices, body(): summed = jnp.sum(lax.all_to_all(sent, PLANE, 0, 0).astype(F32), axis=0)  51 us
    ppermute x6, waiting for transfers between devices, swapped(): return lax.ppermute(block, axis, [(0, 1), (1, 0)])  44.1 us
    ppermute x6, starting transfers between devices, turned(): lax.ppermute(block, COL, [(i, (i + distance) % size) for i in range(size)])  18.4 us
    dot_general x1, matrix products, body(): logits = jnp.dot(every, full_head, preferred_element_type=F32)  12.9 us
    dot_general x1, matrix products, body(): jnp.dot(label_probs, full_back, preferred_element_type=F32).astype(BF)  10.7 us
    ppermute x6, waiting for transfers between devices, turned(): lax.ppermute(block, COL, [(i, (i + distance) % size) for i in range(size)])  9.58 us
    all_to_all x1, starting transfers between devices, gathered(): parts = lax.all_to_all(copies, axes, 0, 0)  7.23 us
    all_to_all x1, starting transfers between devices, body(): summed = jnp.sum(lax.all_to_all(sent, PLANE, 0, 0).astype(F32), axis=0)  7.23 us
  transfers between devices with their start and end apart: 16, of which 6 were waited for; matrix products, arithmetic and copies ran while one was open for 7% of the time, Pallas kernels for 0%

profile of v3, /device:TPU:20, one launch (start us, length us, event | category | flops | bytes accessed | tf_op | source)
XLA Modules:
  0.0 199.6 jit_solution(5583358713209907865)
XLA Ops:
  0.6 6.4 %collective-permute-start = (bf16[24,1024]{1,0:T(8,128)(2,1)}, bf16[24,1024]{1,0:T(8,128)(2,1)S(1)}, u32[]{:S(2)}, u32[]{:S(2)}) collective-permute-start(bf16[24,1024]{1,0:T(8,128)(2,1)} %param.5), channel_id=1, source_target_pairs={{0,3},{1,0},{2,1},{3,2},{4,7},{5,4},{6,5},{7,6},{8,11},{9,8},{10,9... | collective-permute-start | bytes 147464 | tf_op jit(solution)/shard_map/ppermute | solution.py:56
  8.0 2.8 %collective-permute-start.2 = (bf16[24,1024]{1,0:T(8,128)(2,1)}, bf16[24,1024]{1,0:T(8,128)(2,1)S(1)}, u32[]{:S(2)}, u32[]{:S(2)}) collective-permute-start(bf16[24,1024]{1,0:T(8,128)(2,1)} %param.5), channel_id=1, source_target_pairs={{0,1},{1,2},{2,3},{3,0},{4,5},{5,6},{6,7},{7,4},{8,9},{9,10},{10,1... | collective-permute-start | bytes 147464 | tf_op jit(solution)/shard_map/ppermute | solution.py:56
  10.9 4.7 %collective-permute-done.1 = bf16[24,1024]{1,0:T(8,128)(2,1)S(1)} collective-permute-done((bf16[24,1024]{1,0:T(8,128)(2,1)}, bf16[24,1024]{1,0:T(8,128)(2,1)S(1)}, u32[]{:S(2)}, u32[]{:S(2)}) %collective-permute-start.1) | collective-permute-done | bytes 49184 | tf_op jit(solution)/shard_map/ppermute | solution.py:56
  16.4 3.2 %collective-permute-start.4 = (bf16[96,1024]{1,0:T(8,128)(2,1)S(1)}, bf16[96,1024]{1,0:T(8,128)(2,1)S(1)}, u32[]{:S(2)}, u32[]{:S(2)}) collective-permute-start(bf16[96,1024]{1,0:T(8,128)(2,1)S(1)} %pad_maximum_fusion), channel_id=1, source_target_pairs={{0,4},{4,8},{8,12},{12,16},{16,20},{20,24},{24,28},{28,32},{32,36}... | collective-permute-start | bytes 589832 | tf_op jit(solution)/shard_map/ppermute | solution.py:31
  19.6 3.2 %collective-permute-start.3 = (bf16[32,1024]{1,0:T(8,128)(2,1)S(1)}, bf16[32,1024]{1,0:T(8,128)(2,1)S(1)}, u32[]{:S(2)}, u32[]{:S(2)}) collective-permute-start(bf16[32,1024]{1,0:T(8,128)(2,1)S(1)} %pad_maximum_fusion.2), channel_id=1, source_target_pairs={{0,8},{4,12},{8,16},{12,20},{16,24},{20,28},{24,32},{28,36},{32,40... | collective-permute-start | bytes 196616 | tf_op jit(solution)/shard_map/ppermute | solution.py:31
  22.9 4.4 %collective-permute-done.3 = bf16[32,1024]{1,0:T(8,128)(2,1)S(1)} collective-permute-done((bf16[32,1024]{1,0:T(8,128)(2,1)S(1)}, bf16[32,1024]{1,0:T(8,128)(2,1)S(1)}, u32[]{:S(2)}, u32[]{:S(2)}) %collective-permute-start.3) | collective-permute-done | bytes 65568 | tf_op jit(solution)/shard_map/ppermute | solution.py:31
  27.5 4.5 %convolution_convert_fusion = bf16[224,3072]{1,0:T(8,128)(2,1)S(1)} fusion(bf16[1024,3072]{1,0:T(8,128)(2,1)} %param.6, bf16[224,1024]{1,0:T(8,128)(2,1)S(1)} %constant_dynamic-update-slice_fusion, f32[224]{0:T(256)S(1)} %add_rsqrt_fusion), kind=kOutput, calls=%fused_computation.20 | convolution fusion | flops 1410662400 | bytes 8127360 | tf_op jit(solution)/shard_map/dot_general | solution.py:104
  32.1 1.0 copy.19
  34.2 2.9 %exponential_select_fusion = f32[16,96,224]{2,1,0:T(8,128)} fusion(bf16[96,16,64]{0,2,1:T(8,128)(2,1)} %bitcast.32, bf16[224,16,64]{0,2,1:T(8,128)(2,1)} %bitcast.29, pred[96,224]{1,0:T(8,128)(4,1)S(1)} %and_and_fusion), kind=kOutput, calls=%fused_computation.24 | convolution fusion | flops 45072384 | bytes 2053120 | tf_op jit(solution)/shard_map/qhd,khd->hqk/dot_general | solution.py:111
  37.1 2.4 %convolution_convert_fusion.1 = bf16[16,64,96]{2,1,0:T(8,128)(2,1)S(1)} fusion(bf16[224,16,64]{0,2,1:T(8,128)(2,1)S(1)} %bitcast.30, f32[16,96,224]{2,1,0:T(8,128)} %exponential_select_fusion), kind=kOutput, calls=%fused_computation.25 | convolution fusion | flops 44828384 | bytes 2031616 | tf_op jit(solution)/shard_map/hqk,khd->qhd/dot_general | solution.py:122
  40.3 2.1 %broadcast_in_dim.16 = bf16[16,96,1024]{2,1,0:T(8,128)(2,1)} broadcast(bf16[96,1024]{1,0:T(8,128)(2,1)S(1)} %pad_maximum_fusion.1), dimensions={1,2} | broadcast | bytes 3342336 | tf_op jit(solution)/shard_map/broadcast_in_dim | solution.py:23
  42.3 7.2 %all-to-all-start = ((bf16[16,96,1024]{2,1,0:T(8,128)(2,1)}), bf16[16,96,1024]{2,1,0:T(8,128)(2,1)}, u32[]{:S(2)}, u32[]{:S(2)}) async-start(bf16[16,96,1024]{2,1,0:T(8,128)(2,1)} %broadcast_in_dim.16), calls=%async_computation | async-start | bytes 6291456 | tf_op jit(solution)/shard_map/all_to_all | solution.py:24
  49.5 2.4 %collective-permute-start.6 = (bf16[256,2048]{1,0:T(8,128)(2,1)S(1)}, bf16[256,2048]{1,0:T(8,128)(2,1)S(1)}, u32[]{:S(2)}, u32[]{:S(2)}) collective-permute-start(bf16[256,2048]{1,0:T(8,128)(2,1)S(1)} %copy-done.1), channel_id=1, source_target_pairs={{0,128},{128,0},{1,129},{129,1},{2,130},{130,2},{3,131},{131,3},{4... | collective-permute-start | bytes 3145736 | tf_op jit(solution)/shard_map/ppermute | solution.py:35
  52.0 23.9 %collective-permute-done.6 = bf16[256,2048]{1,0:T(8,128)(2,1)S(1)} collective-permute-done((bf16[256,2048]{1,0:T(8,128)(2,1)S(1)}, bf16[256,2048]{1,0:T(8,128)(2,1)S(1)}, u32[]{:S(2)}, u32[]{:S(2)}) %collective-permute-start.6) | collective-permute-done | bytes 1048608 | tf_op jit(solution)/shard_map/ppermute | solution.py:35
  76.4 20.2 %collective-permute-done.9 = bf16[2048,256]{1,0:T(8,128)(2,1)} collective-permute-done((bf16[2048,256]{1,0:T(8,128)(2,1)}, bf16[2048,256]{1,0:T(8,128)(2,1)}, u32[]{:S(2)}, u32[]{:S(2)}) %collective-permute-start.9) | collective-permute-done | bytes 1048608 | tf_op jit(solution)/shard_map/ppermute | solution.py:35
  97.7 12.9 %convert_reduce_fusion = (f32[1536]{0:T(1024)S(1)}, bf16[1536,2048]{1,0:T(8,128)(2,1)}) fusion(bf16[1536,1024]{1,0:T(8,128)(2,1)} %bitcast.5, bf16[256,2048]{1,0:T(8,128)(2,1)} %collective-permute-done.7, bf16[256,2048]{1,0:T(8,128)(2,1)} %copy-done.2, bf16[256,2048]{1,0:T(8,128)(2,1)} %copy-done.3, bf16[256,2048]{1,0:T(8,128)(2,1)S(1)} %copy-done.1), kind=kOutput, calls=%fused_computation | convolution fusion | flops 6474955264 | bytes 13637632 | tf_op jit(solution)/shard_map/dot_general | solution.py:130
  110.7 10.7 %fusion.16 = bf16[1536,1024]{1,0:T(8,128)(2,1)S(1)} fusion(bf16[1536,2048]{1,0:T(8,128)(2,1)} %get-tuple-element.30, bf16[2048,256]{1,0:T(8,128)(2,1)} %collective-permute-done.10, bf16[2048,256]{1,0:T(8,128)(2,1)} %collective-permute-done.9, bf16[2048,256]{1,0:T(8,128)(2,1)} %collective-permute-done.8, bf16[2048,256]{1,0:T(8,128)(2,1)} %param.9), kind=kOutput, calls=%fused_computation.21 | convolution fusion | flops 6460801024 | bytes 13631488 | tf_op jit(solution)/shard_map/dot_general | solution.py:133
  121.4 2.2 %fusion.19 = bf16[16,104,1024]{2,1,0:T(8,128)(2,1)} fusion(bf16[16,3,96]{2,1,0:T(4,128)(2,1)S(1)} %copy.22, bf16[16,96,1024]{2,1,0:T(8,128)(2,1)S(1)} %bitcast.27), kind=kLoop, calls=%fused_computation.22 | loop fusion | flops 10223616 | bytes 6562816 | tf_op jit(solution)/shard_map/concatenate | solution.py:135
  123.6 7.2 %all-to-all-start.1 = ((bf16[16,104,1024]{2,1,0:T(8,128)(2,1)}), bf16[16,104,1024]{2,1,0:T(8,128)(2,1)}, u32[]{:S(2)}, u32[]{:S(2)}) async-start(bf16[16,104,1024]{2,1,0:T(8,128)(2,1)} %fusion.19), calls=%async_computation.1 | async-start | bytes 6815744 | tf_op jit(solution)/shard_map/all_to_all | solution.py:136
  130.9 51.0 %all-to-all-done.1 = bf16[16,104,1024]{2,1,0:T(8,128)(2,1)} async-done(((bf16[16,104,1024]{2,1,0:T(8,128)(2,1)}), bf16[16,104,1024]{2,1,0:T(8,128)(2,1)}, u32[]{:S(2)}, u32[]{:S(2)}) %all-to-all-start.1) | async-done | bytes 3407904 | tf_op jit(solution)/shard_map/all_to_all | solution.py:136
  181.8 2.7 %convert_reduce_fusion.1 = f32[104,1024]{1,0:T(8,128)S(1)} fusion(bf16[16,104,1024]{2,1,0:T(8,128)(2,1)} %all-to-all-done.1), kind=kLoop, calls=%fused_computation.3 | loop fusion | flops 3301376 | bytes 3833856 | tf_op jit(solution)/shard_map/reduce_sum | solution.py:136
  184.9 4.1 %collective-permute-start.12 = (bf16[32,1024]{1,0:T(8,128)(2,1)S(1)}, bf16[32,1024]{1,0:T(8,128)(2,1)S(1)}, u32[]{:S(2)}, u32[]{:S(2)}) collective-permute-start(bf16[32,1024]{1,0:T(8,128)(2,1)S(1)} %get-tuple-element.10), channel_id=1, source_target_pairs={{0,3},{1,0},{2,1},{3,2},{4,7},{5,4},{6,5},{7,6},{8,11},{9,8},{10,9... | collective-permute-start | bytes 196616 | tf_op jit(solution)/shard_map/ppermute | solution.py:56
  189.0 4.0 %collective-permute-start.13 = (bf16[32,1024]{1,0:T(8,128)(2,1)S(1)}, bf16[32,1024]{1,0:T(8,128)(2,1)S(1)}, u32[]{:S(2)}, u32[]{:S(2)}) collective-permute-start(bf16[32,1024]{1,0:T(8,128)(2,1)S(1)} %get-tuple-element.9), channel_id=1, source_target_pairs={{0,2},{1,3},{2,0},{3,1},{4,6},{5,7},{6,4},{7,5},{8,10},{9,11},{10,... | collective-permute-start | bytes 196616 | tf_op jit(solution)/shard_map/ppermute | solution.py:56
  193.0 4.9 %collective-permute-done.13 = bf16[32,1024]{1,0:T(8,128)(2,1)S(1)} collective-permute-done((bf16[32,1024]{1,0:T(8,128)(2,1)S(1)}, bf16[32,1024]{1,0:T(8,128)(2,1)S(1)}, u32[]{:S(2)}, u32[]{:S(2)}) %collective-permute-start.13) | collective-permute-done | bytes 65568 | tf_op jit(solution)/shard_map/ppermute | solution.py:56
  (70 shorter events, 7.8 us)
Async XLA Ops:
  0.6 38.8 %copy-start = (bf16[1024,1024]{1,0:T(8,128)(2,1)S(1)}, bf16[1024,1024]{1,0:T(8,128)(2,1)}, u32[]{:S(2)}) copy-start(bf16[1024,1024]{1,0:T(8,128)(2,1)} %param.7) | copy-start | bytes 6291460
  0.6 10.2 %collective-permute-start = (bf16[24,1024]{1,0:T(8,128)(2,1)}, bf16[24,1024]{1,0:T(8,128)(2,1)S(1)}, u32[]{:S(2)}, u32[]{:S(2)}) collective-permute-start(bf16[24,1024]{1,0:T(8,128)(2,1)} %param.5), channel_id=1, source_target_pairs={{0,3},{1,0},{2,1},{3,2},{4,7},{5,4},{6,5},{7,6},{8,11},{9,8},{10,9... | collective-permute-start | bytes 147464 | tf_op jit(solution)/shard_map/ppermute | solution.py:56
  7.0 8.5 %collective-permute-start.1 = (bf16[24,1024]{1,0:T(8,128)(2,1)}, bf16[24,1024]{1,0:T(8,128)(2,1)S(1)}, u32[]{:S(2)}, u32[]{:S(2)}) collective-permute-start(bf16[24,1024]{1,0:T(8,128)(2,1)} %param.5), channel_id=1, source_target_pairs={{0,2},{1,3},{2,0},{3,1},{4,6},{5,7},{6,4},{7,5},{8,10},{9,11},{10,... | collective-permute-start | bytes 147464 | tf_op jit(solution)/shard_map/ppermute | solution.py:56
  8.0 7.5 %collective-permute-start.2 = (bf16[24,1024]{1,0:T(8,128)(2,1)}, bf16[24,1024]{1,0:T(8,128)(2,1)S(1)}, u32[]{:S(2)}, u32[]{:S(2)}) collective-permute-start(bf16[24,1024]{1,0:T(8,128)(2,1)} %param.5), channel_id=1, source_target_pairs={{0,1},{1,2},{2,3},{3,0},{4,5},{5,6},{6,7},{7,4},{8,9},{9,10},{10,1... | collective-permute-start | bytes 147464 | tf_op jit(solution)/shard_map/ppermute | solution.py:56
  16.4 10.9 %collective-permute-start.4 = (bf16[96,1024]{1,0:T(8,128)(2,1)S(1)}, bf16[96,1024]{1,0:T(8,128)(2,1)S(1)}, u32[]{:S(2)}, u32[]{:S(2)}) collective-permute-start(bf16[96,1024]{1,0:T(8,128)(2,1)S(1)} %pad_maximum_fusion), channel_id=1, source_target_pairs={{0,4},{4,8},{8,12},{12,16},{16,20},{20,24},{24,28},{28,32},{32,36}... | collective-permute-start | bytes 589832 | tf_op jit(solution)/shard_map/ppermute | solution.py:31
  19.6 7.7 %collective-permute-start.3 = (bf16[32,1024]{1,0:T(8,128)(2,1)S(1)}, bf16[32,1024]{1,0:T(8,128)(2,1)S(1)}, u32[]{:S(2)}, u32[]{:S(2)}) collective-permute-start(bf16[32,1024]{1,0:T(8,128)(2,1)S(1)} %pad_maximum_fusion.2), channel_id=1, source_target_pairs={{0,8},{4,12},{8,16},{12,20},{16,24},{20,28},{24,32},{28,36},{32,40... | collective-permute-start | bytes 196616 | tf_op jit(solution)/shard_map/ppermute | solution.py:31
  40.2 9.3 %copy-start.1 = (bf16[256,2048]{1,0:T(8,128)(2,1)S(1)}, bf16[256,2048]{1,0:T(8,128)(2,1)}, u32[]{:S(2)}) copy-start(bf16[256,2048]{1,0:T(8,128)(2,1)} %param.8) | copy-start | bytes 3145732
  42.3 55.3 %all-to-all-start = ((bf16[16,96,1024]{2,1,0:T(8,128)(2,1)}), bf16[16,96,1024]{2,1,0:T(8,128)(2,1)}, u32[]{:S(2)}, u32[]{:S(2)}) async-start(bf16[16,96,1024]{2,1,0:T(8,128)(2,1)} %broadcast_in_dim.16), calls=%async_computation | async-start | bytes 6291456 | tf_op jit(solution)/shard_map/all_to_all | solution.py:24
  49.5 26.4 %collective-permute-start.6 = (bf16[256,2048]{1,0:T(8,128)(2,1)S(1)}, bf16[256,2048]{1,0:T(8,128)(2,1)S(1)}, u32[]{:S(2)}, u32[]{:S(2)}) collective-permute-start(bf16[256,2048]{1,0:T(8,128)(2,1)S(1)} %copy-done.1), channel_id=1, source_target_pairs={{0,128},{128,0},{1,129},{129,1},{2,130},{130,2},{3,131},{131,3},{4... | collective-permute-start | bytes 3145736 | tf_op jit(solution)/shard_map/ppermute | solution.py:35
  51.9 44.7 %collective-permute-start.9 = (bf16[2048,256]{1,0:T(8,128)(2,1)}, bf16[2048,256]{1,0:T(8,128)(2,1)}, u32[]{:S(2)}, u32[]{:S(2)}) collective-permute-start(bf16[2048,256]{1,0:T(8,128)(2,1)} %param.9), channel_id=1, source_target_pairs={{0,128},{128,0},{1,129},{129,1},{2,130},{130,2},{3,131},{131,3},{4... | collective-permute-start | bytes 3145736 | tf_op jit(solution)/shard_map/ppermute | solution.py:35
  52.0 44.6 %collective-permute-start.5 = (bf16[256,2048]{1,0:T(8,128)(2,1)S(1)}, bf16[256,2048]{1,0:T(8,128)(2,1)S(1)}, u32[]{:S(2)}, u32[]{:S(2)}) collective-permute-start(bf16[256,2048]{1,0:T(8,128)(2,1)S(1)} %copy-done.1), channel_id=1, source_target_pairs={{0,64},{64,0},{1,65},{65,1},{2,66},{66,2},{3,67},{67,3},{4,68},{68... | collective-permute-start | bytes 3145736 | tf_op jit(solution)/shard_map/ppermute | solution.py:35
  75.9 20.7 %copy-start.2 = (bf16[256,2048]{1,0:T(8,128)(2,1)}, bf16[256,2048]{1,0:T(8,128)(2,1)S(1)}, u32[]{:S(2)}) copy-start(bf16[256,2048]{1,0:T(8,128)(2,1)S(1)} %collective-permute-done.6) | copy-start | bytes 3145732
  75.9 21.7 %collective-permute-start.7 = (bf16[256,2048]{1,0:T(8,128)(2,1)S(1)}, bf16[256,2048]{1,0:T(8,128)(2,1)}, u32[]{:S(2)}, u32[]{:S(2)}) collective-permute-start(bf16[256,2048]{1,0:T(8,128)(2,1)S(1)} %collective-permute-done.6), channel_id=1, source_target_pairs={{0,64},{64,0},{1,65},{65,1},{2,66},{66,2},{3,67},{67,3},{4,68},{68... | collective-permute-start | bytes 3145736 | tf_op jit(solution)/shard_map/ppermute | solution.py:35
  75.9 34.7 %collective-permute-start.8 = (bf16[2048,256]{1,0:T(8,128)(2,1)}, bf16[2048,256]{1,0:T(8,128)(2,1)}, u32[]{:S(2)}, u32[]{:S(2)}) collective-permute-start(bf16[2048,256]{1,0:T(8,128)(2,1)} %param.9), channel_id=1, source_target_pairs={{0,64},{64,0},{1,65},{65,1},{2,66},{66,2},{3,67},{67,3},{4,68},{68... | collective-permute-start | bytes 3145736 | tf_op jit(solution)/shard_map/ppermute | solution.py:35
  96.6 14.1 %collective-permute-start.10 = (bf16[2048,256]{1,0:T(8,128)(2,1)}, bf16[2048,256]{1,0:T(8,128)(2,1)}, u32[]{:S(2)}, u32[]{:S(2)}) collective-permute-start(bf16[2048,256]{1,0:T(8,128)(2,1)} %collective-permute-done.9), channel_id=1, source_target_pairs={{0,64},{64,0},{1,65},{65,1},{2,66},{66,2},{3,67},{67,3},{4,68},{68... | collective-permute-start | bytes 3145736 | tf_op jit(solution)/shard_map/ppermute | solution.py:35
  96.7 1.0 copy-start.3
  123.6 58.2 %all-to-all-start.1 = ((bf16[16,104,1024]{2,1,0:T(8,128)(2,1)}), bf16[16,104,1024]{2,1,0:T(8,128)(2,1)}, u32[]{:S(2)}, u32[]{:S(2)}) async-start(bf16[16,104,1024]{2,1,0:T(8,128)(2,1)} %fusion.19), calls=%async_computation.1 | async-start | bytes 6815744 | tf_op jit(solution)/shard_map/all_to_all | solution.py:136
  184.8 8.2 %collective-permute-start.11 = (bf16[32,1024]{1,0:T(8,128)(2,1)S(1)}, bf16[32,1024]{1,0:T(8,128)(2,1)S(1)}, u32[]{:S(2)}, u32[]{:S(2)}) collective-permute-start(bf16[32,1024]{1,0:T(8,128)(2,1)S(1)} %get-tuple-element.8), channel_id=1, source_target_pairs={{0,1},{1,2},{2,3},{3,0},{4,5},{5,6},{6,7},{7,4},{8,9},{9,10},{10,1... | collective-permute-start | bytes 196616 | tf_op jit(solution)/shard_map/ppermute | solution.py:56
  184.9 8.1 %collective-permute-start.12 = (bf16[32,1024]{1,0:T(8,128)(2,1)S(1)}, bf16[32,1024]{1,0:T(8,128)(2,1)S(1)}, u32[]{:S(2)}, u32[]{:S(2)}) collective-permute-start(bf16[32,1024]{1,0:T(8,128)(2,1)S(1)} %get-tuple-element.10), channel_id=1, source_target_pairs={{0,3},{1,0},{2,1},{3,2},{4,7},{5,4},{6,5},{7,6},{8,11},{9,8},{10,9... | collective-permute-start | bytes 196616 | tf_op jit(solution)/shard_map/ppermute | solution.py:56
  189.0 8.9 %collective-permute-start.13 = (bf16[32,1024]{1,0:T(8,128)(2,1)S(1)}, bf16[32,1024]{1,0:T(8,128)(2,1)S(1)}, u32[]{:S(2)}, u32[]{:S(2)}) collective-permute-start(bf16[32,1024]{1,0:T(8,128)(2,1)S(1)} %get-tuple-element.9), channel_id=1, source_target_pairs={{0,2},{1,3},{2,0},{3,1},{4,6},{5,7},{6,4},{7,5},{8,10},{9,11},{10,... | collective-permute-start | bytes 196616 | tf_op jit(solution)/shard_map/ppermute | solution.py:56

commit v4 on v3

--- a/solution.py
+++ b/solution.py
@@ -65,12 +65,20 @@
     return jnp.concatenate([jnp.where(late, after[i - 2], after[i]) for i in range(4)], axis=0)
 
 
+def own_rows_first(block):
+    count = block.shape[0] // 4
+    q = [block[i * count : (i + 1) * count] for i in range(4)]
+    place = lax.axis_index(COL)
+    odd = place % 2 == 1
+    q = [jnp.where(odd, q[(i + 1) % 4], q[i]) for i in range(4)]
+    late = place >= 2
+    return jnp.concatenate([jnp.where(late, q[i - 2], q[i]) for i in range(4)], axis=0)
+
+
 def column_sum(blocks):
-    place = lax.axis_index(COL)
-    total = lax.dynamic_index_in_dim(blocks, place, 0, False).astype(F32)
-    for distance in (1, -1, 2):
-        block = lax.dynamic_index_in_dim(blocks, (place + distance) % 4, 0, False)
-        total = total + turned(block, distance).astype(F32)
+    total = blocks[0].astype(F32)
+    for distance in (1, 3, 2):
+        total = total + turned(blocks[distance], distance).astype(F32)
     return total
 
 
@@ -124,6 +132,7 @@
     hidden = (
         own.astype(F32) + jnp.dot(context, attn_out_weight, preferred_element_type=F32)
     ).astype(BF)
+    hidden = own_rows_first(hidden)
     unit = root_norm(hidden.astype(F32)).astype(BF)
 
     every = gathered(from_own(unit), PLANE)
@@ -141,10 +150,9 @@
     owned_totals = jnp.sum(summed[rows : rows + 3, :rows], axis=0)
     back_proj = from_own(summed[:rows]) / owned_totals[:, None]
 
-    own_hidden = lax.dynamic_slice_in_dim(hidden, lax.axis_index(COL) * rows, rows, 0)
     center = back_proj - jnp.mean(back_proj, axis=-1, keepdims=True)
     spread = jnp.mean(center * center, axis=-1, keepdims=True)
-    conditioned = (own_hidden.astype(F32) + center * lax.rsqrt(spread + 1e-05)).astype(BF)
+    conditioned = (hidden[:rows].astype(F32) + center * lax.rsqrt(spread + 1e-05)).astype(BF)
     return (conditioned, jnp.log(owned_totals))
 
 

time: 200 us -> 187 us (0.935)
  the two profiles are of different devices: /device:TPU:20 before, /device:TPU:32 now
where the time goes in v4:
time: 187 us
  waiting for transfers between devices  60 us (32%)
  blocking collectives  49.5 us (26%)
  matrix products  33.8 us (18%)
  starting transfers between devices  32.9 us (18%)
  local copies, waits for them, and re-layouts  5.94 us (3%)
  other arithmetic  3.78 us (2%)
    all_to_all x1, blocking collectives, body(): summed = jnp.sum(lax.all_to_all(sent, PLANE, 0, 0).astype(F32), axis=0)  49.5 us
    ppermute x6, waiting for transfers between devices, swapped(): return lax.ppermute(block, axis, [(0, 1), (1, 0)])  44.2 us
    ppermute x6, starting transfers between devices, turned(): lax.ppermute(block, COL, [(i, (i + distance) % size) for i in range(size)])  17.5 us
    dot_general x1, matrix products, body(): logits = jnp.dot(every, full_head, preferred_element_type=F32)  12.9 us
    dot_general x1, matrix products, body(): jnp.dot(label_probs, full_back, preferred_element_type=F32).astype(BF)  10.7 us
    ppermute x6, waiting for transfers between devices, turned(): lax.ppermute(block, COL, [(i, (i + distance) % size) for i in range(size)])  9.94 us
    ppermute x2, starting transfers between devices, passed_along(): return lax.ppermute(block, axes, route)  8.29 us
    ppermute x2, waiting for transfers between devices, passed_along(): return lax.ppermute(block, axes, route)  5.86 us
  transfers between devices with their start and end apart: 15, of which 7 were waited for; matrix products, arithmetic and copies ran while one was open for 7% of the time, Pallas kernels for 0%

profile of v4, /device:TPU:32, one launch (start us, length us, event | category | flops | bytes accessed | tf_op | source)
XLA Modules:
  0.0 186.9 jit_solution(5553224007177768179)
XLA Ops:
  0.6 5.5 %collective-permute-start = (bf16[24,1024]{1,0:T(8,128)(2,1)}, bf16[24,1024]{1,0:T(8,128)(2,1)S(1)}, u32[]{:S(2)}, u32[]{:S(2)}) collective-permute-start(bf16[24,1024]{1,0:T(8,128)(2,1)} %param.5), channel_id=1, source_target_pairs={{0,3},{1,0},{2,1},{3,2},{4,7},{5,4},{6,5},{7,6},{8,11},{9,8},{10,9... | collective-permute-start | bytes 147464 | tf_op jit(solution)/shard_map/ppermute | solution.py:56
  6.1 1.4 collective-permute-start.1
  7.6 2.4 %collective-permute-start.2 = (bf16[24,1024]{1,0:T(8,128)(2,1)}, bf16[24,1024]{1,0:T(8,128)(2,1)S(1)}, u32[]{:S(2)}, u32[]{:S(2)}) collective-permute-start(bf16[24,1024]{1,0:T(8,128)(2,1)} %param.5), channel_id=1, source_target_pairs={{0,1},{1,2},{2,3},{3,0},{4,5},{5,6},{6,7},{7,4},{8,9},{9,10},{10,1... | collective-permute-start | bytes 147464 | tf_op jit(solution)/shard_map/ppermute | solution.py:56
  10.0 4.4 %collective-permute-done.1 = bf16[24,1024]{1,0:T(8,128)(2,1)S(1)} collective-permute-done((bf16[24,1024]{1,0:T(8,128)(2,1)}, bf16[24,1024]{1,0:T(8,128)(2,1)S(1)}, u32[]{:S(2)}, u32[]{:S(2)}) %collective-permute-start.1) | collective-permute-done | bytes 49184 | tf_op jit(solution)/shard_map/ppermute | solution.py:56
  16.0 3.5 %collective-permute-start.4 = (bf16[96,1024]{1,0:T(8,128)(2,1)S(1)}, bf16[96,1024]{1,0:T(8,128)(2,1)S(1)}, u32[]{:S(2)}, u32[]{:S(2)}) collective-permute-start(bf16[96,1024]{1,0:T(8,128)(2,1)S(1)} %pad_maximum_fusion), channel_id=1, source_target_pairs={{0,4},{4,8},{8,12},{12,16},{16,20},{20,24},{24,28},{28,32},{32,36}... | collective-permute-start | bytes 589832 | tf_op jit(solution)/shard_map/ppermute | solution.py:31
  19.5 4.8 %collective-permute-start.3 = (bf16[32,1024]{1,0:T(8,128)(2,1)S(1)}, bf16[32,1024]{1,0:T(8,128)(2,1)S(1)}, u32[]{:S(2)}, u32[]{:S(2)}) collective-permute-start(bf16[32,1024]{1,0:T(8,128)(2,1)S(1)} %pad_maximum_fusion.3), channel_id=1, source_target_pairs={{0,8},{4,12},{8,16},{12,20},{16,24},{20,28},{24,32},{28,36},{32,40... | collective-permute-start | bytes 196616 | tf_op jit(solution)/shard_map/ppermute | solution.py:31
  24.4 5.9 %collective-permute-done.3 = bf16[32,1024]{1,0:T(8,128)(2,1)S(1)} collective-permute-done((bf16[32,1024]{1,0:T(8,128)(2,1)S(1)}, bf16[32,1024]{1,0:T(8,128)(2,1)S(1)}, u32[]{:S(2)}, u32[]{:S(2)}) %collective-permute-start.3) | collective-permute-done | bytes 65568 | tf_op jit(solution)/shard_map/ppermute | solution.py:31
  30.6 4.5 %convolution_convert_fusion = bf16[224,3072]{1,0:T(8,128)(2,1)S(1)} fusion(bf16[1024,3072]{1,0:T(8,128)(2,1)} %param.6, bf16[224,1024]{1,0:T(8,128)(2,1)S(1)} %constant_dynamic-update-slice_fusion, f32[224]{0:T(256)S(1)} %add_rsqrt_fusion), kind=kOutput, calls=%fused_computation.20 | convolution fusion | flops 1410662400 | bytes 8127360 | tf_op jit(solution)/shard_map/dot_general | solution.py:112
  35.1 1.0 copy.19
  36.1 0.8 copy.18
  37.2 2.9 %exponential_select_fusion = f32[16,96,224]{2,1,0:T(8,128)} fusion(bf16[96,16,64]{0,2,1:T(8,128)(2,1)} %bitcast.33, bf16[224,16,64]{0,2,1:T(8,128)(2,1)} %bitcast.31, pred[96,224]{1,0:T(8,128)(4,1)S(1)} %and_and_fusion), kind=kOutput, calls=%fused_computation.24 | convolution fusion | flops 45072384 | bytes 2053120 | tf_op jit(solution)/shard_map/qhd,khd->hqk/dot_general | solution.py:119
  40.1 2.4 %convolution_convert_fusion.1 = bf16[16,64,96]{2,1,0:T(8,128)(2,1)S(1)} fusion(bf16[224,16,64]{0,2,1:T(8,128)(2,1)S(1)} %bitcast.32, f32[16,96,224]{2,1,0:T(8,128)} %exponential_select_fusion), kind=kOutput, calls=%fused_computation.25 | convolution fusion | flops 44828384 | bytes 2031616 | tf_op jit(solution)/shard_map/hqk,khd->qhd/dot_general | solution.py:130
  43.4 2.0 %broadcast_in_dim.16 = bf16[16,96,1024]{2,1,0:T(8,128)(2,1)} broadcast(bf16[96,1024]{1,0:T(8,128)(2,1)S(1)} %pad_maximum_fusion.2), dimensions={1,2} | broadcast | bytes 3342336 | tf_op jit(solution)/shard_map/broadcast_in_dim | solution.py:23
  45.4 4.5 %all-to-all-start = ((bf16[16,96,1024]{2,1,0:T(8,128)(2,1)}), bf16[16,96,1024]{2,1,0:T(8,128)(2,1)}, u32[]{:S(2)}, u32[]{:S(2)}) async-start(bf16[16,96,1024]{2,1,0:T(8,128)(2,1)} %broadcast_in_dim.16), calls=%async_computation | async-start | bytes 6291456 | tf_op jit(solution)/shard_map/all_to_all | solution.py:24
  50.0 2.0 %collective-permute-start.9 = (bf16[2048,256]{1,0:T(8,128)(2,1)}, bf16[2048,256]{1,0:T(8,128)(2,1)}, u32[]{:S(2)}, u32[]{:S(2)}) collective-permute-start(bf16[2048,256]{1,0:T(8,128)(2,1)} %param.9), channel_id=1, source_target_pairs={{0,128},{128,0},{1,129},{129,1},{2,130},{130,2},{3,131},{131,3},{4... | collective-permute-start | bytes 3145736 | tf_op jit(solution)/shard_map/ppermute | solution.py:35
  52.0 24.0 %collective-permute-done.6 = bf16[256,2048]{1,0:T(8,128)(2,1)S(1)} collective-permute-done((bf16[256,2048]{1,0:T(8,128)(2,1)S(1)}, bf16[256,2048]{1,0:T(8,128)(2,1)S(1)}, u32[]{:S(2)}, u32[]{:S(2)}) %collective-permute-start.6) | collective-permute-done | bytes 1048608 | tf_op jit(solution)/shard_map/ppermute | solution.py:35
  76.6 20.2 %collective-permute-done.9 = bf16[2048,256]{1,0:T(8,128)(2,1)} collective-permute-done((bf16[2048,256]{1,0:T(8,128)(2,1)}, bf16[2048,256]{1,0:T(8,128)(2,1)}, u32[]{:S(2)}, u32[]{:S(2)}) %collective-permute-start.9) | collective-permute-done | bytes 1048608 | tf_op jit(solution)/shard_map/ppermute | solution.py:35
  96.8 1.0 copy-done.3
  97.8 12.9 %convert_reduce_fusion = (f32[1536]{0:T(1024)S(1)}, bf16[1536,2048]{1,0:T(8,128)(2,1)}) fusion(bf16[1536,1024]{1,0:T(8,128)(2,1)} %bitcast.5, bf16[256,2048]{1,0:T(8,128)(2,1)} %collective-permute-done.7, bf16[256,2048]{1,0:T(8,128)(2,1)} %copy-done.2, bf16[256,2048]{1,0:T(8,128)(2,1)} %copy-done.3, bf16[256,2048]{1,0:T(8,128)(2,1)S(1)} %copy-done.1), kind=kOutput, calls=%fused_computation | convolution fusion | flops 6474955264 | bytes 13637632 | tf_op jit(solution)/shard_map/dot_general | solution.py:139
  110.8 10.7 %fusion.16 = bf16[1536,1024]{1,0:T(8,128)(2,1)S(1)} fusion(bf16[1536,2048]{1,0:T(8,128)(2,1)} %get-tuple-element.32, bf16[2048,256]{1,0:T(8,128)(2,1)} %collective-permute-done.10, bf16[2048,256]{1,0:T(8,128)(2,1)} %collective-permute-done.9, bf16[2048,256]{1,0:T(8,128)(2,1)} %collective-permute-done.8, bf16[2048,256]{1,0:T(8,128)(2,1)} %param.9), kind=kOutput, calls=%fused_computation.21 | convolution fusion | flops 6460801024 | bytes 13631488 | tf_op jit(solution)/shard_map/dot_general | solution.py:142
  121.9 49.5 %all_to_all.10 = bf16[16,104,1024]{2,1,0:T(8,128)(2,1)S(1)} all-to-all(bf16[16,104,1024]{2,1,0:T(8,128)(2,1)S(1)} %fusion.19), channel_id=1, replica_groups=mesh['zl'=2,'c'=2,'x'=4,'y'=4,'zh'=4] {'x','y'}, dimensions={0} | all-to-all | bytes 6815744 | tf_op jit(solution)/shard_map/all_to_all | solution.py:145
  172.4 4.1 %collective-permute-start.12 = (bf16[32,1024]{1,0:T(8,128)(2,1)S(1)}, bf16[32,1024]{1,0:T(8,128)(2,1)S(1)}, u32[]{:S(2)}, u32[]{:S(2)}) collective-permute-start(bf16[32,1024]{1,0:T(8,128)(2,1)S(1)} %get-tuple-element.8), channel_id=1, source_target_pairs={{0,3},{1,0},{2,1},{3,2},{4,7},{5,4},{6,5},{7,6},{8,11},{9,8},{10,9... | collective-permute-start | bytes 196616 | tf_op jit(solution)/shard_map/ppermute | solution.py:56
  176.5 4.0 %collective-permute-start.13 = (bf16[32,1024]{1,0:T(8,128)(2,1)S(1)}, bf16[32,1024]{1,0:T(8,128)(2,1)S(1)}, u32[]{:S(2)}, u32[]{:S(2)}) collective-permute-start(bf16[32,1024]{1,0:T(8,128)(2,1)S(1)} %get-tuple-element.7), channel_id=1, source_target_pairs={{0,2},{1,3},{2,0},{3,1},{4,6},{5,7},{6,4},{7,5},{8,10},{9,11},{10,... | collective-permute-start | bytes 196616 | tf_op jit(solution)/shard_map/ppermute | solution.py:56
  180.5 4.7 %collective-permute-done.13 = bf16[32,1024]{1,0:T(8,128)(2,1)S(1)} collective-permute-done((bf16[32,1024]{1,0:T(8,128)(2,1)S(1)}, bf16[32,1024]{1,0:T(8,128)(2,1)S(1)}, u32[]{:S(2)}, u32[]{:S(2)}) %collective-permute-start.13) | collective-permute-done | bytes 65568 | tf_op jit(solution)/shard_map/ppermute | solution.py:56
  (71 shorter events, 7.0 us)
Async XLA Ops:
  0.6 41.9 %copy-start = (bf16[1024,1024]{1,0:T(8,128)(2,1)S(1)}, bf16[1024,1024]{1,0:T(8,128)(2,1)}, u32[]{:S(2)}) copy-start(bf16[1024,1024]{1,0:T(8,128)(2,1)} %param.7) | copy-start | bytes 6291460
  0.6 9.3 %collective-permute-start = (bf16[24,1024]{1,0:T(8,128)(2,1)}, bf16[24,1024]{1,0:T(8,128)(2,1)S(1)}, u32[]{:S(2)}, u32[]{:S(2)}) collective-permute-start(bf16[24,1024]{1,0:T(8,128)(2,1)} %param.5), channel_id=1, source_target_pairs={{0,3},{1,0},{2,1},{3,2},{4,7},{5,4},{6,5},{7,6},{8,11},{9,8},{10,9... | collective-permute-start | bytes 147464 | tf_op jit(solution)/shard_map/ppermute | solution.py:56
  6.1 8.2 %collective-permute-start.1 = (bf16[24,1024]{1,0:T(8,128)(2,1)}, bf16[24,1024]{1,0:T(8,128)(2,1)S(1)}, u32[]{:S(2)}, u32[]{:S(2)}) collective-permute-start(bf16[24,1024]{1,0:T(8,128)(2,1)} %param.5), channel_id=1, source_target_pairs={{0,2},{1,3},{2,0},{3,1},{4,6},{5,7},{6,4},{7,5},{8,10},{9,11},{10,... | collective-permute-start | bytes 147464 | tf_op jit(solution)/shard_map/ppermute | solution.py:56
  7.6 7.6 %collective-permute-start.2 = (bf16[24,1024]{1,0:T(8,128)(2,1)}, bf16[24,1024]{1,0:T(8,128)(2,1)S(1)}, u32[]{:S(2)}, u32[]{:S(2)}) collective-permute-start(bf16[24,1024]{1,0:T(8,128)(2,1)} %param.5), channel_id=1, source_target_pairs={{0,1},{1,2},{2,3},{3,0},{4,5},{5,6},{6,7},{7,4},{8,9},{9,10},{10,1... | collective-permute-start | bytes 147464 | tf_op jit(solution)/shard_map/ppermute | solution.py:56
  16.0 14.3 %collective-permute-start.4 = (bf16[96,1024]{1,0:T(8,128)(2,1)S(1)}, bf16[96,1024]{1,0:T(8,128)(2,1)S(1)}, u32[]{:S(2)}, u32[]{:S(2)}) collective-permute-start(bf16[96,1024]{1,0:T(8,128)(2,1)S(1)} %pad_maximum_fusion), channel_id=1, source_target_pairs={{0,4},{4,8},{8,12},{12,16},{16,20},{20,24},{24,28},{28,32},{32,36}... | collective-permute-start | bytes 589832 | tf_op jit(solution)/shard_map/ppermute | solution.py:31
  19.5 10.8 %collective-permute-start.3 = (bf16[32,1024]{1,0:T(8,128)(2,1)S(1)}, bf16[32,1024]{1,0:T(8,128)(2,1)S(1)}, u32[]{:S(2)}, u32[]{:S(2)}) collective-permute-start(bf16[32,1024]{1,0:T(8,128)(2,1)S(1)} %pad_maximum_fusion.3), channel_id=1, source_target_pairs={{0,8},{4,12},{8,16},{12,20},{16,24},{20,28},{24,32},{28,36},{32,40... | collective-permute-start | bytes 196616 | tf_op jit(solution)/shard_map/ppermute | solution.py:31
  43.4 6.6 %copy-start.1 = (bf16[256,2048]{1,0:T(8,128)(2,1)S(1)}, bf16[256,2048]{1,0:T(8,128)(2,1)}, u32[]{:S(2)}) copy-start(bf16[256,2048]{1,0:T(8,128)(2,1)} %param.8) | copy-start | bytes 3145732
  45.4 52.4 %all-to-all-start = ((bf16[16,96,1024]{2,1,0:T(8,128)(2,1)}), bf16[16,96,1024]{2,1,0:T(8,128)(2,1)}, u32[]{:S(2)}, u32[]{:S(2)}) async-start(bf16[16,96,1024]{2,1,0:T(8,128)(2,1)} %broadcast_in_dim.16), calls=%async_computation | async-start | bytes 6291456 | tf_op jit(solution)/shard_map/all_to_all | solution.py:24
  49.9 26.1 %collective-permute-start.6 = (bf16[256,2048]{1,0:T(8,128)(2,1)S(1)}, bf16[256,2048]{1,0:T(8,128)(2,1)S(1)}, u32[]{:S(2)}, u32[]{:S(2)}) collective-permute-start(bf16[256,2048]{1,0:T(8,128)(2,1)S(1)} %copy-done.1), channel_id=1, source_target_pairs={{0,128},{128,0},{1,129},{129,1},{2,130},{130,2},{3,131},{131,3},{4... | collective-permute-start | bytes 3145736 | tf_op jit(solution)/shard_map/ppermute | solution.py:35
  50.0 46.7 %collective-permute-start.9 = (bf16[2048,256]{1,0:T(8,128)(2,1)}, bf16[2048,256]{1,0:T(8,128)(2,1)}, u32[]{:S(2)}, u32[]{:S(2)}) collective-permute-start(bf16[2048,256]{1,0:T(8,128)(2,1)} %param.9), channel_id=1, source_target_pairs={{0,128},{128,0},{1,129},{129,1},{2,130},{130,2},{3,131},{131,3},{4... | collective-permute-start | bytes 3145736 | tf_op jit(solution)/shard_map/ppermute | solution.py:35
  52.0 44.7 %collective-permute-start.5 = (bf16[256,2048]{1,0:T(8,128)(2,1)S(1)}, bf16[256,2048]{1,0:T(8,128)(2,1)S(1)}, u32[]{:S(2)}, u32[]{:S(2)}) collective-permute-start(bf16[256,2048]{1,0:T(8,128)(2,1)S(1)} %copy-done.1), channel_id=1, source_target_pairs={{0,64},{64,0},{1,65},{65,1},{2,66},{66,2},{3,67},{67,3},{4,68},{68... | collective-permute-start | bytes 3145736 | tf_op jit(solution)/shard_map/ppermute | solution.py:35
  76.0 20.7 %copy-start.2 = (bf16[256,2048]{1,0:T(8,128)(2,1)}, bf16[256,2048]{1,0:T(8,128)(2,1)S(1)}, u32[]{:S(2)}) copy-start(bf16[256,2048]{1,0:T(8,128)(2,1)S(1)} %collective-permute-done.6) | copy-start | bytes 3145732
  76.0 21.7 %collective-permute-start.7 = (bf16[256,2048]{1,0:T(8,128)(2,1)S(1)}, bf16[256,2048]{1,0:T(8,128)(2,1)}, u32[]{:S(2)}, u32[]{:S(2)}) collective-permute-start(bf16[256,2048]{1,0:T(8,128)(2,1)S(1)} %collective-permute-done.6), channel_id=1, source_target_pairs={{0,64},{64,0},{1,65},{65,1},{2,66},{66,2},{3,67},{67,3},{4,68},{68... | collective-permute-start | bytes 3145736 | tf_op jit(solution)/shard_map/ppermute | solution.py:35
  76.0 34.7 %collective-permute-start.8 = (bf16[2048,256]{1,0:T(8,128)(2,1)}, bf16[2048,256]{1,0:T(8,128)(2,1)}, u32[]{:S(2)}, u32[]{:S(2)}) collective-permute-start(bf16[2048,256]{1,0:T(8,128)(2,1)} %param.9), channel_id=1, source_target_pairs={{0,64},{64,0},{1,65},{65,1},{2,66},{66,2},{3,67},{67,3},{4,68},{68... | collective-permute-start | bytes 3145736 | tf_op jit(solution)/shard_map/ppermute | solution.py:35
  96.8 14.0 %collective-permute-start.10 = (bf16[2048,256]{1,0:T(8,128)(2,1)}, bf16[2048,256]{1,0:T(8,128)(2,1)}, u32[]{:S(2)}, u32[]{:S(2)}) collective-permute-start(bf16[2048,256]{1,0:T(8,128)(2,1)} %collective-permute-done.9), channel_id=1, source_target_pairs={{0,64},{64,0},{1,65},{65,1},{2,66},{66,2},{3,67},{67,3},{4,68},{68... | collective-permute-start | bytes 3145736 | tf_op jit(solution)/shard_map/ppermute | solution.py:35
  96.8 1.0 copy-start.3
  172.3 8.2 %collective-permute-start.11 = (bf16[32,1024]{1,0:T(8,128)(2,1)S(1)}, bf16[32,1024]{1,0:T(8,128)(2,1)S(1)}, u32[]{:S(2)}, u32[]{:S(2)}) collective-permute-start(bf16[32,1024]{1,0:T(8,128)(2,1)S(1)} %get-tuple-element.6), channel_id=1, source_target_pairs={{0,1},{1,2},{2,3},{3,0},{4,5},{5,6},{6,7},{7,4},{8,9},{9,10},{10,1... | collective-permute-start | bytes 196616 | tf_op jit(solution)/shard_map/ppermute | solution.py:56
  172.4 8.1 %collective-permute-start.12 = (bf16[32,1024]{1,0:T(8,128)(2,1)S(1)}, bf16[32,1024]{1,0:T(8,128)(2,1)S(1)}, u32[]{:S(2)}, u32[]{:S(2)}) collective-permute-start(bf16[32,1024]{1,0:T(8,128)(2,1)S(1)} %get-tuple-element.8), channel_id=1, source_target_pairs={{0,3},{1,0},{2,1},{3,2},{4,7},{5,4},{6,5},{7,6},{8,11},{9,8},{10,9... | collective-permute-start | bytes 196616 | tf_op jit(solution)/shard_map/ppermute | solution.py:56
  176.5 8.7 %collective-permute-start.13 = (bf16[32,1024]{1,0:T(8,128)(2,1)S(1)}, bf16[32,1024]{1,0:T(8,128)(2,1)S(1)}, u32[]{:S(2)}, u32[]{:S(2)}) collective-permute-start(bf16[32,1024]{1,0:T(8,128)(2,1)S(1)} %get-tuple-element.7), channel_id=1, source_target_pairs={{0,2},{1,3},{2,0},{3,1},{4,6},{5,7},{6,4},{7,5},{8,10},{9,11},{10,... | collective-permute-start | bytes 196616 | tf_op jit(solution)/shard_map/ppermute | solution.py:56

commit v5 on v4

--- a/solution.py
+++ b/solution.py
@@ -3,6 +3,8 @@
 import jax
 import jax.numpy as jnp
 from jax import lax
+from jax.experimental import pallas as pl
+from jax.experimental.pallas import tpu as pltpu
 from jax.sharding import Mesh, PartitionSpec as P
 
 
@@ -35,11 +37,11 @@
     return lax.ppermute(block, axis, [(0, 1), (1, 0)])
 
 
-def over_time(block, axis):
+def over_time(block):
     beside = swapped(block, "c")
     across = swapped(block, "zl")
     corner = swapped(across, "c")
-    return jnp.concatenate([block, beside, across, corner], axis=axis)
+    return block, beside, across, corner
 
 
 def from_own(values):
@@ -94,15 +96,116 @@
     return values * lax.rsqrt(jnp.mean(values * values, axis=-1, keepdims=True) + 1e-06)
 
 
+STEPS = 4
+PARTS = 4
+
+
+def label_kernel(unit_ref, h0, h1, h2, h3, b0, b1, b2, b3, out_ref, head, back, total, sums, sems):
+    step = pl.program_id(0)
+    labels = head.shape[1] // PARTS
+    count = out_ref.shape[0]
+    block = unit_ref.shape[0] // count
+    narrow = back.shape[1] // PARTS
+    pieces = ((h0, h1, h2, h3), (b0, b1, b2, b3))
+
+    def copies(kind, part):
+        span = slice(part * labels, (part + 1) * labels)
+        for q in range(PARTS):
+            if kind == 0:
+                source = pieces[0][q].at[:, span]
+                target = head.at[q * 256 : (q + 1) * 256, span]
+            else:
+                source = pieces[1][q].at[span, :]
+                target = back.at[span, q * narrow : (q + 1) * narrow]
+            yield pltpu.make_async_copy(source, target, sems.at[kind, part, q])
+
+    @pl.when(step == 0)
+    def _():
+        for part in range(PARTS):
+            for kind in range(2):
+                for copy in copies(kind, part):
+                    copy.start()
+
+    def arrive(kind, part):
+        @pl.when(step == 0)
+        def _():
+            for copy in copies(kind, part):
+                copy.wait()
+
+    def logits(part):
+        arrive(0, part)
+        span = slice(part * labels, (part + 1) * labels)
+        return jnp.dot(unit_ref[...], head[:, span], preferred_element_type=F32)
+
+    ahead = logits(0)
+    lanes = None
+    for part in range(PARTS):
+        now = ahead
+        if part + 1 < PARTS:
+            ahead = logits(part + 1)
+        arrive(1, part)
+        probs = jnp.exp(30.0 * jnp.tanh(now * (1.0 / 30.0))).astype(BF)
+        wide = probs.astype(F32)
+        for k in range(labels // 128):
+            column = wide[:, k * 128 : (k + 1) * 128]
+            lanes = column if lanes is None else lanes + column
+        span = slice(part * labels, (part + 1) * labels)
+        value = jnp.dot(probs, back[span, :], preferred_element_type=F32)
+        if part == 0:
+            total[...] = value
+        else:
+            total[...] += value
+    sums[0 : count * block, :] = lanes
+    sums[count * block :, :] = jnp.zeros((sums.shape[0] - count * block, 128), F32)
+    row = lax.broadcasted_iota(jnp.int32, (8, 128), 0)
+    for s in range(count):
+        for j in range(total.shape[1] // 128):
+            tile = total[s * block : (s + 1) * block, j * 128 : (j + 1) * 128]
+            out_ref[s, j * block : (j + 1) * block, :] = tile.astype(BF)
+        flat = jnp.sum(sums[s * block : s * block + 128, :].T, axis=0, keepdims=True)
+        high = flat.astype(BF).astype(F32)
+        mid = (flat - high).astype(BF).astype(F32)
+        low = flat - high - mid
+        split = jnp.where(row == 0, high, jnp.where(row == 1, mid, jnp.where(row == 2, low, 0.0)))
+        out_ref[s, 8 * block :, :] = split.astype(BF)
+
+
+def label_sums(unit, head_parts, back_parts):
+    frames, width = unit.shape
+    labels = head_parts[0].shape[1]
+    slots = 16
+    block = frames // slots
+    count = slots // STEPS
+    rows = 8 * block + 8
+    return pl.pallas_call(
+        label_kernel,
+        grid=(STEPS,),
+        in_specs=[pl.BlockSpec((count * block, width), lambda i: (i, 0))]
+        + [pl.BlockSpec(memory_space=pl.ANY)] * 8,
+        out_specs=pl.BlockSpec((count, rows, 128), lambda i: (i, 0, 0)),
+        out_shape=jax.ShapeDtypeStruct((slots, rows, 128), BF),
+        scratch_shapes=[
+            pltpu.VMEM((width, labels), BF),
+            pltpu.VMEM((labels, width), BF),
+            pltpu.VMEM((count * block, width), F32),
+            pltpu.VMEM((count * block + 32, 128), F32),
+            pltpu.SemaphoreType.DMA((2, PARTS, 4)),
+        ],
+        compiler_params=pltpu.CompilerParams(vmem_limit_bytes=40 * 2**20),
+        cost_estimate=pl.CostEstimate(
+            flops=4 * frames * width * labels, bytes_accessed=16 * 2**20, transcendentals=2 * frames * labels
+        ),
+    )(unit, *head_parts, *back_parts)
+
+
 def body(frames, qkv_weight, attn_out_weight, head_weight, back_weight):
     rows = frames.shape[0]
     width = frames.shape[1]
-    planes = lax.axis_size(PLANE)
     cols = lax.axis_size(COL)
     block = rows * cols
     far = WIN - block
-    full_head = over_time(head_weight, 0)
-    full_back = over_time(back_weight, 1)
+    head_parts = over_time(head_weight)
+    back_parts = over_time(back_weight)
 
     own = column_rows(frames)
     prev = passed_along(own, BLOCKS, 1)
@@ -136,19 +239,16 @@
     unit = root_norm(hidden.astype(F32)).astype(BF)
 
     every = gathered(from_own(unit), PLANE)
-    logits = jnp.dot(every, full_head, preferred_element_type=F32)
-    label_probs = jnp.exp(30.0 * jnp.tanh(logits / 30.0)).astype(BF)
-    totals = jnp.sum(label_probs.astype(F32), axis=-1)
-    partial = jnp.dot(label_probs, full_back, preferred_element_type=F32).astype(BF)
-    split = three_rows(totals.reshape(planes, block), width)
-    sent = jnp.concatenate([partial.reshape(planes, block, width), split], axis=1)
+    sent = label_sums(every, head_parts, back_parts)
     summed = jnp.sum(lax.all_to_all(sent, PLANE, 0, 0).astype(F32), axis=0)
-    block_totals = jnp.sum(summed[block : block + 3, :block], axis=0)
-    split = three_rows(block_totals.reshape(cols, rows), width)
-    sent = jnp.concatenate([summed[:block].astype(BF).reshape(cols, rows, width), split], axis=1)
+    block_totals = jnp.sum(summed[8 * block : 8 * block + 3, :block], axis=0)
+    split = three_rows(block_totals.reshape(cols, rows), 128)
+    parts = summed[: 8 * block].astype(BF).reshape(8, cols, rows, 128).transpose(1, 0, 2, 3)
+    sent = jnp.concatenate([parts.reshape(cols, 8 * rows, 128), split], axis=1)
     summed = column_sum(sent)
-    owned_totals = jnp.sum(summed[rows : rows + 3, :rows], axis=0)
-    back_proj = from_own(summed[:rows]) / owned_totals[:, None]
+    owned_totals = jnp.sum(summed[8 * rows : 8 * rows + 3, :rows], axis=0)
+    back_proj = summed[: 8 * rows].reshape(8, rows, 128).transpose(1, 0, 2).reshape(rows, width)
+    back_proj = from_own(back_proj) / owned_totals[:, None]
 
     center = back_proj - jnp.mean(back_proj, axis=-1, keepdims=True)
     spread = jnp.mean(center * center, axis=-1, keepdims=True)

time: 187 us -> 195 us (1.043)
  matrix products: 33.8 us -> 10.3 us
  Pallas kernels: 0 us -> 21.6 us
  local copies, waits for them, and re-layouts: 5.94 us -> 18.9 us
    dot_general x2 -> x0, matrix products: 23.6 us -> none  [the longest x1 12.9 us: body(): logits = jnp.dot(every, full_head, preferred_element_type=F32)]
    pallas_call x0 -> x1, Pallas kernels: none -> 21.6 us  [label_sums(): pl.pallas_call(label_kernel, grid=(STEPS,), in_specs=[pl.BlockSpec((count...]
    unnamed x15 -> x36, local copies, waits for them, and re-layouts: 1.06 us -> 14.7 us
    ppermute x6, waiting for transfers between devices: 44.2 us -> 41 us  [swapped(): return lax.ppermute(block, axis, [(0, 1), (1, 0)])]
    ppermute x2, waiting for transfers between devices: 5.86 us -> 7.9 us  [passed_along(): return lax.ppermute(block, axes, route)]
  transfers between devices with their start and end apart: 15 -> 15, of which waited for: 7 -> 9; matrix products, arithmetic and copies ran while one was open for 7% -> 0% of each run, Pallas kernels for 0% -> 0%
where the time goes in v5:
time: 195 us; the launch traced here: 194 us
  waiting for transfers between devices  58.4 us (30%)
  blocking collectives  47.6 us (24%)
  starting transfers between devices  32.7 us (17%)
  Pallas kernels  21.6 us (11%)
  local copies, waits for them, and re-layouts  18.9 us (10%)
  matrix products  10.3 us (5%)
  other arithmetic  3.74 us (2%)
    all_to_all x1, blocking collectives, body(): summed = jnp.sum(lax.all_to_all(sent, PLANE, 0, 0).astype(F32), axis=0)  47.6 us
    ppermute x6, waiting for transfers between devices, swapped(): return lax.ppermute(block, axis, [(0, 1), (1, 0)])  41 us
    pallas_call x1, Pallas kernels, label_sums(): pl.pallas_call(label_kernel, grid=(STEPS,), in_specs=[pl.BlockSpec((count...  21.6 us
    ppermute x6, starting transfers between devices, turned(): lax.ppermute(block, COL, [(i, (i + distance) % size) for i in range(size)])  17.7 us
    unnamed x36, local copies, waits for them, and re-layouts  14.7 us
    ppermute x6, waiting for transfers between devices, turned(): lax.ppermute(block, COL, [(i, (i + distance) % size) for i in range(size)])  9.47 us
    ppermute x2, waiting for transfers between devices, passed_along(): return lax.ppermute(block, axes, route)  7.9 us
    ppermute x2, starting transfers between devices, passed_along(): return lax.ppermute(block, axes, route)  7.69 us
  transfers between devices with their start and end apart: 15, of which 9 were waited for; matrix products, arithmetic and copies ran while one was open for 0% of the time, Pallas kernels for 0%

profile of v5, /device:TPU:32, one launch (start us, length us, event | category | flops | bytes accessed | tf_op | source)
XLA Modules:
  0.0 194.2 jit_solution(961370699339606820)
XLA Ops:
  0.6 6.4 %collective-permute-start.1 = (bf16[24,1024]{1,0:T(8,128)(2,1)}, bf16[24,1024]{1,0:T(8,128)(2,1)S(1)}, u32[]{:S(2)}, u32[]{:S(2)}) collective-permute-start(bf16[24,1024]{1,0:T(8,128)(2,1)} %param.5), channel_id=1, source_target_pairs={{0,2},{1,3},{2,0},{3,1},{4,6},{5,7},{6,4},{7,5},{8,10},{9,11},{10,... | collective-permute-start | bytes 147464 | tf_op jit(solution)/shard_map/ppermute | solution.py:58
  7.6 2.4 %collective-permute-start.2 = (bf16[24,1024]{1,0:T(8,128)(2,1)}, bf16[24,1024]{1,0:T(8,128)(2,1)S(1)}, u32[]{:S(2)}, u32[]{:S(2)}) collective-permute-start(bf16[24,1024]{1,0:T(8,128)(2,1)} %param.5), channel_id=1, source_target_pairs={{0,1},{1,2},{2,3},{3,0},{4,5},{5,6},{6,7},{7,4},{8,9},{9,10},{10,1... | collective-permute-start | bytes 147464 | tf_op jit(solution)/shard_map/ppermute | solution.py:58
  10.4 2.4 %collective-permute-done = bf16[24,1024]{1,0:T(8,128)(2,1)S(1)} collective-permute-done((bf16[24,1024]{1,0:T(8,128)(2,1)}, bf16[24,1024]{1,0:T(8,128)(2,1)S(1)}, u32[]{:S(2)}, u32[]{:S(2)}) %collective-permute-start) | collective-permute-done | bytes 49184 | tf_op jit(solution)/shard_map/ppermute | solution.py:58
  12.7 1.7 collective-permute-done.2
  15.2 5.1 %collective-permute-start.3 = (bf16[32,1024]{1,0:T(8,128)(2,1)S(1)}, bf16[32,1024]{1,0:T(8,128)(2,1)S(1)}, u32[]{:S(2)}, u32[]{:S(2)}) collective-permute-start(bf16[32,1024]{1,0:T(8,128)(2,1)S(1)} %pad_maximum_fusion.3), channel_id=1, source_target_pairs={{0,8},{4,12},{8,16},{12,20},{16,24},{20,28},{24,32},{28,36},{32,40... | collective-permute-start | bytes 196616 | tf_op jit(solution)/shard_map/ppermute | solution.py:33
  20.4 2.6 %collective-permute-start.4 = (bf16[96,1024]{1,0:T(8,128)(2,1)S(1)}, bf16[96,1024]{1,0:T(8,128)(2,1)S(1)}, u32[]{:S(2)}, u32[]{:S(2)}) collective-permute-start(bf16[96,1024]{1,0:T(8,128)(2,1)S(1)} %pad_maximum_fusion), channel_id=1, source_target_pairs={{0,4},{4,8},{8,12},{12,16},{16,20},{20,24},{24,28},{28,32},{32,36}... | collective-permute-start | bytes 589832 | tf_op jit(solution)/shard_map/ppermute | solution.py:33
  23.7 1.9 collective-permute-done.3
  25.5 6.0 %collective-permute-done.4 = bf16[96,1024]{1,0:T(8,128)(2,1)S(1)} collective-permute-done((bf16[96,1024]{1,0:T(8,128)(2,1)S(1)}, bf16[96,1024]{1,0:T(8,128)(2,1)S(1)}, u32[]{:S(2)}, u32[]{:S(2)}) %collective-permute-start.4) | collective-permute-done | bytes 196640 | tf_op jit(solution)/shard_map/ppermute | solution.py:33
  31.8 4.5 %convolution_convert_fusion = bf16[224,3072]{1,0:T(8,128)(2,1)S(1)} fusion(bf16[1024,3072]{1,0:T(8,128)(2,1)} %param.6, bf16[224,1024]{1,0:T(8,128)(2,1)S(1)} %constant_dynamic-update-slice_fusion, f32[224]{0:T(256)S(1)} %add_rsqrt_fusion), kind=kOutput, calls=%fused_computation.1 | convolution fusion | flops 1410662400 | bytes 8127360 | tf_op jit(solution)/shard_map/dot_general | solution.py:215
  37.8 2.9 %exponential_select_fusion = f32[16,96,224]{2,1,0:T(8,128)} fusion(bf16[96,16,64]{0,2,1:T(8,128)(2,1)S(1)} %bitcast.42, bf16[224,16,64]{0,2,1:T(8,128)(2,1)} %bitcast.38, pred[96,224]{1,0:T(8,128)(4,1)} %and_and_fusion), kind=kOutput, calls=%fused_computation.3 | convolution fusion | flops 45072384 | bytes 2053120 | tf_op jit(solution)/shard_map/qhd,khd->hqk/dot_general | solution.py:222
  40.7 2.5 %convolution_convert_fusion.1 = bf16[16,64,96]{2,1,0:T(8,128)(2,1)S(1)} fusion(bf16[224,16,64]{0,2,1:T(8,128)(2,1)S(1)} %bitcast.39, f32[16,96,224]{2,1,0:T(8,128)} %exponential_select_fusion), kind=kOutput, calls=%fused_computation.4 | convolution fusion | flops 44828384 | bytes 2031616 | tf_op jit(solution)/shard_map/hqk,khd->qhd/dot_general | solution.py:233
  44.0 2.1 %broadcast_in_dim.16 = bf16[16,96,1024]{2,1,0:T(8,128)(2,1)} broadcast(bf16[96,1024]{1,0:T(8,128)(2,1)S(1)} %pad_maximum_fusion.2), dimensions={1,2} | broadcast | bytes 3342336 | tf_op jit(solution)/shard_map/broadcast_in_dim | solution.py:25
  46.1 4.6 %all-to-all-start = ((bf16[16,96,1024]{2,1,0:T(8,128)(2,1)}), bf16[16,96,1024]{2,1,0:T(8,128)(2,1)}, u32[]{:S(2)}, u32[]{:S(2)}) async-start(bf16[16,96,1024]{2,1,0:T(8,128)(2,1)} %broadcast_in_dim.16), calls=%async_computation | async-start | bytes 6291456 | tf_op jit(solution)/shard_map/all_to_all | solution.py:26
  50.8 2.0 %collective-permute-start.9 = (bf16[2048,256]{1,0:T(8,128)(2,1)}, bf16[2048,256]{1,0:T(8,128)(2,1)S(1)}, u32[]{:S(2)}, u32[]{:S(2)}) collective-permute-start(bf16[2048,256]{1,0:T(8,128)(2,1)} %b0.1), channel_id=1, source_target_pairs={{0,128},{128,0},{1,129},{129,1},{2,130},{130,2},{3,131},{131,3},{4... | collective-permute-start | bytes 3145736 | tf_op jit(solution)/shard_map/ppermute | solution.py:37
  53.4 23.5 %collective-permute-done.6.h2 = bf16[256,2048]{1,0:T(8,128)(2,1)S(1)} collective-permute-done((bf16[256,2048]{1,0:T(8,128)(2,1)S(1)}, bf16[256,2048]{1,0:T(8,128)(2,1)S(1)}, u32[]{:S(2)}, u32[]{:S(2)}) %collective-permute-start.6) | collective-permute-done | bytes 1048608 | tf_op jit(solution)/shard_map/ppermute | solution.py:37
  77.9 17.5 %collective-permute-done.9.b2 = bf16[2048,256]{1,0:T(8,128)(2,1)S(1)} collective-permute-done((bf16[2048,256]{1,0:T(8,128)(2,1)}, bf16[2048,256]{1,0:T(8,128)(2,1)S(1)}, u32[]{:S(2)}, u32[]{:S(2)}) %collective-permute-start.9) | collective-permute-done | bytes 1048608 | tf_op jit(solution)/shard_map/ppermute | solution.py:37
  100.5 1.2 copy-done.2
  101.7 1.2 copy-done.4
  105.4 1.2 copy-done.10
  109.1 21.6 %shard_map.68 = bf16[16,776,128]{2,1,0:T(8,128)(2,1)} custom-call(bf16[1536,1024]{1,0:T(8,128)(2,1)} %bitcast.5.unit_ref, bf16[256,2048]{1,0:T(8,128)(2,1)S(1)} %copy-done.1, bf16[256,2048]{1,0:T(8,128)(2,1)S(1)} %copy-done.8, bf16[256,2048]{1,0:T(8,128)(2,1)S(1)} %copy-done.4, bf16[256,2048]{1,0:T(8,128)(2,1)S(1)} %copy-done.12, ...), custom_call_target="tpu_custom_call" | custom-call | flops 12884901888 | bytes 16777216 | tf_op jit(solution)/shard_map/pallas_call | solution.py:180
  130.7 47.6 %all_to_all.10 = bf16[16,776,128]{2,1,0:T(8,128)(2,1)S(1)} all-to-all(bf16[16,776,128]{2,1,0:T(8,128)(2,1)} %shard_map.68), channel_id=1, replica_groups=mesh['zl'=2,'c'=2,'x'=4,'y'=4,'zh'=4] {'x','y'}, dimensions={0} | all-to-all | bytes 6356992 | tf_op jit(solution)/shard_map/all_to_all | solution.py:243
  180.1 6.8 %collective-permute-start.13 = (bf16[200,128]{1,0:T(8,128)(2,1)S(1)}, bf16[200,128]{1,0:T(8,128)(2,1)S(1)}, u32[]{:S(2)}, u32[]{:S(2)}) collective-permute-start(bf16[200,128]{1,0:T(8,128)(2,1)S(1)} %get-tuple-element.7), channel_id=1, source_target_pairs={{0,2},{1,3},{2,0},{3,1},{4,6},{5,7},{6,4},{7,5},{8,10},{9,11},{10,... | collective-permute-start | bytes 153608 | tf_op jit(solution)/shard_map/ppermute | solution.py:58
  187.4 2.5 %collective-permute-done.13 = bf16[200,128]{1,0:T(8,128)(2,1)S(1)} collective-permute-done((bf16[200,128]{1,0:T(8,128)(2,1)S(1)}, bf16[200,128]{1,0:T(8,128)(2,1)S(1)}, u32[]{:S(2)}, u32[]{:S(2)}) %collective-permute-start.13) | collective-permute-done | bytes 51232 | tf_op jit(solution)/shard_map/ppermute | solution.py:58
  189.9 2.5 %collective-permute-done.12 = bf16[200,128]{1,0:T(8,128)(2,1)S(1)} collective-permute-done((bf16[200,128]{1,0:T(8,128)(2,1)S(1)}, bf16[200,128]{1,0:T(8,128)(2,1)S(1)}, u32[]{:S(2)}, u32[]{:S(2)}) %collective-permute-start.12) | collective-permute-done | bytes 51232 | tf_op jit(solution)/shard_map/ppermute | solution.py:58
  (90 shorter events, 20.7 us)
Async XLA Ops:
  0.6 42.5 %copy-start = (bf16[1024,1024]{1,0:T(8,128)(2,1)S(1)}, bf16[1024,1024]{1,0:T(8,128)(2,1)}, u32[]{:S(2)}) copy-start(bf16[1024,1024]{1,0:T(8,128)(2,1)} %param.7) | copy-start | bytes 6291460
  0.6 9.7 %collective-permute-start.1 = (bf16[24,1024]{1,0:T(8,128)(2,1)}, bf16[24,1024]{1,0:T(8,128)(2,1)S(1)}, u32[]{:S(2)}, u32[]{:S(2)}) collective-permute-start(bf16[24,1024]{1,0:T(8,128)(2,1)} %param.5), channel_id=1, source_target_pairs={{0,2},{1,3},{2,0},{3,1},{4,6},{5,7},{6,4},{7,5},{8,10},{9,11},{10,... | collective-permute-start | bytes 147464 | tf_op jit(solution)/shard_map/ppermute | solution.py:58
  7.0 5.7 %collective-permute-start = (bf16[24,1024]{1,0:T(8,128)(2,1)}, bf16[24,1024]{1,0:T(8,128)(2,1)S(1)}, u32[]{:S(2)}, u32[]{:S(2)}) collective-permute-start(bf16[24,1024]{1,0:T(8,128)(2,1)} %param.5), channel_id=1, source_target_pairs={{0,3},{1,0},{2,1},{3,2},{4,7},{5,4},{6,5},{7,6},{8,11},{9,8},{10,9... | collective-permute-start | bytes 147464 | tf_op jit(solution)/shard_map/ppermute | solution.py:58
  7.6 6.8 %collective-permute-start.2 = (bf16[24,1024]{1,0:T(8,128)(2,1)}, bf16[24,1024]{1,0:T(8,128)(2,1)S(1)}, u32[]{:S(2)}, u32[]{:S(2)}) collective-permute-start(bf16[24,1024]{1,0:T(8,128)(2,1)} %param.5), channel_id=1, source_target_pairs={{0,1},{1,2},{2,3},{3,0},{4,5},{5,6},{6,7},{7,4},{8,9},{9,10},{10,1... | collective-permute-start | bytes 147464 | tf_op jit(solution)/shard_map/ppermute | solution.py:58
  15.2 10.3 %collective-permute-start.3 = (bf16[32,1024]{1,0:T(8,128)(2,1)S(1)}, bf16[32,1024]{1,0:T(8,128)(2,1)S(1)}, u32[]{:S(2)}, u32[]{:S(2)}) collective-permute-start(bf16[32,1024]{1,0:T(8,128)(2,1)S(1)} %pad_maximum_fusion.3), channel_id=1, source_target_pairs={{0,8},{4,12},{8,16},{12,20},{16,24},{20,28},{24,32},{28,36},{32,40... | collective-permute-start | bytes 196616 | tf_op jit(solution)/shard_map/ppermute | solution.py:33
  20.4 11.2 %collective-permute-start.4 = (bf16[96,1024]{1,0:T(8,128)(2,1)S(1)}, bf16[96,1024]{1,0:T(8,128)(2,1)S(1)}, u32[]{:S(2)}, u32[]{:S(2)}) collective-permute-start(bf16[96,1024]{1,0:T(8,128)(2,1)S(1)} %pad_maximum_fusion), channel_id=1, source_target_pairs={{0,4},{4,8},{8,12},{12,16},{16,20},{20,24},{24,28},{28,32},{32,36}... | collective-permute-start | bytes 589832 | tf_op jit(solution)/shard_map/ppermute | solution.py:33
  46.1 4.6 %copy-start.1 = (bf16[256,2048]{1,0:T(8,128)(2,1)S(1)}, bf16[256,2048]{1,0:T(8,128)(2,1)}, u32[]{:S(2)}) copy-start(bf16[256,2048]{1,0:T(8,128)(2,1)} %h0.1) | copy-start | bytes 3145732
  46.1 54.4 %all-to-all-start = ((bf16[16,96,1024]{2,1,0:T(8,128)(2,1)}), bf16[16,96,1024]{2,1,0:T(8,128)(2,1)}, u32[]{:S(2)}, u32[]{:S(2)}) async-start(bf16[16,96,1024]{2,1,0:T(8,128)(2,1)} %broadcast_in_dim.16), calls=%async_computation | async-start | bytes 6291456 | tf_op jit(solution)/shard_map/all_to_all | solution.py:26
  50.7 26.1 %collective-permute-start.6 = (bf16[256,2048]{1,0:T(8,128)(2,1)S(1)}, bf16[256,2048]{1,0:T(8,128)(2,1)S(1)}, u32[]{:S(2)}, u32[]{:S(2)}) collective-permute-start(bf16[256,2048]{1,0:T(8,128)(2,1)S(1)} %copy-done.1), channel_id=1, source_target_pairs={{0,128},{128,0},{1,129},{129,1},{2,130},{130,2},{3,131},{131,3},{4... | collective-permute-start | bytes 3145736 | tf_op jit(solution)/shard_map/ppermute | solution.py:37
  50.8 44.6 %collective-permute-start.9 = (bf16[2048,256]{1,0:T(8,128)(2,1)}, bf16[2048,256]{1,0:T(8,128)(2,1)S(1)}, u32[]{:S(2)}, u32[]{:S(2)}) collective-permute-start(bf16[2048,256]{1,0:T(8,128)(2,1)} %b0.1), channel_id=1, source_target_pairs={{0,128},{128,0},{1,129},{129,1},{2,130},{130,2},{3,131},{131,3},{4... | collective-permute-start | bytes 3145736 | tf_op jit(solution)/shard_map/ppermute | solution.py:37
  52.9 43.5 %collective-permute-start.5 = (bf16[256,2048]{1,0:T(8,128)(2,1)S(1)}, bf16[256,2048]{1,0:T(8,128)(2,1)S(1)}, u32[]{:S(2)}, u32[]{:S(2)}) collective-permute-start(bf16[256,2048]{1,0:T(8,128)(2,1)S(1)} %copy-done.1), channel_id=1, source_target_pairs={{0,64},{64,0},{1,65},{65,1},{2,66},{66,2},{3,67},{67,3},{4,68},{68... | collective-permute-start | bytes 3145736 | tf_op jit(solution)/shard_map/ppermute | solution.py:37
  52.9 44.5 %collective-permute-start.8 = (bf16[2048,256]{1,0:T(8,128)(2,1)}, bf16[2048,256]{1,0:T(8,128)(2,1)S(1)}, u32[]{:S(2)}, u32[]{:S(2)}) collective-permute-start(bf16[2048,256]{1,0:T(8,128)(2,1)} %b0.1), channel_id=1, source_target_pairs={{0,64},{64,0},{1,65},{65,1},{2,66},{66,2},{3,67},{67,3},{4,68},{68... | collective-permute-start | bytes 3145736 | tf_op jit(solution)/shard_map/ppermute | solution.py:37
  76.9 21.5 %collective-permute-start.7 = (bf16[256,2048]{1,0:T(8,128)(2,1)S(1)}, bf16[256,2048]{1,0:T(8,128)(2,1)S(1)}, u32[]{:S(2)}, u32[]{:S(2)}) collective-permute-start(bf16[256,2048]{1,0:T(8,128)(2,1)S(1)} %collective-permute-done.6.h2), channel_id=1, source_target_pairs={{0,64},{64,0},{1,65},{65,1},{2,66},{66,2},{3,67},{67,3},{4,68},{68... | collective-permute-start | bytes 3145736 | tf_op jit(solution)/shard_map/ppermute | solution.py:37
  95.4 4.0 %collective-permute-start.10 = (bf16[2048,256]{1,0:T(8,128)(2,1)S(1)}, bf16[2048,256]{1,0:T(8,128)(2,1)S(1)}, u32[]{:S(2)}, u32[]{:S(2)}) collective-permute-start(bf16[2048,256]{1,0:T(8,128)(2,1)S(1)} %collective-permute-done.9.b2), channel_id=1, source_target_pairs={{0,64},{64,0},{1,65},{65,1},{2,66},{66,2},{3,67},{67,3},{4,68},{68... | collective-permute-start | bytes 3145736 | tf_op jit(solution)/shard_map/ppermute | solution.py:37
  100.5 1.2 copy-start.2
  101.7 1.2 copy-start.4
  102.9 1.2 copy-start.6
  104.2 1.2 copy-start.8
  105.4 1.2 copy-start.10
  106.6 1.2 copy-start.12
  107.8 1.2 copy-start.14
  179.0 8.4 %collective-permute-start.11 = (bf16[200,128]{1,0:T(8,128)(2,1)S(1)}, bf16[200,128]{1,0:T(8,128)(2,1)S(1)}, u32[]{:S(2)}, u32[]{:S(2)}) collective-permute-start(bf16[200,128]{1,0:T(8,128)(2,1)S(1)} %get-tuple-element.6), channel_id=1, source_target_pairs={{0,1},{1,2},{2,3},{3,0},{4,5},{5,6},{6,7},{7,4},{8,9},{9,10},{10,1... | collective-permute-start | bytes 153608 | tf_op jit(solution)/shard_map/ppermute | solution.py:58
  180.1 9.8 %collective-permute-start.13 = (bf16[200,128]{1,0:T(8,128)(2,1)S(1)}, bf16[200,128]{1,0:T(8,128)(2,1)S(1)}, u32[]{:S(2)}, u32[]{:S(2)}) collective-permute-start(bf16[200,128]{1,0:T(8,128)(2,1)S(1)} %get-tuple-element.7), channel_id=1, source_target_pairs={{0,2},{1,3},{2,0},{3,1},{4,6},{5,7},{6,4},{7,5},{8,10},{9,11},{10,... | collective-permute-start | bytes 153608 | tf_op jit(solution)/shard_map/ppermute | solution.py:58
  186.9 5.6 %collective-permute-start.12 = (bf16[200,128]{1,0:T(8,128)(2,1)S(1)}, bf16[200,128]{1,0:T(8,128)(2,1)S(1)}, u32[]{:S(2)}, u32[]{:S(2)}) collective-permute-start(bf16[200,128]{1,0:T(8,128)(2,1)S(1)} %get-tuple-element.8), channel_id=1, source_target_pairs={{0,3},{1,0},{2,1},{3,2},{4,7},{5,4},{6,5},{7,6},{8,11},{9,8},{10,9... | collective-permute-start | bytes 153608 | tf_op jit(solution)/shard_map/ppermute | solution.py:58
  (6 other events, 6.1 us)

commit v6 on v5

--- a/solution.py
+++ b/solution.py
@@ -181,7 +181,7 @@
         label_kernel,
         grid=(STEPS,),
         in_specs=[pl.BlockSpec((count * block, width), lambda i: (i, 0))]
-        + [pl.BlockSpec(memory_space=pl.ANY)] * 8,
+        + [pl.BlockSpec(memory_space=pltpu.HBM)] * 8,
         out_specs=pl.BlockSpec((count, rows, 128), lambda i: (i, 0, 0)),
         out_shape=jax.ShapeDtypeStruct((slots, rows, 128), BF),
         scratch_shapes=[
@@ -191,11 +191,11 @@
             pltpu.VMEM((count * block + 32, 128), F32),
             pltpu.SemaphoreType.DMA((2, PARTS, 4)),
         ],
-        compiler_params=pltpu.CompilerParams(vmem_limit_bytes=40 * 2**20),
+        compiler_params=pltpu.CompilerParams(vmem_limit_bytes=20 * 2**20),
         cost_estimate=pl.CostEstimate(
             flops=4 * frames * width * labels, bytes_accessed=16 * 2**20, transcendentals=2 * frames * labels
         ),
-    )(unit, *head_parts, *back_parts)
+    )(unit, *[pltpu.with_memory_space_constraint(p, pltpu.HBM) for p in (*head_parts, *back_parts)])
 
 
 def body(frames, qkv_weight, attn_out_weight, head_weight, back_weight):

time: 195 us -> 182 us (0.933)
  local copies, waits for them, and re-layouts: 18.9 us -> 6.99 us
    unnamed x36 -> x20, local copies, waits for them, and re-layouts: 14.7 us -> 2.77 us
where the time goes in v6:
time: 182 us
  waiting for transfers between devices  59.5 us (33%)
  blocking collectives  47 us (26%)
  starting transfers between devices  32.7 us (18%)
  Pallas kernels  21 us (12%)
  matrix products  10.2 us (6%)
  local copies, waits for them, and re-layouts  6.99 us (4%)
  other arithmetic  3.74 us (2%)
    all_to_all x1, blocking collectives, body(): summed = jnp.sum(lax.all_to_all(sent, PLANE, 0, 0).astype(F32), axis=0)  47 us
    ppermute x6, waiting for transfers between devices, swapped(): return lax.ppermute(block, axis, [(0, 1), (1, 0)])  42.1 us
    pallas_call x1, Pallas kernels, label_sums(): pl.pallas_call(label_kernel, grid=(STEPS,), in_specs=[pl.BlockSpec((count...  21 us
    ppermute x6, starting transfers between devices, turned(): lax.ppermute(block, COL, [(i, (i + distance) % size) for i in range(size)])  17.8 us
    ppermute x6, waiting for transfers between devices, turned(): lax.ppermute(block, COL, [(i, (i + distance) % size) for i in range(size)])  9.47 us
    ppermute x2, waiting for transfers between devices, passed_along(): return lax.ppermute(block, axes, route)  7.9 us
    ppermute x2, starting transfers between devices, passed_along(): return lax.ppermute(block, axes, route)  7.69 us
    all_to_all x1, starting transfers between devices, gathered(): parts = lax.all_to_all(copies, axes, 0, 0)  4.61 us
  transfers between devices with their start and end apart: 15, of which 9 were waited for; matrix products, arithmetic and copies ran while one was open for 0% of the time, Pallas kernels for 0%

profile of v6, /device:TPU:32, one launch (start us, length us, event | category | flops | bytes accessed | tf_op | source)
XLA Modules:
  0.0 182.0 jit_solution(7339475211589299698)
XLA Ops:
  0.6 6.4 %collective-permute-start.1 = (bf16[24,1024]{1,0:T(8,128)(2,1)}, bf16[24,1024]{1,0:T(8,128)(2,1)S(1)}, u32[]{:S(2)}, u32[]{:S(2)}) collective-permute-start(bf16[24,1024]{1,0:T(8,128)(2,1)} %param.5), channel_id=1, source_target_pairs={{0,2},{1,3},{2,0},{3,1},{4,6},{5,7},{6,4},{7,5},{8,10},{9,11},{10,... | collective-permute-start | bytes 147464 | tf_op jit(solution)/shard_map/ppermute | solution.py:58
  7.6 2.4 %collective-permute-start.2 = (bf16[24,1024]{1,0:T(8,128)(2,1)}, bf16[24,1024]{1,0:T(8,128)(2,1)S(1)}, u32[]{:S(2)}, u32[]{:S(2)}) collective-permute-start(bf16[24,1024]{1,0:T(8,128)(2,1)} %param.5), channel_id=1, source_target_pairs={{0,1},{1,2},{2,3},{3,0},{4,5},{5,6},{6,7},{7,4},{8,9},{9,10},{10,1... | collective-permute-start | bytes 147464 | tf_op jit(solution)/shard_map/ppermute | solution.py:58
  10.4 2.4 %collective-permute-done = bf16[24,1024]{1,0:T(8,128)(2,1)S(1)} collective-permute-done((bf16[24,1024]{1,0:T(8,128)(2,1)}, bf16[24,1024]{1,0:T(8,128)(2,1)S(1)}, u32[]{:S(2)}, u32[]{:S(2)}) %collective-permute-start) | collective-permute-done | bytes 49184 | tf_op jit(solution)/shard_map/ppermute | solution.py:58
  12.7 1.7 collective-permute-done.2
  15.2 5.1 %collective-permute-start.3 = (bf16[32,1024]{1,0:T(8,128)(2,1)S(1)}, bf16[32,1024]{1,0:T(8,128)(2,1)S(1)}, u32[]{:S(2)}, u32[]{:S(2)}) collective-permute-start(bf16[32,1024]{1,0:T(8,128)(2,1)S(1)} %pad_maximum_fusion.3), channel_id=1, source_target_pairs={{0,8},{4,12},{8,16},{12,20},{16,24},{20,28},{24,32},{28,36},{32,40... | collective-permute-start | bytes 196616 | tf_op jit(solution)/shard_map/ppermute | solution.py:33
  20.4 2.6 %collective-permute-start.4 = (bf16[96,1024]{1,0:T(8,128)(2,1)S(1)}, bf16[96,1024]{1,0:T(8,128)(2,1)S(1)}, u32[]{:S(2)}, u32[]{:S(2)}) collective-permute-start(bf16[96,1024]{1,0:T(8,128)(2,1)S(1)} %pad_maximum_fusion), channel_id=1, source_target_pairs={{0,4},{4,8},{8,12},{12,16},{16,20},{20,24},{24,28},{28,32},{32,36}... | collective-permute-start | bytes 589832 | tf_op jit(solution)/shard_map/ppermute | solution.py:33
  23.7 1.9 %collective-permute-done.3 = bf16[32,1024]{1,0:T(8,128)(2,1)S(1)} collective-permute-done((bf16[32,1024]{1,0:T(8,128)(2,1)S(1)}, bf16[32,1024]{1,0:T(8,128)(2,1)S(1)}, u32[]{:S(2)}, u32[]{:S(2)}) %collective-permute-start.3) | collective-permute-done | bytes 65568 | tf_op jit(solution)/shard_map/ppermute | solution.py:33
  25.5 6.0 %collective-permute-done.4 = bf16[96,1024]{1,0:T(8,128)(2,1)S(1)} collective-permute-done((bf16[96,1024]{1,0:T(8,128)(2,1)S(1)}, bf16[96,1024]{1,0:T(8,128)(2,1)S(1)}, u32[]{:S(2)}, u32[]{:S(2)}) %collective-permute-start.4) | collective-permute-done | bytes 196640 | tf_op jit(solution)/shard_map/ppermute | solution.py:33
  31.8 4.5 %convolution_convert_fusion = bf16[224,3072]{1,0:T(8,128)(2,1)S(1)} fusion(bf16[1024,3072]{1,0:T(8,128)(2,1)} %param.6, bf16[224,1024]{1,0:T(8,128)(2,1)S(1)} %constant_dynamic-update-slice_fusion, f32[224]{0:T(256)S(1)} %add_rsqrt_fusion), kind=kOutput, calls=%fused_computation.1 | convolution fusion | flops 1410662400 | bytes 8127360 | tf_op jit(solution)/shard_map/dot_general | solution.py:215
  36.4 1.0 copy.26
  37.8 2.8 %exponential_select_fusion = f32[16,96,224]{2,1,0:T(8,128)} fusion(bf16[96,16,64]{0,2,1:T(8,128)(2,1)S(1)} %bitcast.42, bf16[224,16,64]{0,2,1:T(8,128)(2,1)} %bitcast.38, pred[96,224]{1,0:T(8,128)(4,1)} %and_and_fusion), kind=kOutput, calls=%fused_computation.3 | convolution fusion | flops 45072384 | bytes 2053120 | tf_op jit(solution)/shard_map/qhd,khd->hqk/dot_general | solution.py:222
  40.6 2.4 %convolution_convert_fusion.1 = bf16[16,64,96]{2,1,0:T(8,128)(2,1)S(1)} fusion(bf16[224,16,64]{0,2,1:T(8,128)(2,1)S(1)} %bitcast.39, f32[16,96,224]{2,1,0:T(8,128)} %exponential_select_fusion), kind=kOutput, calls=%fused_computation.4 | convolution fusion | flops 44828384 | bytes 2031616 | tf_op jit(solution)/shard_map/hqk,khd->qhd/dot_general | solution.py:233
  43.8 2.1 %broadcast_in_dim.16 = bf16[16,96,1024]{2,1,0:T(8,128)(2,1)} broadcast(bf16[96,1024]{1,0:T(8,128)(2,1)S(1)} %pad_maximum_fusion.2), dimensions={1,2} | broadcast | bytes 3342336 | tf_op jit(solution)/shard_map/broadcast_in_dim | solution.py:25
  45.9 4.6 %all-to-all-start = ((bf16[16,96,1024]{2,1,0:T(8,128)(2,1)}), bf16[16,96,1024]{2,1,0:T(8,128)(2,1)}, u32[]{:S(2)}, u32[]{:S(2)}) async-start(bf16[16,96,1024]{2,1,0:T(8,128)(2,1)} %broadcast_in_dim.16), calls=%async_computation | async-start | bytes 6291456 | tf_op jit(solution)/shard_map/all_to_all | solution.py:26
  50.7 2.0 %collective-permute-start.9 = (bf16[2048,256]{1,0:T(8,128)(2,1)}, bf16[2048,256]{1,0:T(8,128)(2,1)S(1)}, u32[]{:S(2)}, u32[]{:S(2)}) collective-permute-start(bf16[2048,256]{1,0:T(8,128)(2,1)} %b0.1), channel_id=1, source_target_pairs={{0,128},{128,0},{1,129},{129,1},{2,130},{130,2},{3,131},{131,3},{4... | collective-permute-start | bytes 3145736 | tf_op jit(solution)/shard_map/ppermute | solution.py:37
  53.2 23.5 %collective-permute-done.6.h2 = bf16[256,2048]{1,0:T(8,128)(2,1)S(1)} collective-permute-done((bf16[256,2048]{1,0:T(8,128)(2,1)S(1)}, bf16[256,2048]{1,0:T(8,128)(2,1)S(1)}, u32[]{:S(2)}, u32[]{:S(2)}) %collective-permute-start.6) | collective-permute-done | bytes 1048608 | tf_op jit(solution)/shard_map/ppermute | solution.py:37
  76.7 18.6 %collective-permute-done.9.b2 = bf16[2048,256]{1,0:T(8,128)(2,1)S(1)} collective-permute-done((bf16[2048,256]{1,0:T(8,128)(2,1)}, bf16[2048,256]{1,0:T(8,128)(2,1)S(1)}, u32[]{:S(2)}, u32[]{:S(2)}) %collective-permute-start.9) | collective-permute-done | bytes 1048608 | tf_op jit(solution)/shard_map/ppermute | solution.py:37
  97.0 1.1 copy-done.6
  98.0 21.0 %shard_map.68 = bf16[16,776,128]{2,1,0:T(8,128)(2,1)S(1)} custom-call(bf16[1536,1024]{1,0:T(8,128)(2,1)} %bitcast.5.unit_ref, bf16[256,2048]{1,0:T(8,128)(2,1)} %h0.1, bf16[256,2048]{1,0:T(8,128)(2,1)} %copy-done.4, bf16[256,2048]{1,0:T(8,128)(2,1)} %copy-done.2, bf16[256,2048]{1,0:T(8,128)(2,1)} %copy-done.6, bf16[2048,256]{1,0:T(8,128)(2,1)} %b0.1, ...), custom_call_target="tpu_custom_call" | custom-call | flops 12884901888 | bytes 16777216 | tf_op jit(solution)/shard_map/pallas_call | solution.py:180
  119.1 47.0 %all_to_all.10 = bf16[16,776,128]{2,1,0:T(8,128)(2,1)S(1)} all-to-all(bf16[16,776,128]{2,1,0:T(8,128)(2,1)S(1)} %shard_map.68), channel_id=1, replica_groups=mesh['zl'=2,'c'=2,'x'=4,'y'=4,'zh'=4] {'x','y'}, dimensions={0} | all-to-all | bytes 6356992 | tf_op jit(solution)/shard_map/all_to_all | solution.py:243
  166.8 1.1 collective-permute-start.11
  167.9 6.8 %collective-permute-start.13 = (bf16[200,128]{1,0:T(8,128)(2,1)S(1)}, bf16[200,128]{1,0:T(8,128)(2,1)S(1)}, u32[]{:S(2)}, u32[]{:S(2)}) collective-permute-start(bf16[200,128]{1,0:T(8,128)(2,1)S(1)} %get-tuple-element.7), channel_id=1, source_target_pairs={{0,2},{1,3},{2,0},{3,1},{4,6},{5,7},{6,4},{7,5},{8,10},{9,11},{10,... | collective-permute-start | bytes 153608 | tf_op jit(solution)/shard_map/ppermute | solution.py:58
  175.3 2.4 %collective-permute-done.13 = bf16[200,128]{1,0:T(8,128)(2,1)S(1)} collective-permute-done((bf16[200,128]{1,0:T(8,128)(2,1)S(1)}, bf16[200,128]{1,0:T(8,128)(2,1)S(1)}, u32[]{:S(2)}, u32[]{:S(2)}) %collective-permute-start.13) | collective-permute-done | bytes 51232 | tf_op jit(solution)/shard_map/ppermute | solution.py:58
  177.6 2.6 %collective-permute-done.12 = bf16[200,128]{1,0:T(8,128)(2,1)S(1)} collective-permute-done((bf16[200,128]{1,0:T(8,128)(2,1)S(1)}, bf16[200,128]{1,0:T(8,128)(2,1)S(1)}, u32[]{:S(2)}, u32[]{:S(2)}) %collective-permute-start.12) | collective-permute-done | bytes 51232 | tf_op jit(solution)/shard_map/ppermute | solution.py:58
  (74 shorter events, 9.2 us)
Async XLA Ops:
  0.6 42.4 %copy-start = (bf16[1024,1024]{1,0:T(8,128)(2,1)S(1)}, bf16[1024,1024]{1,0:T(8,128)(2,1)}, u32[]{:S(2)}) copy-start(bf16[1024,1024]{1,0:T(8,128)(2,1)} %param.7) | copy-start | bytes 6291460
  0.6 9.7 %collective-permute-start.1 = (bf16[24,1024]{1,0:T(8,128)(2,1)}, bf16[24,1024]{1,0:T(8,128)(2,1)S(1)}, u32[]{:S(2)}, u32[]{:S(2)}) collective-permute-start(bf16[24,1024]{1,0:T(8,128)(2,1)} %param.5), channel_id=1, source_target_pairs={{0,2},{1,3},{2,0},{3,1},{4,6},{5,7},{6,4},{7,5},{8,10},{9,11},{10,... | collective-permute-start | bytes 147464 | tf_op jit(solution)/shard_map/ppermute | solution.py:58
  7.0 5.7 %collective-permute-start = (bf16[24,1024]{1,0:T(8,128)(2,1)}, bf16[24,1024]{1,0:T(8,128)(2,1)S(1)}, u32[]{:S(2)}, u32[]{:S(2)}) collective-permute-start(bf16[24,1024]{1,0:T(8,128)(2,1)} %param.5), channel_id=1, source_target_pairs={{0,3},{1,0},{2,1},{3,2},{4,7},{5,4},{6,5},{7,6},{8,11},{9,8},{10,9... | collective-permute-start | bytes 147464 | tf_op jit(solution)/shard_map/ppermute | solution.py:58
  7.6 6.8 %collective-permute-start.2 = (bf16[24,1024]{1,0:T(8,128)(2,1)}, bf16[24,1024]{1,0:T(8,128)(2,1)S(1)}, u32[]{:S(2)}, u32[]{:S(2)}) collective-permute-start(bf16[24,1024]{1,0:T(8,128)(2,1)} %param.5), channel_id=1, source_target_pairs={{0,1},{1,2},{2,3},{3,0},{4,5},{5,6},{6,7},{7,4},{8,9},{9,10},{10,1... | collective-permute-start | bytes 147464 | tf_op jit(solution)/shard_map/ppermute | solution.py:58
  15.2 10.3 %collective-permute-start.3 = (bf16[32,1024]{1,0:T(8,128)(2,1)S(1)}, bf16[32,1024]{1,0:T(8,128)(2,1)S(1)}, u32[]{:S(2)}, u32[]{:S(2)}) collective-permute-start(bf16[32,1024]{1,0:T(8,128)(2,1)S(1)} %pad_maximum_fusion.3), channel_id=1, source_target_pairs={{0,8},{4,12},{8,16},{12,20},{16,24},{20,28},{24,32},{28,36},{32,40... | collective-permute-start | bytes 196616 | tf_op jit(solution)/shard_map/ppermute | solution.py:33
  20.4 11.2 %collective-permute-start.4 = (bf16[96,1024]{1,0:T(8,128)(2,1)S(1)}, bf16[96,1024]{1,0:T(8,128)(2,1)S(1)}, u32[]{:S(2)}, u32[]{:S(2)}) collective-permute-start(bf16[96,1024]{1,0:T(8,128)(2,1)S(1)} %pad_maximum_fusion), channel_id=1, source_target_pairs={{0,4},{4,8},{8,12},{12,16},{16,20},{20,24},{24,28},{28,32},{32,36}... | collective-permute-start | bytes 589832 | tf_op jit(solution)/shard_map/ppermute | solution.py:33
  45.9 4.6 %copy-start.1 = (bf16[256,2048]{1,0:T(8,128)(2,1)S(1)}, bf16[256,2048]{1,0:T(8,128)(2,1)}, u32[]{:S(2)}) copy-start(bf16[256,2048]{1,0:T(8,128)(2,1)} %h0.1) | copy-start | bytes 3145732
  45.9 52.1 %all-to-all-start = ((bf16[16,96,1024]{2,1,0:T(8,128)(2,1)}), bf16[16,96,1024]{2,1,0:T(8,128)(2,1)}, u32[]{:S(2)}, u32[]{:S(2)}) async-start(bf16[16,96,1024]{2,1,0:T(8,128)(2,1)} %broadcast_in_dim.16), calls=%async_computation | async-start | bytes 6291456 | tf_op jit(solution)/shard_map/all_to_all | solution.py:26
  50.6 26.1 %collective-permute-start.6 = (bf16[256,2048]{1,0:T(8,128)(2,1)S(1)}, bf16[256,2048]{1,0:T(8,128)(2,1)S(1)}, u32[]{:S(2)}, u32[]{:S(2)}) collective-permute-start(bf16[256,2048]{1,0:T(8,128)(2,1)S(1)} %copy-done.1), channel_id=1, source_target_pairs={{0,128},{128,0},{1,129},{129,1},{2,130},{130,2},{3,131},{131,3},{4... | collective-permute-start | bytes 3145736 | tf_op jit(solution)/shard_map/ppermute | solution.py:37
  50.7 44.6 %collective-permute-start.9 = (bf16[2048,256]{1,0:T(8,128)(2,1)}, bf16[2048,256]{1,0:T(8,128)(2,1)S(1)}, u32[]{:S(2)}, u32[]{:S(2)}) collective-permute-start(bf16[2048,256]{1,0:T(8,128)(2,1)} %b0.1), channel_id=1, source_target_pairs={{0,128},{128,0},{1,129},{129,1},{2,130},{130,2},{3,131},{131,3},{4... | collective-permute-start | bytes 3145736 | tf_op jit(solution)/shard_map/ppermute | solution.py:37
  52.7 42.6 %collective-permute-start.5 = (bf16[256,2048]{1,0:T(8,128)(2,1)S(1)}, bf16[256,2048]{1,0:T(8,128)(2,1)S(1)}, u32[]{:S(2)}, u32[]{:S(2)}) collective-permute-start(bf16[256,2048]{1,0:T(8,128)(2,1)S(1)} %copy-done.1), channel_id=1, source_target_pairs={{0,64},{64,0},{1,65},{65,1},{2,66},{66,2},{3,67},{67,3},{4,68},{68... | collective-permute-start | bytes 3145736 | tf_op jit(solution)/shard_map/ppermute | solution.py:37
  52.7 42.6 %collective-permute-start.8 = (bf16[2048,256]{1,0:T(8,128)(2,1)}, bf16[2048,256]{1,0:T(8,128)(2,1)S(1)}, u32[]{:S(2)}, u32[]{:S(2)}) collective-permute-start(bf16[2048,256]{1,0:T(8,128)(2,1)} %b0.1), channel_id=1, source_target_pairs={{0,64},{64,0},{1,65},{65,1},{2,66},{66,2},{3,67},{67,3},{4,68},{68... | collective-permute-start | bytes 3145736 | tf_op jit(solution)/shard_map/ppermute | solution.py:37
  76.7 18.6 %copy-start.2 = (bf16[256,2048]{1,0:T(8,128)(2,1)}, bf16[256,2048]{1,0:T(8,128)(2,1)S(1)}, u32[]{:S(2)}) copy-start(bf16[256,2048]{1,0:T(8,128)(2,1)S(1)} %collective-permute-done.6.h2) | copy-start | bytes 3145732
  76.7 18.6 %collective-permute-start.7 = (bf16[256,2048]{1,0:T(8,128)(2,1)S(1)}, bf16[256,2048]{1,0:T(8,128)(2,1)S(1)}, u32[]{:S(2)}, u32[]{:S(2)}) collective-permute-start(bf16[256,2048]{1,0:T(8,128)(2,1)S(1)} %collective-permute-done.6.h2), channel_id=1, source_target_pairs={{0,64},{64,0},{1,65},{65,1},{2,66},{66,2},{3,67},{67,3},{4,68},{68... | collective-permute-start | bytes 3145736 | tf_op jit(solution)/shard_map/ppermute | solution.py:37
  95.2 1.0 copy-start.3
  95.2 2.8 %collective-permute-start.10 = (bf16[2048,256]{1,0:T(8,128)(2,1)S(1)}, bf16[2048,256]{1,0:T(8,128)(2,1)}, u32[]{:S(2)}, u32[]{:S(2)}) collective-permute-start(bf16[2048,256]{1,0:T(8,128)(2,1)S(1)} %collective-permute-done.9.b2), channel_id=1, source_target_pairs={{0,64},{64,0},{1,65},{65,1},{2,66},{66,2},{3,67},{67,3},{4,68},{68... | collective-permute-start | bytes 3145736 | tf_op jit(solution)/shard_map/ppermute | solution.py:37
  95.3 1.4 copy-start.4
  95.3 1.7 copy-start.5
  97.0 1.1 copy-start.6
  166.8 8.5 %collective-permute-start.11 = (bf16[200,128]{1,0:T(8,128)(2,1)S(1)}, bf16[200,128]{1,0:T(8,128)(2,1)S(1)}, u32[]{:S(2)}, u32[]{:S(2)}) collective-permute-start(bf16[200,128]{1,0:T(8,128)(2,1)S(1)} %get-tuple-element.6), channel_id=1, source_target_pairs={{0,1},{1,2},{2,3},{3,0},{4,5},{5,6},{6,7},{7,4},{8,9},{9,10},{10,1... | collective-permute-start | bytes 153608 | tf_op jit(solution)/shard_map/ppermute | solution.py:58
  167.9 9.7 %collective-permute-start.13 = (bf16[200,128]{1,0:T(8,128)(2,1)S(1)}, bf16[200,128]{1,0:T(8,128)(2,1)S(1)}, u32[]{:S(2)}, u32[]{:S(2)}) collective-permute-start(bf16[200,128]{1,0:T(8,128)(2,1)S(1)} %get-tuple-element.7), channel_id=1, source_target_pairs={{0,2},{1,3},{2,0},{3,1},{4,6},{5,7},{6,4},{7,5},{8,10},{9,11},{10,... | collective-permute-start | bytes 153608 | tf_op jit(solution)/shard_map/ppermute | solution.py:58
  174.7 5.6 %collective-permute-start.12 = (bf16[200,128]{1,0:T(8,128)(2,1)S(1)}, bf16[200,128]{1,0:T(8,128)(2,1)S(1)}, u32[]{:S(2)}, u32[]{:S(2)}) collective-permute-start(bf16[200,128]{1,0:T(8,128)(2,1)S(1)} %get-tuple-element.8), channel_id=1, source_target_pairs={{0,3},{1,0},{2,1},{3,2},{4,7},{5,4},{6,5},{7,6},{8,11},{9,8},{10,9... | collective-permute-start | bytes 153608 | tf_op jit(solution)/shard_map/ppermute | solution.py:58

commit v7 on v6

--- a/solution.py
+++ b/solution.py
@@ -80,7 +80,8 @@
 def column_sum(blocks):
     total = blocks[0].astype(F32)
     for distance in (1, 3, 2):
-        total = total + turned(blocks[distance], distance).astype(F32)
+        block = turned(blocks[distance], distance)
+        total = total + block.astype(F32)
     return total
 
 
@@ -198,6 +199,84 @@
     )(unit, *[pltpu.with_memory_space_constraint(p, pltpu.HBM) for p in (*head_parts, *back_parts)])
 
 
+def attention_kernel(first_ref, far_ref, near_ref, own_ref, qkv_ref, merge_ref, out_ref, normed, query, key, value, context,
+                     weight, merge, sems):
+    block, width = own_ref.shape
+    wide = weight.shape[2]
+    many = weight.shape[0]
+    copies = [
+        pltpu.make_async_copy(qkv_ref.at[:, i * wide : (i + 1) * wide], weight.at[i], sems.at[i])
+        for i in range(many)
+    ] + [pltpu.make_async_copy(merge_ref, merge, sems.at[many])]
+    for copy in copies:
+        copy.start()
+    past = far_ref.shape[0] + near_ref.shape[0]
+    keys = past + block
+    row = 0
+    for ref in (far_ref, near_ref, own_ref):
+        normed[row : row + ref.shape[0], :] = root_norm(ref[...].astype(F32)).astype(BF)
+        row += ref.shape[0]
+    for i in range(many):
+        copies[i].wait()
+        part, start = divmod(i * wide, width)
+        ref = (query, key, value)[part]
+        span = slice(start, start + wide)
+        lowest = past if part == 0 else 0
+        product = jnp.dot(normed[lowest:keys, :], weight[i], preferred_element_type=F32)
+        ref[0 : keys - lowest, span] = product.astype(BF)
+        if part:
+            ref[keys:, span] = jnp.zeros((ref.shape[0] - keys, wide), BF)
+    padded = key.shape[0]
+    r = lax.broadcasted_iota(jnp.int32, (block, padded), 0)
+    j = lax.broadcasted_iota(jnp.int32, (block, padded), 1)
+    allowed = (j <= r + past) & (j > r + past - WIN) & (j < keys) & (first_ref[0] - past + j >= 0)
+    lane = lax.broadcasted_iota(jnp.int32, (block, 128), 1)
+    for pair in range(width // 128):
+        span = slice(pair * 128, (pair + 1) * 128)
+        both = query[:, span].astype(F32)
+        parts = []
+        for side in range(2):
+            mine = (lane >= HEAD_DIM) == (side == 1)
+            one = jnp.where(mine, both, 0.0).astype(BF)
+            scores = lax.dot_general(one, key[:, span], (((1,), (1,)), ((), ())), preferred_element_type=F32)
+            scores = 50.0 * jnp.tanh(scores * (1.0 / math.sqrt(HEAD_DIM)) * (1.0 / 50.0))
+            expo = jnp.where(allowed, jnp.exp(scores), 0.0)
+            weights = (expo / jnp.sum(expo, axis=-1, keepdims=True)).astype(BF)
+            parts.append(jnp.dot(weights, value[:, span], preferred_element_type=F32))
+        context[:, span] = jnp.where(lane >= HEAD_DIM, parts[1], parts[0]).astype(BF)
+    copies[many].wait()
+    merged = jnp.dot(context[...], merge[...], preferred_element_type=F32)
+    out_ref[...] = (own_ref[...].astype(F32) + merged).astype(BF)
+
+
+def attended(first, far, near, own, qkv_weight, merge_weight):
+    block, width = own.shape
+    keys = far.shape[0] + near.shape[0] + block
+    padded = -(-keys // 128) * 128
+    vmem = pl.BlockSpec(memory_space=pltpu.VMEM)
+    return pl.pallas_call(
+        attention_kernel,
+        in_specs=[pl.BlockSpec(memory_space=pltpu.SMEM)] + [vmem] * 3 + [pl.BlockSpec(memory_space=pl.ANY)] * 2,
+        out_specs=vmem,
+        out_shape=jax.ShapeDtypeStruct((block, width), BF),
+        scratch_shapes=[
+            pltpu.VMEM((keys, width), BF),
+            pltpu.VMEM((block, width), BF),
+            pltpu.VMEM((padded, width), BF),
+            pltpu.VMEM((padded, width), BF),
+            pltpu.VMEM((block, width), BF),
+            pltpu.VMEM((3 * width // 512, width, 512), BF),
+            pltpu.VMEM((width, width), BF),
+            pltpu.SemaphoreType.DMA((3 * width // 512 + 1,)),
+        ],
+        compiler_params=pltpu.CompilerParams(vmem_limit_bytes=24 * 2**20),
+        cost_estimate=pl.CostEstimate(
+            flops=8 * keys * width * width, bytes_accessed=9 * 2**20, transcendentals=2 * HEADS * block * keys
+        ),
+        name="qkv",
+    )(first, far, near, own, *[pltpu.with_memory_space_constraint(w, pltpu.HBM) for w in (qkv_weight, merge_weight)])
+
+
 def body(frames, qkv_weight, attn_out_weight, head_weight, back_weight):
     rows = frames.shape[0]
     width = frames.shape[1]
@@ -210,31 +289,8 @@
     own = column_rows(frames)
     prev = passed_along(own, BLOCKS, 1)
     prev2 = passed_along(own[block - far :], BLOCKS, 2)
-    keys = WIN + block
-    normed = root_norm(jnp.concatenate([prev2, prev, own], axis=0).astype(F32)).astype(BF)
-    project = jnp.dot(normed, qkv_weight, preferred_element_type=F32).astype(BF)
-    query = project[WIN:, :width].reshape(block, HEADS, HEAD_DIM)
-    key_part = project[:, width : 2 * width].reshape(keys, HEADS, HEAD_DIM)
-    value_part = project[:, 2 * width :].reshape(keys, HEADS, HEAD_DIM)
-    first = lax.axis_index(BLOCKS) * block
-    query_pos = first + jnp.arange(block, dtype=jnp.int32)
-    key_pos = first - WIN + jnp.arange(keys, dtype=jnp.int32)
-    scores = jnp.einsum(
-        "qhd,khd->hqk", query, key_part, preferred_element_type=F32
-    ) / math.sqrt(HEAD_DIM)
-    scores = 50.0 * jnp.tanh(scores / 50.0)
-    allowed = (
-        (key_pos[None, :] <= query_pos[:, None])
-        & (key_pos[None, :] > query_pos[:, None] - WIN)
-        & (key_pos[None, :] >= 0)
-    )
-    expo = jnp.where(allowed[None], jnp.exp(scores), 0.0)
-    weights = (expo / jnp.sum(expo, axis=-1, keepdims=True)).astype(BF)
-    context = jnp.einsum("hqk,khd->qhd", weights, value_part, preferred_element_type=F32)
-    context = context.astype(BF).reshape(block, width)
-    hidden = (
-        own.astype(F32) + jnp.dot(context, attn_out_weight, preferred_element_type=F32)
-    ).astype(BF)
+    first = lax.axis_index(BLOCKS).astype(jnp.int32)[None] * block
+    hidden = attended(first, prev2, prev, own, qkv_weight, attn_out_weight)
     hidden = own_rows_first(hidden)
     unit = root_norm(hidden.astype(F32)).astype(BF)
 

time: 182 us -> 175 us (0.962)
  matrix products: 10.2 us -> 0 us
  Pallas kernels: 21 us -> 27.7 us
    dot_general x4 -> x0, matrix products: 10.2 us -> none  [the longest x1 4.46 us: body(): project = jnp.dot(normed, qkv_weight, preferred_element_type=F32).astype(BF)]
    pallas_call x0 -> x1, Pallas kernels: none -> 7.85 us  [attended(): pl.pallas_call(attention_kernel, in_specs=[pl.BlockSpec(memory_space=pltp...]
    ppermute x6, waiting for transfers between devices: 42.1 us -> 44.5 us  [swapped(): return lax.ppermute(block, axis, [(0, 1), (1, 0)])]
    ppermute x2, waiting for transfers between devices: 7.9 us -> 5.94 us  [passed_along(): return lax.ppermute(block, axes, route)]
  transfers between devices with their start and end apart: 15 -> 15, of which waited for: 9 -> 8; matrix products, arithmetic and copies ran while one was open for 0% -> 0% of each run, Pallas kernels for 0% -> 0%
where the time goes in v7:
time: 175 us
  waiting for transfers between devices  59.8 us (34%)
  blocking collectives  47 us (27%)
  starting transfers between devices  31.2 us (18%)
  Pallas kernels  27.7 us (16%)
  local copies, waits for them, and re-layouts  5.32 us (3%)
  other arithmetic  2.84 us (2%)
    all_to_all x1, blocking collectives, body(): summed = jnp.sum(lax.all_to_all(sent, PLANE, 0, 0).astype(F32), axis=0)  47 us
    ppermute x6, waiting for transfers between devices, swapped(): return lax.ppermute(block, axis, [(0, 1), (1, 0)])  44.5 us
    pallas_call x1, Pallas kernels, label_sums(): pl.pallas_call(label_kernel, grid=(STEPS,), in_specs=[pl.BlockSpec((count...  19.8 us
    ppermute x6, starting transfers between devices, turned(): lax.ppermute(block, COL, [(i, (i + distance) % size) for i in range(size)])  16.5 us
    ppermute x6, waiting for transfers between devices, turned(): lax.ppermute(block, COL, [(i, (i + distance) % size) for i in range(size)])  9.42 us
    ppermute x2, starting transfers between devices, passed_along(): return lax.ppermute(block, axes, route)  8.29 us
    pallas_call x1, Pallas kernels, attended(): pl.pallas_call(attention_kernel, in_specs=[pl.BlockSpec(memory_space=pltp...  7.85 us
    ppermute x2, waiting for transfers between devices, passed_along(): return lax.ppermute(block, axes, route)  5.94 us
  transfers between devices with their start and end apart: 15, of which 8 were waited for; matrix products, arithmetic and copies ran while one was open for 0% of the time, Pallas kernels for 0%

profile of v7, /device:TPU:32, one launch (start us, length us, event | category | flops | bytes accessed | tf_op | source)
XLA Modules:
  0.0 174.6 jit_solution(6928957888115577570)
XLA Ops:
  0.6 5.5 %collective-permute-start.1 = (bf16[24,1024]{1,0:T(8,128)(2,1)}, bf16[24,1024]{1,0:T(8,128)(2,1)S(1)}, u32[]{:S(2)}, u32[]{:S(2)}) collective-permute-start(bf16[24,1024]{1,0:T(8,128)(2,1)} %param.5), channel_id=1, source_target_pairs={{0,3},{1,0},{2,1},{3,2},{4,7},{5,4},{6,5},{7,6},{8,11},{9,8},{10,9... | collective-permute-start | bytes 147464 | tf_op jit(solution)/shard_map/ppermute | solution.py:58
  6.1 3.8 %collective-permute-start.2 = (bf16[24,1024]{1,0:T(8,128)(2,1)}, bf16[24,1024]{1,0:T(8,128)(2,1)S(1)}, u32[]{:S(2)}, u32[]{:S(2)}) collective-permute-start(bf16[24,1024]{1,0:T(8,128)(2,1)} %param.5), channel_id=1, source_target_pairs={{0,2},{1,3},{2,0},{3,1},{4,6},{5,7},{6,4},{7,5},{8,10},{9,11},{10,... | collective-permute-start | bytes 147464 | tf_op jit(solution)/shard_map/ppermute | solution.py:58
  9.9 5.2 %collective-permute-done = bf16[24,1024]{1,0:T(8,128)(2,1)S(1)} collective-permute-done((bf16[24,1024]{1,0:T(8,128)(2,1)}, bf16[24,1024]{1,0:T(8,128)(2,1)S(1)}, u32[]{:S(2)}, u32[]{:S(2)}) %collective-permute-start) | collective-permute-done | bytes 49184 | tf_op jit(solution)/shard_map/ppermute | solution.py:58
  15.2 0.8 broadcast_select_fusion.21
  16.0 3.5 %collective-permute-start.4 = (bf16[96,1024]{1,0:T(8,128)(2,1)S(1)}, bf16[96,1024]{1,0:T(8,128)(2,1)S(1)}, u32[]{:S(2)}, u32[]{:S(2)}) collective-permute-start(bf16[96,1024]{1,0:T(8,128)(2,1)S(1)} %pad_maximum_fusion.own_ref), channel_id=1, source_target_pairs={{0,4},{4,8},{8,12},{12,16},{16,20},{20,24},{24,28},{28,32},{32,36}... | collective-permute-start | bytes 589832 | tf_op jit(solution)/shard_map/ppermute | solution.py:33
  19.5 4.8 %collective-permute-start.3 = (bf16[32,1024]{1,0:T(8,128)(2,1)S(1)}, bf16[32,1024]{1,0:T(8,128)(2,1)S(1)}, u32[]{:S(2)}, u32[]{:S(2)}) collective-permute-start(bf16[32,1024]{1,0:T(8,128)(2,1)S(1)} %pad_maximum_fusion.3), channel_id=1, source_target_pairs={{0,8},{4,12},{8,16},{12,20},{16,24},{20,28},{24,32},{28,36},{32,40... | collective-permute-start | bytes 196616 | tf_op jit(solution)/shard_map/ppermute | solution.py:33
  24.3 5.9 %collective-permute-done.3.far_ref = bf16[32,1024]{1,0:T(8,128)(2,1)S(1)} collective-permute-done((bf16[32,1024]{1,0:T(8,128)(2,1)S(1)}, bf16[32,1024]{1,0:T(8,128)(2,1)S(1)}, u32[]{:S(2)}, u32[]{:S(2)}) %collective-permute-start.3) | collective-permute-done | bytes 65568 | tf_op jit(solution)/shard_map/ppermute | solution.py:33
  30.3 7.8 %qkv.1 = bf16[96,1024]{1,0:T(8,128)(2,1)S(1)} custom-call(s32[1]{0:T(128)} %bitcast.first_ref, bf16[32,1024]{1,0:T(8,128)(2,1)S(1)} %collective-permute-done.3.far_ref, bf16[96,1024]{1,0:T(8,128)(2,1)S(1)} %collective-permute-done.4.near_ref, bf16[96,1024]{1,0:T(8,128)(2,1)S(1)} %pad_maximum_fusion.own_ref, bf16[1024,3072]{1,0:T(8,128)(2,1)} %qkv_ref.1, ...), custom_call_target="tpu_custom_call" | custom-call | flops 1879048192 | bytes 9437184 | tf_op jit(solution)/shard_map/qkv/pallas_call | solution.py:257
  38.5 2.0 %broadcast_in_dim.2 = bf16[16,96,1024]{2,1,0:T(8,128)(2,1)} broadcast(bf16[96,1024]{1,0:T(8,128)(2,1)S(1)} %pad_maximum_fusion.2), dimensions={1,2} | broadcast | bytes 3342336 | tf_op jit(solution)/shard_map/broadcast_in_dim | solution.py:25
  40.5 3.7 %all-to-all-start = ((bf16[16,96,1024]{2,1,0:T(8,128)(2,1)}), bf16[16,96,1024]{2,1,0:T(8,128)(2,1)S(1)}, u32[]{:S(2)}, u32[]{:S(2)}) async-start(bf16[16,96,1024]{2,1,0:T(8,128)(2,1)} %broadcast_in_dim.2), calls=%async_computation | async-start | bytes 6291456 | tf_op jit(solution)/shard_map/all_to_all | solution.py:26
  44.5 1.9 %collective-permute-start.9 = (bf16[2048,256]{1,0:T(8,128)(2,1)}, bf16[2048,256]{1,0:T(8,128)(2,1)S(1)}, u32[]{:S(2)}, u32[]{:S(2)}) collective-permute-start(bf16[2048,256]{1,0:T(8,128)(2,1)} %b0.1), channel_id=1, source_target_pairs={{0,128},{128,0},{1,129},{129,1},{2,130},{130,2},{3,131},{131,3},{4... | collective-permute-start | bytes 3145736 | tf_op jit(solution)/shard_map/ppermute | solution.py:37
  46.9 23.7 %collective-permute-done.6.h2 = bf16[256,2048]{1,0:T(8,128)(2,1)S(1)} collective-permute-done((bf16[256,2048]{1,0:T(8,128)(2,1)}, bf16[256,2048]{1,0:T(8,128)(2,1)S(1)}, u32[]{:S(2)}, u32[]{:S(2)}) %collective-permute-start.6) | collective-permute-done | bytes 1048608 | tf_op jit(solution)/shard_map/ppermute | solution.py:37
  70.6 20.6 %collective-permute-done.9.b2 = bf16[2048,256]{1,0:T(8,128)(2,1)S(1)} collective-permute-done((bf16[2048,256]{1,0:T(8,128)(2,1)}, bf16[2048,256]{1,0:T(8,128)(2,1)S(1)}, u32[]{:S(2)}, u32[]{:S(2)}) %collective-permute-start.9) | collective-permute-done | bytes 1048608 | tf_op jit(solution)/shard_map/ppermute | solution.py:37
  91.3 1.0 copy-done.1
  92.9 1.0 copy-done.4
  94.0 19.8 %shard_map.68 = bf16[16,776,128]{2,1,0:T(8,128)(2,1)S(1)} custom-call(bf16[1536,1024]{1,0:T(8,128)(2,1)S(1)} %bitcast.24, bf16[256,2048]{1,0:T(8,128)(2,1)} %h0.1, bf16[256,2048]{1,0:T(8,128)(2,1)} %copy-done.2, bf16[256,2048]{1,0:T(8,128)(2,1)} %copy-done, bf16[256,2048]{1,0:T(8,128)(2,1)} %copy-done.4, bf16[2048,256]{1,0:T(8,128)(2,1)} %b0.1, ...), custom_call_target="tpu_custom_call" | custom-call | flops 12884901888 | bytes 16777216 | tf_op jit(solution)/shard_map/pallas_call | solution.py:181
  113.8 47.0 %all_to_all.10 = bf16[16,776,128]{2,1,0:T(8,128)(2,1)S(1)} all-to-all(bf16[16,776,128]{2,1,0:T(8,128)(2,1)S(1)} %shard_map.68), channel_id=1, replica_groups=mesh['zl'=2,'c'=2,'x'=4,'y'=4,'zh'=4] {'x','y'}, dimensions={0} | all-to-all | bytes 6356992 | tf_op jit(solution)/shard_map/all_to_all | solution.py:299
  161.5 1.8 %collective-permute-start.11 = (bf16[200,128]{1,0:T(8,128)(2,1)S(1)}, bf16[200,128]{1,0:T(8,128)(2,1)S(1)}, u32[]{:S(2)}, u32[]{:S(2)}) collective-permute-start(bf16[200,128]{1,0:T(8,128)(2,1)S(1)} %get-tuple-element.4), channel_id=1, source_target_pairs={{0,1},{1,2},{2,3},{3,0},{4,5},{5,6},{6,7},{7,4},{8,9},{9,10},{10,1... | collective-permute-start | bytes 153608 | tf_op jit(solution)/shard_map/ppermute | solution.py:58
  163.3 4.2 %collective-permute-start.13 = (bf16[200,128]{1,0:T(8,128)(2,1)S(1)}, bf16[200,128]{1,0:T(8,128)(2,1)S(1)}, u32[]{:S(2)}, u32[]{:S(2)}) collective-permute-start(bf16[200,128]{1,0:T(8,128)(2,1)S(1)} %get-tuple-element.5), channel_id=1, source_target_pairs={{0,2},{1,3},{2,0},{3,1},{4,6},{5,7},{6,4},{7,5},{8,10},{9,11},{10,... | collective-permute-start | bytes 153608 | tf_op jit(solution)/shard_map/ppermute | solution.py:58
  167.5 1.2 collective-permute-start.12
  168.8 3.0 %collective-permute-done.13 = bf16[200,128]{1,0:T(8,128)(2,1)S(1)} collective-permute-done((bf16[200,128]{1,0:T(8,128)(2,1)S(1)}, bf16[200,128]{1,0:T(8,128)(2,1)S(1)}, u32[]{:S(2)}, u32[]{:S(2)}) %collective-permute-start.13) | collective-permute-done | bytes 51232 | tf_op jit(solution)/shard_map/ppermute | solution.py:58
  171.8 1.1 collective-permute-done.12
  173.0 0.5 log.3
  173.9 0.7 add_convert_fusion
  (50 shorter events, 3.1 us)
Async XLA Ops:
  0.6 9.3 %collective-permute-start.1 = (bf16[24,1024]{1,0:T(8,128)(2,1)}, bf16[24,1024]{1,0:T(8,128)(2,1)S(1)}, u32[]{:S(2)}, u32[]{:S(2)}) collective-permute-start(bf16[24,1024]{1,0:T(8,128)(2,1)} %param.5), channel_id=1, source_target_pairs={{0,3},{1,0},{2,1},{3,2},{4,7},{5,4},{6,5},{7,6},{8,11},{9,8},{10,9... | collective-permute-start | bytes 147464 | tf_op jit(solution)/shard_map/ppermute | solution.py:58
  6.1 9.0 %collective-permute-start = (bf16[24,1024]{1,0:T(8,128)(2,1)}, bf16[24,1024]{1,0:T(8,128)(2,1)S(1)}, u32[]{:S(2)}, u32[]{:S(2)}) collective-permute-start(bf16[24,1024]{1,0:T(8,128)(2,1)} %param.5), channel_id=1, source_target_pairs={{0,1},{1,2},{2,3},{3,0},{4,5},{5,6},{6,7},{7,4},{8,9},{9,10},{10,1... | collective-permute-start | bytes 147464 | tf_op jit(solution)/shard_map/ppermute | solution.py:58
  6.1 9.0 %collective-permute-start.2 = (bf16[24,1024]{1,0:T(8,128)(2,1)}, bf16[24,1024]{1,0:T(8,128)(2,1)S(1)}, u32[]{:S(2)}, u32[]{:S(2)}) collective-permute-start(bf16[24,1024]{1,0:T(8,128)(2,1)} %param.5), channel_id=1, source_target_pairs={{0,2},{1,3},{2,0},{3,1},{4,6},{5,7},{6,4},{7,5},{8,10},{9,11},{10,... | collective-permute-start | bytes 147464 | tf_op jit(solution)/shard_map/ppermute | solution.py:58
  16.0 14.3 %collective-permute-start.4 = (bf16[96,1024]{1,0:T(8,128)(2,1)S(1)}, bf16[96,1024]{1,0:T(8,128)(2,1)S(1)}, u32[]{:S(2)}, u32[]{:S(2)}) collective-permute-start(bf16[96,1024]{1,0:T(8,128)(2,1)S(1)} %pad_maximum_fusion.own_ref), channel_id=1, source_target_pairs={{0,4},{4,8},{8,12},{12,16},{16,20},{20,24},{24,28},{28,32},{32,36}... | collective-permute-start | bytes 589832 | tf_op jit(solution)/shard_map/ppermute | solution.py:33
  19.5 10.8 %collective-permute-start.3 = (bf16[32,1024]{1,0:T(8,128)(2,1)S(1)}, bf16[32,1024]{1,0:T(8,128)(2,1)S(1)}, u32[]{:S(2)}, u32[]{:S(2)}) collective-permute-start(bf16[32,1024]{1,0:T(8,128)(2,1)S(1)} %pad_maximum_fusion.3), channel_id=1, source_target_pairs={{0,8},{4,12},{8,16},{12,20},{16,24},{20,28},{24,32},{28,36},{32,40... | collective-permute-start | bytes 196616 | tf_op jit(solution)/shard_map/ppermute | solution.py:33
  40.5 53.5 %all-to-all-start = ((bf16[16,96,1024]{2,1,0:T(8,128)(2,1)}), bf16[16,96,1024]{2,1,0:T(8,128)(2,1)S(1)}, u32[]{:S(2)}, u32[]{:S(2)}) async-start(bf16[16,96,1024]{2,1,0:T(8,128)(2,1)} %broadcast_in_dim.2), calls=%async_computation | async-start | bytes 6291456 | tf_op jit(solution)/shard_map/all_to_all | solution.py:26
  44.3 26.3 %collective-permute-start.6 = (bf16[256,2048]{1,0:T(8,128)(2,1)}, bf16[256,2048]{1,0:T(8,128)(2,1)S(1)}, u32[]{:S(2)}, u32[]{:S(2)}) collective-permute-start(bf16[256,2048]{1,0:T(8,128)(2,1)} %h0.1), channel_id=1, source_target_pairs={{0,128},{128,0},{1,129},{129,1},{2,130},{130,2},{3,131},{131,3},{4... | collective-permute-start | bytes 3145736 | tf_op jit(solution)/shard_map/ppermute | solution.py:37
  44.5 46.7 %collective-permute-start.9 = (bf16[2048,256]{1,0:T(8,128)(2,1)}, bf16[2048,256]{1,0:T(8,128)(2,1)S(1)}, u32[]{:S(2)}, u32[]{:S(2)}) collective-permute-start(bf16[2048,256]{1,0:T(8,128)(2,1)} %b0.1), channel_id=1, source_target_pairs={{0,128},{128,0},{1,129},{129,1},{2,130},{130,2},{3,131},{131,3},{4... | collective-permute-start | bytes 3145736 | tf_op jit(solution)/shard_map/ppermute | solution.py:37
  46.4 44.8 %collective-permute-start.5 = (bf16[256,2048]{1,0:T(8,128)(2,1)}, bf16[256,2048]{1,0:T(8,128)(2,1)S(1)}, u32[]{:S(2)}, u32[]{:S(2)}) collective-permute-start(bf16[256,2048]{1,0:T(8,128)(2,1)} %h0.1), channel_id=1, source_target_pairs={{0,64},{64,0},{1,65},{65,1},{2,66},{66,2},{3,67},{67,3},{4,68},{68... | collective-permute-start | bytes 3145736 | tf_op jit(solution)/shard_map/ppermute | solution.py:37
  46.4 44.9 %collective-permute-start.8 = (bf16[2048,256]{1,0:T(8,128)(2,1)}, bf16[2048,256]{1,0:T(8,128)(2,1)S(1)}, u32[]{:S(2)}, u32[]{:S(2)}) collective-permute-start(bf16[2048,256]{1,0:T(8,128)(2,1)} %b0.1), channel_id=1, source_target_pairs={{0,64},{64,0},{1,65},{65,1},{2,66},{66,2},{3,67},{67,3},{4,68},{68... | collective-permute-start | bytes 3145736 | tf_op jit(solution)/shard_map/ppermute | solution.py:37
  70.6 20.7 %copy-start = (bf16[256,2048]{1,0:T(8,128)(2,1)}, bf16[256,2048]{1,0:T(8,128)(2,1)S(1)}, u32[]{:S(2)}) copy-start(bf16[256,2048]{1,0:T(8,128)(2,1)S(1)} %collective-permute-done.6.h2) | copy-start | bytes 3145732
  70.6 20.7 %collective-permute-start.7 = (bf16[256,2048]{1,0:T(8,128)(2,1)S(1)}, bf16[256,2048]{1,0:T(8,128)(2,1)S(1)}, u32[]{:S(2)}, u32[]{:S(2)}) collective-permute-start(bf16[256,2048]{1,0:T(8,128)(2,1)S(1)} %collective-permute-done.6.h2), channel_id=1, source_target_pairs={{0,64},{64,0},{1,65},{65,1},{2,66},{66,2},{3,67},{67,3},{4,68},{68... | collective-permute-start | bytes 3145736 | tf_op jit(solution)/shard_map/ppermute | solution.py:37
  91.2 1.0 copy-start.1
  91.2 2.8 %collective-permute-start.10 = (bf16[2048,256]{1,0:T(8,128)(2,1)S(1)}, bf16[2048,256]{1,0:T(8,128)(2,1)}, u32[]{:S(2)}, u32[]{:S(2)}) collective-permute-start(bf16[2048,256]{1,0:T(8,128)(2,1)S(1)} %collective-permute-done.9.b2), channel_id=1, source_target_pairs={{0,64},{64,0},{1,65},{65,1},{2,66},{66,2},{3,67},{67,3},{4,68},{68... | collective-permute-start | bytes 3145736 | tf_op jit(solution)/shard_map/ppermute | solution.py:37
  91.2 1.3 copy-start.2
  91.2 1.6 copy-start.3
  92.9 1.0 copy-start.4
  161.5 7.3 %collective-permute-start.11 = (bf16[200,128]{1,0:T(8,128)(2,1)S(1)}, bf16[200,128]{1,0:T(8,128)(2,1)S(1)}, u32[]{:S(2)}, u32[]{:S(2)}) collective-permute-start(bf16[200,128]{1,0:T(8,128)(2,1)S(1)} %get-tuple-element.4), channel_id=1, source_target_pairs={{0,1},{1,2},{2,3},{3,0},{4,5},{5,6},{6,7},{7,4},{8,9},{9,10},{10,1... | collective-permute-start | bytes 153608 | tf_op jit(solution)/shard_map/ppermute | solution.py:58
  163.3 8.5 %collective-permute-start.13 = (bf16[200,128]{1,0:T(8,128)(2,1)S(1)}, bf16[200,128]{1,0:T(8,128)(2,1)S(1)}, u32[]{:S(2)}, u32[]{:S(2)}) collective-permute-start(bf16[200,128]{1,0:T(8,128)(2,1)S(1)} %get-tuple-element.5), channel_id=1, source_target_pairs={{0,2},{1,3},{2,0},{3,1},{4,6},{5,7},{6,4},{7,5},{8,10},{9,11},{10,... | collective-permute-start | bytes 153608 | tf_op jit(solution)/shard_map/ppermute | solution.py:58
  167.5 5.4 %collective-permute-start.12 = (bf16[200,128]{1,0:T(8,128)(2,1)S(1)}, bf16[200,128]{1,0:T(8,128)(2,1)S(1)}, u32[]{:S(2)}, u32[]{:S(2)}) collective-permute-start(bf16[200,128]{1,0:T(8,128)(2,1)S(1)} %get-tuple-element.6), channel_id=1, source_target_pairs={{0,3},{1,0},{2,1},{3,2},{4,7},{5,4},{6,5},{7,6},{8,11},{9,8},{10,9... | collective-permute-start | bytes 153608 | tf_op jit(solution)/shard_map/ppermute | solution.py:58

commit v8 on v7

--- a/solution.py
+++ b/solution.py
@@ -20,13 +20,6 @@
 EVERY = BLOCKS + (COL,)
 
 
-def gathered(block, axes):
-    size = lax.axis_size(axes)
-    copies = lax.optimization_barrier(jnp.broadcast_to(block[None], (size,) + block.shape))
-    parts = lax.all_to_all(copies, axes, 0, 0)
-    return parts.reshape((size * block.shape[0],) + block.shape[1:])
-
-
 def passed_along(block, axes, distance):
     devices = range(lax.axis_size(axes))
     route = [(i, i + distance) for i in devices if i + distance in devices]
@@ -67,19 +60,9 @@
     return jnp.concatenate([jnp.where(late, after[i - 2], after[i]) for i in range(4)], axis=0)
 
 
-def own_rows_first(block):
-    count = block.shape[0] // 4
-    q = [block[i * count : (i + 1) * count] for i in range(4)]
-    place = lax.axis_index(COL)
-    odd = place % 2 == 1
-    q = [jnp.where(odd, q[(i + 1) % 4], q[i]) for i in range(4)]
-    late = place >= 2
-    return jnp.concatenate([jnp.where(late, q[i - 2], q[i]) for i in range(4)], axis=0)
-
-
 def column_sum(blocks):
     total = blocks[0].astype(F32)
-    for distance in (1, 3, 2):
+    for distance in (2, 1, 3):
         block = turned(blocks[distance], distance)
         total = total + block.astype(F32)
     return total
@@ -101,7 +84,7 @@
 PARTS = 4
 
 
-def label_kernel(unit_ref, h0, h1, h2, h3, b0, b1, b2, b3, out_ref, head, back, total, sums, sems):
+def label_kernel(seen_ref, unit_ref, h0, h1, h2, h3, b0, b1, b2, b3, out_ref, head, back, total, sums, sems):
     step = pl.program_id(0)
     labels = head.shape[1] // PARTS
     count = out_ref.shape[0]
@@ -171,7 +154,11 @@
         out_ref[s, 8 * block :, :] = split.astype(BF)
 
 
-def label_sums(unit, head_parts, back_parts):
+def in_hbm(block):
+    return pltpu.with_memory_space_constraint(block, pltpu.HBM)
+
+
+def label_sums(seen, unit, head_parts, back_parts):
     frames, width = unit.shape
     labels = head_parts[0].shape[1]
     slots = 16
@@ -181,8 +168,8 @@
     return pl.pallas_call(
         label_kernel,
         grid=(STEPS,),
-        in_specs=[pl.BlockSpec((count * block, width), lambda i: (i, 0))]
-        + [pl.BlockSpec(memory_space=pltpu.HBM)] * 8,
+        in_specs=[pl.BlockSpec(memory_space=pltpu.SMEM), pl.BlockSpec((count * block, width), lambda i: (i, 0))]
+        + [pl.BlockSpec(memory_space=pl.ANY)] * 8,
         out_specs=pl.BlockSpec((count, rows, 128), lambda i: (i, 0, 0)),
         out_shape=jax.ShapeDtypeStruct((slots, rows, 128), BF),
         scratch_shapes=[
@@ -196,11 +183,11 @@
         cost_estimate=pl.CostEstimate(
             flops=4 * frames * width * labels, bytes_accessed=16 * 2**20, transcendentals=2 * frames * labels
         ),
-    )(unit, *[pltpu.with_memory_space_constraint(p, pltpu.HBM) for p in (*head_parts, *back_parts)])
-
-
-def attention_kernel(first_ref, far_ref, near_ref, own_ref, qkv_ref, merge_ref, out_ref, normed, query, key, value, context,
-                     weight, merge, sems):
+    )(seen, unit, in_hbm(head_parts[0]), *head_parts[1:], in_hbm(back_parts[0]), *back_parts[1:])
+
+
+def attention_kernel(place_ref, far_ref, near_ref, own_ref, qkv_ref, merge_ref, out_ref, mine_ref, normed, query, key, value,
+                     context, weight, merge, hidden, unit, moved, sems):
     block, width = own_ref.shape
     wide = weight.shape[2]
     many = weight.shape[0]
@@ -229,7 +216,7 @@
     padded = key.shape[0]
     r = lax.broadcasted_iota(jnp.int32, (block, padded), 0)
     j = lax.broadcasted_iota(jnp.int32, (block, padded), 1)
-    allowed = (j <= r + past) & (j > r + past - WIN) & (j < keys) & (first_ref[0] - past + j >= 0)
+    allowed = (j <= r + past) & (j > r + past - WIN) & (j < keys) & (place_ref[0] - past + j >= 0)
     lane = lax.broadcasted_iota(jnp.int32, (block, 128), 1)
     for pair in range(width // 128):
         span = slice(pair * 128, (pair + 1) * 128)
@@ -246,10 +233,23 @@
         context[:, span] = jnp.where(lane >= HEAD_DIM, parts[1], parts[0]).astype(BF)
     copies[many].wait()
     merged = jnp.dot(context[...], merge[...], preferred_element_type=F32)
-    out_ref[...] = (own_ref[...].astype(F32) + merged).astype(BF)
-
-
-def attended(first, far, near, own, qkv_weight, merge_weight):
+    hidden[...] = (own_ref[...].astype(F32) + merged).astype(BF).astype(F32)
+    unit[...] = root_norm(hidden[...]).astype(BF).astype(F32)
+    rows = mine_ref.shape[0]
+    mine_ref[...] = hidden[pl.ds(pl.multiple_of(place_ref[1] * rows, 8), rows), :].astype(BF)
+    quarter = width // 4
+    for k in range(4):
+        row = pl.multiple_of(lax.rem(place_ref[1] + k, 4) * rows, 8)
+        for q in range(4):
+            column = pl.multiple_of(lax.bitwise_xor(place_ref[2], q) * quarter, quarter)
+            piece = unit[pl.ds(row, rows), pl.ds(column, quarter)]
+            moved[k * rows : (k + 1) * rows, q * quarter : (q + 1) * quarter] = piece
+    spread = moved[...].astype(BF)
+    for s in range(out_ref.shape[0]):
+        out_ref[s] = spread
+
+
+def attended(place, far, near, own, qkv_weight, merge_weight, copies):
     block, width = own.shape
     keys = far.shape[0] + near.shape[0] + block
     padded = -(-keys // 128) * 128
@@ -257,8 +257,11 @@
     return pl.pallas_call(
         attention_kernel,
         in_specs=[pl.BlockSpec(memory_space=pltpu.SMEM)] + [vmem] * 3 + [pl.BlockSpec(memory_space=pl.ANY)] * 2,
-        out_specs=vmem,
-        out_shape=jax.ShapeDtypeStruct((block, width), BF),
+        out_specs=[vmem, vmem],
+        out_shape=[
+            jax.ShapeDtypeStruct((copies, block, width), BF),
+            jax.ShapeDtypeStruct((block // 4, width), BF),
+        ],
         scratch_shapes=[
             pltpu.VMEM((keys, width), BF),
             pltpu.VMEM((block, width), BF),
@@ -267,6 +270,9 @@
             pltpu.VMEM((block, width), BF),
             pltpu.VMEM((3 * width // 512, width, 512), BF),
             pltpu.VMEM((width, width), BF),
+            pltpu.VMEM((block, width), F32),
+            pltpu.VMEM((block, width), F32),
+            pltpu.VMEM((block, width), F32),
             pltpu.SemaphoreType.DMA((3 * width // 512 + 1,)),
         ],
         compiler_params=pltpu.CompilerParams(vmem_limit_bytes=24 * 2**20),
@@ -274,7 +280,7 @@
             flops=8 * keys * width * width, bytes_accessed=9 * 2**20, transcendentals=2 * HEADS * block * keys
         ),
         name="qkv",
-    )(first, far, near, own, *[pltpu.with_memory_space_constraint(w, pltpu.HBM) for w in (qkv_weight, merge_weight)])
+    )(place, far, near, own, *[pltpu.with_memory_space_constraint(w, pltpu.HBM) for w in (qkv_weight, merge_weight)])
 
 
 def body(frames, qkv_weight, attn_out_weight, head_weight, back_weight):
@@ -289,13 +295,13 @@
     own = column_rows(frames)
     prev = passed_along(own, BLOCKS, 1)
     prev2 = passed_along(own[block - far :], BLOCKS, 2)
-    first = lax.axis_index(BLOCKS).astype(jnp.int32)[None] * block
-    hidden = attended(first, prev2, prev, own, qkv_weight, attn_out_weight)
-    hidden = own_rows_first(hidden)
-    unit = root_norm(hidden.astype(F32)).astype(BF)
-
-    every = gathered(from_own(unit), PLANE)
-    sent = label_sums(every, head_parts, back_parts)
+    place = jnp.stack([lax.axis_index(BLOCKS) * block, lax.axis_index(COL), lax.axis_index(TIME)])
+    copies, hidden = attended(
+        place.astype(jnp.int32), prev2, prev, own, qkv_weight, attn_out_weight, lax.axis_size(PLANE)
+    )
+    every = lax.all_to_all(copies, PLANE, 0, 0).reshape(-1, width)
+    seen = jnp.max(every[:8, :128].astype(F32), keepdims=True)
+    sent = label_sums(seen, every, head_parts, back_parts)
     summed = jnp.sum(lax.all_to_all(sent, PLANE, 0, 0).astype(F32), axis=0)
     block_totals = jnp.sum(summed[8 * block : 8 * block + 3, :block], axis=0)
     split = three_rows(block_totals.reshape(cols, rows), 128)
@@ -308,7 +314,7 @@
 
     center = back_proj - jnp.mean(back_proj, axis=-1, keepdims=True)
     spread = jnp.mean(center * center, axis=-1, keepdims=True)
-    conditioned = (hidden[:rows].astype(F32) + center * lax.rsqrt(spread + 1e-05)).astype(BF)
+    conditioned = (hidden.astype(F32) + center * lax.rsqrt(spread + 1e-05)).astype(BF)
     return (conditioned, jnp.log(owned_totals))
 
 

time: 175 us -> 176 us (level)
  waiting for transfers between devices: 59.8 us -> 63.1 us
  local copies, waits for them, and re-layouts: 5.32 us -> 2.33 us
    broadcast_in_dim x1 -> x0, local copies, waits for them, and re-layouts: 2.03 us -> none  [gathered(): jnp.broadcast_to(block[None], (size,) + block.shape)]
where the time goes in v8:
time: 176 us
  waiting for transfers between devices  63.1 us (36%)
  blocking collectives  47 us (27%)
  starting transfers between devices  30 us (17%)
  Pallas kernels  28.7 us (16%)
  other arithmetic  3.21 us (2%)
  local copies, waits for them, and re-layouts  2.33 us (1%)
    all_to_all x1, blocking collectives, body(): summed = jnp.sum(lax.all_to_all(sent, PLANE, 0, 0).astype(F32), axis=0)  47 us
    ppermute x6, waiting for transfers between devices, swapped(): return lax.ppermute(block, axis, [(0, 1), (1, 0)])  46.1 us
    pallas_call x1, Pallas kernels, label_sums(): pl.pallas_call(label_kernel, grid=(STEPS,), in_specs=[pl.BlockSpec(memory...  19.8 us
    ppermute x6, starting transfers between devices, turned(): lax.ppermute(block, COL, [(i, (i + distance) % size) for i in range(size)])  15.3 us
    ppermute x6, waiting for transfers between devices, turned(): lax.ppermute(block, COL, [(i, (i + distance) % size) for i in range(size)])  11.1 us
    pallas_call x1, Pallas kernels, attended(): pl.pallas_call(attention_kernel, in_specs=[pl.BlockSpec(memory_space=pltp...  8.88 us
    ppermute x2, starting transfers between devices, passed_along(): return lax.ppermute(block, axes, route)  8.29 us
    ppermute x2, waiting for transfers between devices, passed_along(): return lax.ppermute(block, axes, route)  5.87 us
  transfers between devices with their start and end apart: 15, of which 8 were waited for; matrix products, arithmetic and copies ran while one was open for 0% of the time, Pallas kernels for 0%

profile of v8, /device:TPU:32, one launch (start us, length us, event | category | flops | bytes accessed | tf_op | source)
XLA Modules:
  0.0 175.7 jit_solution(6996174975036682806)
XLA Ops:
  0.6 5.5 %collective-permute-start.1 = (bf16[24,1024]{1,0:T(8,128)(2,1)}, bf16[24,1024]{1,0:T(8,128)(2,1)S(1)}, u32[]{:S(2)}, u32[]{:S(2)}) collective-permute-start(bf16[24,1024]{1,0:T(8,128)(2,1)} %param.5), channel_id=1, source_target_pairs={{0,3},{1,0},{2,1},{3,2},{4,7},{5,4},{6,5},{7,6},{8,11},{9,8},{10,9... | collective-permute-start | bytes 147464 | tf_op jit(solution)/shard_map/ppermute | solution.py:51
  6.1 3.8 %collective-permute-start.2 = (bf16[24,1024]{1,0:T(8,128)(2,1)}, bf16[24,1024]{1,0:T(8,128)(2,1)S(1)}, u32[]{:S(2)}, u32[]{:S(2)}) collective-permute-start(bf16[24,1024]{1,0:T(8,128)(2,1)} %param.5), channel_id=1, source_target_pairs={{0,2},{1,3},{2,0},{3,1},{4,6},{5,7},{6,4},{7,5},{8,10},{9,11},{10,... | collective-permute-start | bytes 147464 | tf_op jit(solution)/shard_map/ppermute | solution.py:51
  9.9 5.2 %collective-permute-done = bf16[24,1024]{1,0:T(8,128)(2,1)S(1)} collective-permute-done((bf16[24,1024]{1,0:T(8,128)(2,1)}, bf16[24,1024]{1,0:T(8,128)(2,1)S(1)}, u32[]{:S(2)}, u32[]{:S(2)}) %collective-permute-start) | collective-permute-done | bytes 49184 | tf_op jit(solution)/shard_map/ppermute | solution.py:51
  15.2 0.8 broadcast_select_fusion.5
  16.0 3.5 %collective-permute-start.4 = (bf16[96,1024]{1,0:T(8,128)(2,1)S(1)}, bf16[96,1024]{1,0:T(8,128)(2,1)S(1)}, u32[]{:S(2)}, u32[]{:S(2)}) collective-permute-start(bf16[96,1024]{1,0:T(8,128)(2,1)S(1)} %pad_maximum_fusion.own_ref), channel_id=1, source_target_pairs={{0,4},{4,8},{8,12},{12,16},{16,20},{20,24},{24,28},{28,32},{32,36}... | collective-permute-start | bytes 589832 | tf_op jit(solution)/shard_map/ppermute | solution.py:26
  19.5 4.8 %collective-permute-start.3 = (bf16[32,1024]{1,0:T(8,128)(2,1)S(1)}, bf16[32,1024]{1,0:T(8,128)(2,1)S(1)}, u32[]{:S(2)}, u32[]{:S(2)}) collective-permute-start(bf16[32,1024]{1,0:T(8,128)(2,1)S(1)} %pad_maximum_fusion.1), channel_id=1, source_target_pairs={{0,8},{4,12},{8,16},{12,20},{16,24},{20,28},{24,32},{28,36},{32,40... | collective-permute-start | bytes 196616 | tf_op jit(solution)/shard_map/ppermute | solution.py:26
  24.4 5.9 %collective-permute-done.3.far_ref = bf16[32,1024]{1,0:T(8,128)(2,1)S(1)} collective-permute-done((bf16[32,1024]{1,0:T(8,128)(2,1)S(1)}, bf16[32,1024]{1,0:T(8,128)(2,1)S(1)}, u32[]{:S(2)}, u32[]{:S(2)}) %collective-permute-start.3) | collective-permute-done | bytes 65568 | tf_op jit(solution)/shard_map/ppermute | solution.py:26
  30.3 8.9 %qkv.1 = (bf16[16,96,1024]{2,1,0:T(8,128)(2,1)S(1)}, bf16[24,1024]{1,0:T(8,128)(2,1)S(1)}) custom-call(s32[3]{0:T(128)S(1)} %pad_add_fusion.place_ref, bf16[32,1024]{1,0:T(8,128)(2,1)S(1)} %collective-permute-done.3.far_ref, bf16[96,1024]{1,0:T(8,128)(2,1)S(1)} %collective-permute-done.4.near_ref, bf16[96,1024]{1,0:T(8,128)(2,1)S(1)} %pad_maximum_fusion.own_ref, ...), custom_call_target="tpu_custom_call" | custom-call | flops 1879048192 | bytes 9437184 | tf_op jit(solution)/shard_map/qkv/pallas_call | solution.py:257
  39.2 1.6 copy-done
  40.8 3.7 %all-to-all-start = ((bf16[16,96,1024]{2,1,0:T(8,128)(2,1)}), bf16[16,96,1024]{2,1,0:T(8,128)(2,1)S(1)}, u32[]{:S(2)}, u32[]{:S(2)}) async-start(bf16[16,96,1024]{2,1,0:T(8,128)(2,1)} %copy-done), calls=%async_computation | async-start | bytes 6291456 | tf_op jit(solution)/shard_map/all_to_all | solution.py:302
  44.8 1.9 %collective-permute-start.9 = (bf16[2048,256]{1,0:T(8,128)(2,1)}, bf16[2048,256]{1,0:T(8,128)(2,1)}, u32[]{:S(2)}, u32[]{:S(2)}) collective-permute-start(bf16[2048,256]{1,0:T(8,128)(2,1)} %b0.1), channel_id=1, source_target_pairs={{0,128},{128,0},{1,129},{129,1},{2,130},{130,2},{3,131},{131,3},{4... | collective-permute-start | bytes 3145736 | tf_op jit(solution)/shard_map/ppermute | solution.py:30
  47.2 23.8 %collective-permute-done.6.h2 = bf16[256,2048]{1,0:T(8,128)(2,1)} collective-permute-done((bf16[256,2048]{1,0:T(8,128)(2,1)}, bf16[256,2048]{1,0:T(8,128)(2,1)}, u32[]{:S(2)}, u32[]{:S(2)}) %collective-permute-start.6) | collective-permute-done | bytes 1048608 | tf_op jit(solution)/shard_map/ppermute | solution.py:30
  71.0 20.6 %collective-permute-done.9.b2 = bf16[2048,256]{1,0:T(8,128)(2,1)} collective-permute-done((bf16[2048,256]{1,0:T(8,128)(2,1)}, bf16[2048,256]{1,0:T(8,128)(2,1)}, u32[]{:S(2)}, u32[]{:S(2)}) %collective-permute-start.9) | collective-permute-done | bytes 1048608 | tf_op jit(solution)/shard_map/ppermute | solution.py:30
  91.6 0.6 slice_reduce_fusion.2
  92.9 1.7 collective-permute-done.10.b3
  94.6 19.8 %shard_map.68 = bf16[16,776,128]{2,1,0:T(8,128)(2,1)S(1)} custom-call(f32[1,1]{1,0:T(1,128)S(6)} %convert.20.seen_ref, bf16[1536,1024]{1,0:T(8,128)(2,1)S(1)} %bitcast.29, bf16[256,2048]{1,0:T(8,128)(2,1)} %h0.1, bf16[256,2048]{1,0:T(8,128)(2,1)} %collective-permute-done.5.h1, bf16[256,2048]{1,0:T(8,128)(2,1)} %collective-permute-done.6.h2, ...), custom_call_target="tpu_custom_call" | custom-call | flops 12884901888 | bytes 16777216 | tf_op jit(solution)/shard_map/pallas_call | solution.py:168
  114.5 47.0 %all_to_all.10 = bf16[16,776,128]{2,1,0:T(8,128)(2,1)S(1)} all-to-all(bf16[16,776,128]{2,1,0:T(8,128)(2,1)S(1)} %shard_map.68), channel_id=1, replica_groups=mesh['zl'=2,'c'=2,'x'=4,'y'=4,'zh'=4] {'x','y'}, dimensions={0} | all-to-all | bytes 6356992 | tf_op jit(solution)/shard_map/all_to_all | solution.py:305
  162.1 3.1 %collective-permute-start.11 = (bf16[200,128]{1,0:T(8,128)(2,1)S(1)}, bf16[200,128]{1,0:T(8,128)(2,1)S(1)}, u32[]{:S(2)}, u32[]{:S(2)}) collective-permute-start(bf16[200,128]{1,0:T(8,128)(2,1)S(1)} %get-tuple-element.8), channel_id=1, source_target_pairs={{0,2},{1,3},{2,0},{3,1},{4,6},{5,7},{6,4},{7,5},{8,10},{9,11},{10,... | collective-permute-start | bytes 153608 | tf_op jit(solution)/shard_map/ppermute | solution.py:51
  165.2 2.3 %collective-permute-start.13 = (bf16[200,128]{1,0:T(8,128)(2,1)S(1)}, bf16[200,128]{1,0:T(8,128)(2,1)S(1)}, u32[]{:S(2)}, u32[]{:S(2)}) collective-permute-start(bf16[200,128]{1,0:T(8,128)(2,1)S(1)} %get-tuple-element.9), channel_id=1, source_target_pairs={{0,3},{1,0},{2,1},{3,2},{4,7},{5,4},{6,5},{7,6},{8,11},{9,8},{10,9... | collective-permute-start | bytes 153608 | tf_op jit(solution)/shard_map/ppermute | solution.py:51
  167.5 0.6 collective-permute-start.12
  168.1 2.3 %collective-permute-done.11 = bf16[200,128]{1,0:T(8,128)(2,1)S(1)} collective-permute-done((bf16[200,128]{1,0:T(8,128)(2,1)S(1)}, bf16[200,128]{1,0:T(8,128)(2,1)S(1)}, u32[]{:S(2)}, u32[]{:S(2)}) %collective-permute-start.11) | collective-permute-done | bytes 51232 | tf_op jit(solution)/shard_map/ppermute | solution.py:51
  170.4 1.4 collective-permute-done.13
  171.9 2.1 %collective-permute-done.12 = bf16[200,128]{1,0:T(8,128)(2,1)S(1)} collective-permute-done((bf16[200,128]{1,0:T(8,128)(2,1)S(1)}, bf16[200,128]{1,0:T(8,128)(2,1)S(1)}, u32[]{:S(2)}, u32[]{:S(2)}) %collective-permute-start.12) | collective-permute-done | bytes 51232 | tf_op jit(solution)/shard_map/ppermute | solution.py:51
  175.0 0.7 add_convert_fusion
  (37 shorter events, 2.5 us)
Async XLA Ops:
  0.6 9.3 %collective-permute-start.1 = (bf16[24,1024]{1,0:T(8,128)(2,1)}, bf16[24,1024]{1,0:T(8,128)(2,1)S(1)}, u32[]{:S(2)}, u32[]{:S(2)}) collective-permute-start(bf16[24,1024]{1,0:T(8,128)(2,1)} %param.5), channel_id=1, source_target_pairs={{0,3},{1,0},{2,1},{3,2},{4,7},{5,4},{6,5},{7,6},{8,11},{9,8},{10,9... | collective-permute-start | bytes 147464 | tf_op jit(solution)/shard_map/ppermute | solution.py:51
  6.1 9.0 %collective-permute-start = (bf16[24,1024]{1,0:T(8,128)(2,1)}, bf16[24,1024]{1,0:T(8,128)(2,1)S(1)}, u32[]{:S(2)}, u32[]{:S(2)}) collective-permute-start(bf16[24,1024]{1,0:T(8,128)(2,1)} %param.5), channel_id=1, source_target_pairs={{0,1},{1,2},{2,3},{3,0},{4,5},{5,6},{6,7},{7,4},{8,9},{9,10},{10,1... | collective-permute-start | bytes 147464 | tf_op jit(solution)/shard_map/ppermute | solution.py:51
  6.1 9.0 %collective-permute-start.2 = (bf16[24,1024]{1,0:T(8,128)(2,1)}, bf16[24,1024]{1,0:T(8,128)(2,1)S(1)}, u32[]{:S(2)}, u32[]{:S(2)}) collective-permute-start(bf16[24,1024]{1,0:T(8,128)(2,1)} %param.5), channel_id=1, source_target_pairs={{0,2},{1,3},{2,0},{3,1},{4,6},{5,7},{6,4},{7,5},{8,10},{9,11},{10,... | collective-permute-start | bytes 147464 | tf_op jit(solution)/shard_map/ppermute | solution.py:51
  16.0 14.3 %collective-permute-start.4 = (bf16[96,1024]{1,0:T(8,128)(2,1)S(1)}, bf16[96,1024]{1,0:T(8,128)(2,1)S(1)}, u32[]{:S(2)}, u32[]{:S(2)}) collective-permute-start(bf16[96,1024]{1,0:T(8,128)(2,1)S(1)} %pad_maximum_fusion.own_ref), channel_id=1, source_target_pairs={{0,4},{4,8},{8,12},{12,16},{16,20},{20,24},{24,28},{28,32},{32,36}... | collective-permute-start | bytes 589832 | tf_op jit(solution)/shard_map/ppermute | solution.py:26
  19.5 10.8 %collective-permute-start.3 = (bf16[32,1024]{1,0:T(8,128)(2,1)S(1)}, bf16[32,1024]{1,0:T(8,128)(2,1)S(1)}, u32[]{:S(2)}, u32[]{:S(2)}) collective-permute-start(bf16[32,1024]{1,0:T(8,128)(2,1)S(1)} %pad_maximum_fusion.1), channel_id=1, source_target_pairs={{0,8},{4,12},{8,16},{12,20},{16,24},{20,28},{24,32},{28,36},{32,40... | collective-permute-start | bytes 196616 | tf_op jit(solution)/shard_map/ppermute | solution.py:26
  39.2 1.7 copy-start
  40.8 50.8 %all-to-all-start = ((bf16[16,96,1024]{2,1,0:T(8,128)(2,1)}), bf16[16,96,1024]{2,1,0:T(8,128)(2,1)S(1)}, u32[]{:S(2)}, u32[]{:S(2)}) async-start(bf16[16,96,1024]{2,1,0:T(8,128)(2,1)} %copy-done), calls=%async_computation | async-start | bytes 6291456 | tf_op jit(solution)/shard_map/all_to_all | solution.py:302
  44.6 26.4 %collective-permute-start.6 = (bf16[256,2048]{1,0:T(8,128)(2,1)}, bf16[256,2048]{1,0:T(8,128)(2,1)}, u32[]{:S(2)}, u32[]{:S(2)}) collective-permute-start(bf16[256,2048]{1,0:T(8,128)(2,1)} %h0.1), channel_id=1, source_target_pairs={{0,128},{128,0},{1,129},{129,1},{2,130},{130,2},{3,131},{131,3},{4... | collective-permute-start | bytes 3145736 | tf_op jit(solution)/shard_map/ppermute | solution.py:30
  44.8 46.8 %collective-permute-start.9 = (bf16[2048,256]{1,0:T(8,128)(2,1)}, bf16[2048,256]{1,0:T(8,128)(2,1)}, u32[]{:S(2)}, u32[]{:S(2)}) collective-permute-start(bf16[2048,256]{1,0:T(8,128)(2,1)} %b0.1), channel_id=1, source_target_pairs={{0,128},{128,0},{1,129},{129,1},{2,130},{130,2},{3,131},{131,3},{4... | collective-permute-start | bytes 3145736 | tf_op jit(solution)/shard_map/ppermute | solution.py:30
  46.7 46.2 %collective-permute-start.5 = (bf16[256,2048]{1,0:T(8,128)(2,1)}, bf16[256,2048]{1,0:T(8,128)(2,1)}, u32[]{:S(2)}, u32[]{:S(2)}) collective-permute-start(bf16[256,2048]{1,0:T(8,128)(2,1)} %h0.1), channel_id=1, source_target_pairs={{0,64},{64,0},{1,65},{65,1},{2,66},{66,2},{3,67},{67,3},{4,68},{68... | collective-permute-start | bytes 3145736 | tf_op jit(solution)/shard_map/ppermute | solution.py:30
  46.7 46.2 %collective-permute-start.8 = (bf16[2048,256]{1,0:T(8,128)(2,1)}, bf16[2048,256]{1,0:T(8,128)(2,1)}, u32[]{:S(2)}, u32[]{:S(2)}) collective-permute-start(bf16[2048,256]{1,0:T(8,128)(2,1)} %b0.1), channel_id=1, source_target_pairs={{0,64},{64,0},{1,65},{65,1},{2,66},{66,2},{3,67},{67,3},{4,68},{68... | collective-permute-start | bytes 3145736 | tf_op jit(solution)/shard_map/ppermute | solution.py:30
  71.0 21.9 %collective-permute-start.7 = (bf16[256,2048]{1,0:T(8,128)(2,1)}, bf16[256,2048]{1,0:T(8,128)(2,1)}, u32[]{:S(2)}, u32[]{:S(2)}) collective-permute-start(bf16[256,2048]{1,0:T(8,128)(2,1)} %collective-permute-done.6.h2), channel_id=1, source_target_pairs={{0,64},{64,0},{1,65},{65,1},{2,66},{66,2},{3,67},{67,3},{4,68},{68... | collective-permute-start | bytes 3145736 | tf_op jit(solution)/shard_map/ppermute | solution.py:30
  91.6 3.0 %collective-permute-start.10 = (bf16[2048,256]{1,0:T(8,128)(2,1)}, bf16[2048,256]{1,0:T(8,128)(2,1)}, u32[]{:S(2)}, u32[]{:S(2)}) collective-permute-start(bf16[2048,256]{1,0:T(8,128)(2,1)} %collective-permute-done.9.b2), channel_id=1, source_target_pairs={{0,64},{64,0},{1,65},{65,1},{2,66},{66,2},{3,67},{67,3},{4,68},{68... | collective-permute-start | bytes 3145736 | tf_op jit(solution)/shard_map/ppermute | solution.py:30
  162.1 8.3 %collective-permute-start.11 = (bf16[200,128]{1,0:T(8,128)(2,1)S(1)}, bf16[200,128]{1,0:T(8,128)(2,1)S(1)}, u32[]{:S(2)}, u32[]{:S(2)}) collective-permute-start(bf16[200,128]{1,0:T(8,128)(2,1)S(1)} %get-tuple-element.8), channel_id=1, source_target_pairs={{0,2},{1,3},{2,0},{3,1},{4,6},{5,7},{6,4},{7,5},{8,10},{9,11},{10,... | collective-permute-start | bytes 153608 | tf_op jit(solution)/shard_map/ppermute | solution.py:51
  165.2 6.7 %collective-permute-start.13 = (bf16[200,128]{1,0:T(8,128)(2,1)S(1)}, bf16[200,128]{1,0:T(8,128)(2,1)S(1)}, u32[]{:S(2)}, u32[]{:S(2)}) collective-permute-start(bf16[200,128]{1,0:T(8,128)(2,1)S(1)} %get-tuple-element.9), channel_id=1, source_target_pairs={{0,3},{1,0},{2,1},{3,2},{4,7},{5,4},{6,5},{7,6},{8,11},{9,8},{10,9... | collective-permute-start | bytes 153608 | tf_op jit(solution)/shard_map/ppermute | solution.py:51
  167.5 6.5 %collective-permute-start.12 = (bf16[200,128]{1,0:T(8,128)(2,1)S(1)}, bf16[200,128]{1,0:T(8,128)(2,1)S(1)}, u32[]{:S(2)}, u32[]{:S(2)}) collective-permute-start(bf16[200,128]{1,0:T(8,128)(2,1)S(1)} %get-tuple-element.10), channel_id=1, source_target_pairs={{0,1},{1,2},{2,3},{3,0},{4,5},{5,6},{6,7},{7,4},{8,9},{9,10},{10,1... | collective-permute-start | bytes 153608 | tf_op jit(solution)/shard_map/ppermute | solution.py:51

commit v9 on v7

--- a/solution.py
+++ b/solution.py
@@ -77,12 +77,45 @@
     return jnp.concatenate([jnp.where(late, q[i - 2], q[i]) for i in range(4)], axis=0)
 
 
-def column_sum(blocks):
-    total = blocks[0].astype(F32)
-    for distance in (1, 3, 2):
-        block = turned(blocks[distance], distance)
-        total = total + block.astype(F32)
-    return total
+def column_parts(blocks):
+    return [blocks[0]] + [turned(blocks[distance], distance) for distance in (2, 1, 3)]
+
+
+def finish_kernel(place_ref, p0, p1, p2, p3, hidden_ref, out_ref, log_ref, summed):
+    rows, width = hidden_ref.shape
+    summed[...] = p0[...].astype(F32) + p1[...].astype(F32) + p2[...].astype(F32) + p3[...].astype(F32)
+    groups = width // 128
+    last = groups * rows
+    total = jnp.sum(summed[last : last + 3, :], axis=0, keepdims=True)
+    log_ref[...] = jnp.broadcast_to(jnp.log(total), log_ref.shape)
+    column = jnp.broadcast_to(total, (128, 128)).T[:rows, :]
+    pieces = []
+    for j in range(groups):
+        group = lax.bitwise_xor(place_ref[0], j // 2) * 2 + j % 2
+        piece = summed[pl.ds(pl.multiple_of(group * rows, 8), rows), :]
+        pieces.append(piece / column)
+    mean = jnp.sum(sum(pieces), axis=-1, keepdims=True) * (1.0 / width)
+    pieces = [piece - mean for piece in pieces]
+    spread = jnp.sum(sum(piece * piece for piece in pieces), axis=-1, keepdims=True) * (1.0 / width)
+    scale = lax.rsqrt(spread + 1e-05)
+    for j in range(groups):
+        span = slice(j * 128, (j + 1) * 128)
+        out_ref[:, span] = (hidden_ref[:, span].astype(F32) + pieces[j] * scale).astype(BF)
+
+
+def finished(place, parts, hidden):
+    vmem = pl.BlockSpec(memory_space=pltpu.VMEM)
+    return pl.pallas_call(
+        finish_kernel,
+        in_specs=[pl.BlockSpec(memory_space=pltpu.SMEM)] + [vmem] * 5,
+        out_specs=[vmem, vmem],
+        out_shape=[
+            jax.ShapeDtypeStruct(hidden.shape, BF),
+            jax.ShapeDtypeStruct((8, 128), F32),
+        ],
+        scratch_shapes=[pltpu.VMEM(parts[0].shape, F32)],
+        compiler_params=pltpu.CompilerParams(vmem_limit_bytes=4 * 2**20),
+    )(place, *parts, hidden)
 
 
 def three_rows(totals, width):
@@ -279,7 +312,6 @@
 
 def body(frames, qkv_weight, attn_out_weight, head_weight, back_weight):
     rows = frames.shape[0]
-    width = frames.shape[1]
     cols = lax.axis_size(COL)
     block = rows * cols
     far = WIN - block
@@ -301,15 +333,9 @@
     split = three_rows(block_totals.reshape(cols, rows), 128)
     parts = summed[: 8 * block].astype(BF).reshape(8, cols, rows, 128).transpose(1, 0, 2, 3)
     sent = jnp.concatenate([parts.reshape(cols, 8 * rows, 128), split], axis=1)
-    summed = column_sum(sent)
-    owned_totals = jnp.sum(summed[8 * rows : 8 * rows + 3, :rows], axis=0)
-    back_proj = summed[: 8 * rows].reshape(8, rows, 128).transpose(1, 0, 2).reshape(rows, width)
-    back_proj = from_own(back_proj) / owned_totals[:, None]
-
-    center = back_proj - jnp.mean(back_proj, axis=-1, keepdims=True)
-    spread = jnp.mean(center * center, axis=-1, keepdims=True)
-    conditioned = (hidden[:rows].astype(F32) + center * lax.rsqrt(spread + 1e-05)).astype(BF)
-    return (conditioned, jnp.log(owned_totals))
+    place = lax.axis_index(TIME).astype(jnp.int32)[None]
+    conditioned, logs = finished(place, column_parts(sent), hidden[:rows])
+    return (conditioned, logs[0, :rows])
 
 
 def solution(mesh):

time: 175 us -> 176 us (level)
  waiting for transfers between devices: 59.8 us -> 61.9 us
    ppermute x6, waiting for transfers between devices: 9.42 us -> 11.5 us  [turned(): lax.ppermute(block, COL, [(i, (i + distance) % size) for i in range(size)])]
  transfers between devices with their start and end apart: 15 -> 15, of which waited for: 8 -> 7; matrix products, arithmetic and copies ran while one was open for 0% -> 0% of each run, Pallas kernels for 0% -> 0%
where the time goes in v9:
time: 176 us; the launch traced here: 175 us
  waiting for transfers between devices  61.9 us (35%)
  blocking collectives  47 us (27%)
  starting transfers between devices  30 us (17%)
  Pallas kernels  28.6 us (16%)
  local copies, waits for them, and re-layouts  5.3 us (3%)
    all_to_all x1, blocking collectives, body(): summed = jnp.sum(lax.all_to_all(sent, PLANE, 0, 0).astype(F32), axis=0)  47 us
    ppermute x6, waiting for transfers between devices, swapped(): return lax.ppermute(block, axis, [(0, 1), (1, 0)])  44.4 us
    pallas_call x1, Pallas kernels, label_sums(): pl.pallas_call(label_kernel, grid=(STEPS,), in_specs=[pl.BlockSpec((count...  19.8 us
    ppermute x6, starting transfers between devices, turned(): lax.ppermute(block, COL, [(i, (i + distance) % size) for i in range(size)])  15.4 us
    ppermute x6, waiting for transfers between devices, turned(): lax.ppermute(block, COL, [(i, (i + distance) % size) for i in range(size)])  11.5 us
    ppermute x2, starting transfers between devices, passed_along(): return lax.ppermute(block, axes, route)  8.29 us
    pallas_call x1, Pallas kernels, attended(): pl.pallas_call(attention_kernel, in_specs=[pl.BlockSpec(memory_space=pltp...  7.85 us
    ppermute x2, waiting for transfers between devices, passed_along(): return lax.ppermute(block, axes, route)  5.94 us
  transfers between devices with their start and end apart: 15, of which 7 were waited for; matrix products, arithmetic and copies ran while one was open for 0% of the time, Pallas kernels for 0%

profile of v9, /device:TPU:32, one launch (start us, length us, event | category | flops | bytes accessed | tf_op | source)
XLA Modules:
  0.0 175.3 jit_solution(4868372839846565109)
XLA Ops:
  0.6 5.5 %collective-permute-start.1 = (bf16[24,1024]{1,0:T(8,128)(2,1)}, bf16[24,1024]{1,0:T(8,128)(2,1)S(1)}, u32[]{:S(2)}, u32[]{:S(2)}) collective-permute-start(bf16[24,1024]{1,0:T(8,128)(2,1)} %param.5), channel_id=1, source_target_pairs={{0,3},{1,0},{2,1},{3,2},{4,7},{5,4},{6,5},{7,6},{8,11},{9,8},{10,9... | collective-permute-start | bytes 147464 | tf_op jit(solution)/shard_map/ppermute | solution.py:58
  6.1 3.8 %collective-permute-start.2 = (bf16[24,1024]{1,0:T(8,128)(2,1)}, bf16[24,1024]{1,0:T(8,128)(2,1)S(1)}, u32[]{:S(2)}, u32[]{:S(2)}) collective-permute-start(bf16[24,1024]{1,0:T(8,128)(2,1)} %param.5), channel_id=1, source_target_pairs={{0,2},{1,3},{2,0},{3,1},{4,6},{5,7},{6,4},{7,5},{8,10},{9,11},{10,... | collective-permute-start | bytes 147464 | tf_op jit(solution)/shard_map/ppermute | solution.py:58
  9.9 5.2 %collective-permute-done = bf16[24,1024]{1,0:T(8,128)(2,1)S(1)} collective-permute-done((bf16[24,1024]{1,0:T(8,128)(2,1)}, bf16[24,1024]{1,0:T(8,128)(2,1)S(1)}, u32[]{:S(2)}, u32[]{:S(2)}) %collective-permute-start) | collective-permute-done | bytes 49184 | tf_op jit(solution)/shard_map/ppermute | solution.py:58
  15.2 0.8 broadcast_select_fusion.13
  16.0 3.5 %collective-permute-start.4 = (bf16[96,1024]{1,0:T(8,128)(2,1)S(1)}, bf16[96,1024]{1,0:T(8,128)(2,1)S(1)}, u32[]{:S(2)}, u32[]{:S(2)}) collective-permute-start(bf16[96,1024]{1,0:T(8,128)(2,1)S(1)} %pad_maximum_fusion.own_ref), channel_id=1, source_target_pairs={{0,4},{4,8},{8,12},{12,16},{16,20},{20,24},{24,28},{28,32},{32,36}... | collective-permute-start | bytes 589832 | tf_op jit(solution)/shard_map/ppermute | solution.py:33
  19.5 4.8 %collective-permute-start.3 = (bf16[32,1024]{1,0:T(8,128)(2,1)S(1)}, bf16[32,1024]{1,0:T(8,128)(2,1)S(1)}, u32[]{:S(2)}, u32[]{:S(2)}) collective-permute-start(bf16[32,1024]{1,0:T(8,128)(2,1)S(1)} %pad_maximum_fusion.3), channel_id=1, source_target_pairs={{0,8},{4,12},{8,16},{12,20},{16,24},{20,28},{24,32},{28,36},{32,40... | collective-permute-start | bytes 196616 | tf_op jit(solution)/shard_map/ppermute | solution.py:33
  24.3 5.9 %collective-permute-done.3.far_ref = bf16[32,1024]{1,0:T(8,128)(2,1)S(1)} collective-permute-done((bf16[32,1024]{1,0:T(8,128)(2,1)S(1)}, bf16[32,1024]{1,0:T(8,128)(2,1)S(1)}, u32[]{:S(2)}, u32[]{:S(2)}) %collective-permute-start.3) | collective-permute-done | bytes 65568 | tf_op jit(solution)/shard_map/ppermute | solution.py:33
  30.3 7.8 %qkv.1 = bf16[96,1024]{1,0:T(8,128)(2,1)S(1)} custom-call(s32[1]{0:T(128)} %bitcast.1.first_ref, bf16[32,1024]{1,0:T(8,128)(2,1)S(1)} %collective-permute-done.3.far_ref, bf16[96,1024]{1,0:T(8,128)(2,1)S(1)} %collective-permute-done.4.near_ref, bf16[96,1024]{1,0:T(8,128)(2,1)S(1)} %pad_maximum_fusion.own_ref, bf16[1024,3072]{1,0:T(8,128)(2,1)} %qkv_ref.1, ...), custom_call_target="tpu_custom_call" | custom-call | flops 1879048192 | bytes 9437184 | tf_op jit(solution)/shard_map/qkv/pallas_call | solution.py:290
  38.5 2.0 %broadcast_in_dim.5 = bf16[16,96,1024]{2,1,0:T(8,128)(2,1)} broadcast(bf16[96,1024]{1,0:T(8,128)(2,1)S(1)} %pad_maximum_fusion.2), dimensions={1,2} | broadcast | bytes 3342336 | tf_op jit(solution)/shard_map/broadcast_in_dim | solution.py:25
  40.5 3.7 %all-to-all-start = ((bf16[16,96,1024]{2,1,0:T(8,128)(2,1)}), bf16[16,96,1024]{2,1,0:T(8,128)(2,1)S(1)}, u32[]{:S(2)}, u32[]{:S(2)}) async-start(bf16[16,96,1024]{2,1,0:T(8,128)(2,1)} %broadcast_in_dim.5), calls=%async_computation | async-start | bytes 6291456 | tf_op jit(solution)/shard_map/all_to_all | solution.py:26
  44.5 1.9 %collective-permute-start.9 = (bf16[2048,256]{1,0:T(8,128)(2,1)}, bf16[2048,256]{1,0:T(8,128)(2,1)S(1)}, u32[]{:S(2)}, u32[]{:S(2)}) collective-permute-start(bf16[2048,256]{1,0:T(8,128)(2,1)} %b0.1), channel_id=1, source_target_pairs={{0,128},{128,0},{1,129},{129,1},{2,130},{130,2},{3,131},{131,3},{4... | collective-permute-start | bytes 3145736 | tf_op jit(solution)/shard_map/ppermute | solution.py:37
  46.9 23.7 %collective-permute-done.6.h2 = bf16[256,2048]{1,0:T(8,128)(2,1)S(1)} collective-permute-done((bf16[256,2048]{1,0:T(8,128)(2,1)}, bf16[256,2048]{1,0:T(8,128)(2,1)S(1)}, u32[]{:S(2)}, u32[]{:S(2)}) %collective-permute-start.6) | collective-permute-done | bytes 1048608 | tf_op jit(solution)/shard_map/ppermute | solution.py:37
  70.6 20.6 %collective-permute-done.9.b2 = bf16[2048,256]{1,0:T(8,128)(2,1)S(1)} collective-permute-done((bf16[2048,256]{1,0:T(8,128)(2,1)}, bf16[2048,256]{1,0:T(8,128)(2,1)S(1)}, u32[]{:S(2)}, u32[]{:S(2)}) %collective-permute-start.9) | collective-permute-done | bytes 1048608 | tf_op jit(solution)/shard_map/ppermute | solution.py:37
  91.3 1.0 copy-done.1
  92.9 1.0 copy-done.4
  94.0 19.8 %shard_map.68 = bf16[16,776,128]{2,1,0:T(8,128)(2,1)S(1)} custom-call(bf16[1536,1024]{1,0:T(8,128)(2,1)S(1)} %bitcast.19, bf16[256,2048]{1,0:T(8,128)(2,1)} %h0.1, bf16[256,2048]{1,0:T(8,128)(2,1)} %copy-done.2, bf16[256,2048]{1,0:T(8,128)(2,1)} %copy-done, bf16[256,2048]{1,0:T(8,128)(2,1)} %copy-done.4, bf16[2048,256]{1,0:T(8,128)(2,1)} %b0.1, ...), custom_call_target="tpu_custom_call" | custom-call | flops 12884901888 | bytes 16777216 | tf_op jit(solution)/shard_map/pallas_call | solution.py:214
  113.8 47.0 %all_to_all.10 = bf16[16,776,128]{2,1,0:T(8,128)(2,1)S(1)} all-to-all(bf16[16,776,128]{2,1,0:T(8,128)(2,1)S(1)} %shard_map.68), channel_id=1, replica_groups=mesh['zl'=2,'c'=2,'x'=4,'y'=4,'zh'=4] {'x','y'}, dimensions={0} | all-to-all | bytes 6356992 | tf_op jit(solution)/shard_map/all_to_all | solution.py:331
  161.5 3.6 %collective-permute-start.13 = (bf16[200,128]{1,0:T(8,128)(2,1)S(1)}, bf16[200,128]{1,0:T(8,128)(2,1)S(1)}, u32[]{:S(2)}, u32[]{:S(2)}) collective-permute-start(bf16[200,128]{1,0:T(8,128)(2,1)S(1)} %get-tuple-element.6), channel_id=1, source_target_pairs={{0,3},{1,0},{2,1},{3,2},{4,7},{5,4},{6,5},{7,6},{8,11},{9,8},{10,9... | collective-permute-start | bytes 153608 | tf_op jit(solution)/shard_map/ppermute | solution.py:58
  165.1 1.7 collective-permute-start.11
  166.9 0.7 collective-permute-start.12
  167.6 5.6 %collective-permute-done.11.p1 = bf16[200,128]{1,0:T(8,128)(2,1)S(1)} collective-permute-done((bf16[200,128]{1,0:T(8,128)(2,1)S(1)}, bf16[200,128]{1,0:T(8,128)(2,1)S(1)}, u32[]{:S(2)}, u32[]{:S(2)}) %collective-permute-start.11) | collective-permute-done | bytes 51232 | tf_op jit(solution)/shard_map/ppermute | solution.py:58
  173.2 0.8 collective-permute-done.12.p2
  173.9 0.9 shard_map.69
  174.8 0.5 slice_bitcast_fusion
  (41 shorter events, 2.5 us)
Async XLA Ops:
  0.6 9.3 %collective-permute-start.1 = (bf16[24,1024]{1,0:T(8,128)(2,1)}, bf16[24,1024]{1,0:T(8,128)(2,1)S(1)}, u32[]{:S(2)}, u32[]{:S(2)}) collective-permute-start(bf16[24,1024]{1,0:T(8,128)(2,1)} %param.5), channel_id=1, source_target_pairs={{0,3},{1,0},{2,1},{3,2},{4,7},{5,4},{6,5},{7,6},{8,11},{9,8},{10,9... | collective-permute-start | bytes 147464 | tf_op jit(solution)/shard_map/ppermute | solution.py:58
  6.1 9.0 %collective-permute-start = (bf16[24,1024]{1,0:T(8,128)(2,1)}, bf16[24,1024]{1,0:T(8,128)(2,1)S(1)}, u32[]{:S(2)}, u32[]{:S(2)}) collective-permute-start(bf16[24,1024]{1,0:T(8,128)(2,1)} %param.5), channel_id=1, source_target_pairs={{0,1},{1,2},{2,3},{3,0},{4,5},{5,6},{6,7},{7,4},{8,9},{9,10},{10,1... | collective-permute-start | bytes 147464 | tf_op jit(solution)/shard_map/ppermute | solution.py:58
  6.1 9.0 %collective-permute-start.2 = (bf16[24,1024]{1,0:T(8,128)(2,1)}, bf16[24,1024]{1,0:T(8,128)(2,1)S(1)}, u32[]{:S(2)}, u32[]{:S(2)}) collective-permute-start(bf16[24,1024]{1,0:T(8,128)(2,1)} %param.5), channel_id=1, source_target_pairs={{0,2},{1,3},{2,0},{3,1},{4,6},{5,7},{6,4},{7,5},{8,10},{9,11},{10,... | collective-permute-start | bytes 147464 | tf_op jit(solution)/shard_map/ppermute | solution.py:58
  16.0 14.3 %collective-permute-start.4 = (bf16[96,1024]{1,0:T(8,128)(2,1)S(1)}, bf16[96,1024]{1,0:T(8,128)(2,1)S(1)}, u32[]{:S(2)}, u32[]{:S(2)}) collective-permute-start(bf16[96,1024]{1,0:T(8,128)(2,1)S(1)} %pad_maximum_fusion.own_ref), channel_id=1, source_target_pairs={{0,4},{4,8},{8,12},{12,16},{16,20},{20,24},{24,28},{28,32},{32,36}... | collective-permute-start | bytes 589832 | tf_op jit(solution)/shard_map/ppermute | solution.py:33
  19.5 10.8 %collective-permute-start.3 = (bf16[32,1024]{1,0:T(8,128)(2,1)S(1)}, bf16[32,1024]{1,0:T(8,128)(2,1)S(1)}, u32[]{:S(2)}, u32[]{:S(2)}) collective-permute-start(bf16[32,1024]{1,0:T(8,128)(2,1)S(1)} %pad_maximum_fusion.3), channel_id=1, source_target_pairs={{0,8},{4,12},{8,16},{12,20},{16,24},{20,28},{24,32},{28,36},{32,40... | collective-permute-start | bytes 196616 | tf_op jit(solution)/shard_map/ppermute | solution.py:33
  40.5 53.5 %all-to-all-start = ((bf16[16,96,1024]{2,1,0:T(8,128)(2,1)}), bf16[16,96,1024]{2,1,0:T(8,128)(2,1)S(1)}, u32[]{:S(2)}, u32[]{:S(2)}) async-start(bf16[16,96,1024]{2,1,0:T(8,128)(2,1)} %broadcast_in_dim.5), calls=%async_computation | async-start | bytes 6291456 | tf_op jit(solution)/shard_map/all_to_all | solution.py:26
  44.3 26.3 %collective-permute-start.6 = (bf16[256,2048]{1,0:T(8,128)(2,1)}, bf16[256,2048]{1,0:T(8,128)(2,1)S(1)}, u32[]{:S(2)}, u32[]{:S(2)}) collective-permute-start(bf16[256,2048]{1,0:T(8,128)(2,1)} %h0.1), channel_id=1, source_target_pairs={{0,128},{128,0},{1,129},{129,1},{2,130},{130,2},{3,131},{131,3},{4... | collective-permute-start | bytes 3145736 | tf_op jit(solution)/shard_map/ppermute | solution.py:37
  44.5 46.7 %collective-permute-start.9 = (bf16[2048,256]{1,0:T(8,128)(2,1)}, bf16[2048,256]{1,0:T(8,128)(2,1)S(1)}, u32[]{:S(2)}, u32[]{:S(2)}) collective-permute-start(bf16[2048,256]{1,0:T(8,128)(2,1)} %b0.1), channel_id=1, source_target_pairs={{0,128},{128,0},{1,129},{129,1},{2,130},{130,2},{3,131},{131,3},{4... | collective-permute-start | bytes 3145736 | tf_op jit(solution)/shard_map/ppermute | solution.py:37
  46.4 44.8 %collective-permute-start.5 = (bf16[256,2048]{1,0:T(8,128)(2,1)}, bf16[256,2048]{1,0:T(8,128)(2,1)S(1)}, u32[]{:S(2)}, u32[]{:S(2)}) collective-permute-start(bf16[256,2048]{1,0:T(8,128)(2,1)} %h0.1), channel_id=1, source_target_pairs={{0,64},{64,0},{1,65},{65,1},{2,66},{66,2},{3,67},{67,3},{4,68},{68... | collective-permute-start | bytes 3145736 | tf_op jit(solution)/shard_map/ppermute | solution.py:37
  46.4 44.9 %collective-permute-start.8 = (bf16[2048,256]{1,0:T(8,128)(2,1)}, bf16[2048,256]{1,0:T(8,128)(2,1)S(1)}, u32[]{:S(2)}, u32[]{:S(2)}) collective-permute-start(bf16[2048,256]{1,0:T(8,128)(2,1)} %b0.1), channel_id=1, source_target_pairs={{0,64},{64,0},{1,65},{65,1},{2,66},{66,2},{3,67},{67,3},{4,68},{68... | collective-permute-start | bytes 3145736 | tf_op jit(solution)/shard_map/ppermute | solution.py:37
  70.6 20.7 %copy-start = (bf16[256,2048]{1,0:T(8,128)(2,1)}, bf16[256,2048]{1,0:T(8,128)(2,1)S(1)}, u32[]{:S(2)}) copy-start(bf16[256,2048]{1,0:T(8,128)(2,1)S(1)} %collective-permute-done.6.h2) | copy-start | bytes 3145732
  70.6 20.7 %collective-permute-start.7 = (bf16[256,2048]{1,0:T(8,128)(2,1)S(1)}, bf16[256,2048]{1,0:T(8,128)(2,1)S(1)}, u32[]{:S(2)}, u32[]{:S(2)}) collective-permute-start(bf16[256,2048]{1,0:T(8,128)(2,1)S(1)} %collective-permute-done.6.h2), channel_id=1, source_target_pairs={{0,64},{64,0},{1,65},{65,1},{2,66},{66,2},{3,67},{67,3},{4,68},{68... | collective-permute-start | bytes 3145736 | tf_op jit(solution)/shard_map/ppermute | solution.py:37
  91.2 1.0 copy-start.1
  91.2 2.8 %collective-permute-start.10 = (bf16[2048,256]{1,0:T(8,128)(2,1)S(1)}, bf16[2048,256]{1,0:T(8,128)(2,1)}, u32[]{:S(2)}, u32[]{:S(2)}) collective-permute-start(bf16[2048,256]{1,0:T(8,128)(2,1)S(1)} %collective-permute-done.9.b2), channel_id=1, source_target_pairs={{0,64},{64,0},{1,65},{65,1},{2,66},{66,2},{3,67},{67,3},{4,68},{68... | collective-permute-start | bytes 3145736 | tf_op jit(solution)/shard_map/ppermute | solution.py:37
  91.2 1.3 copy-start.2
  91.2 1.6 copy-start.3
  92.9 1.0 copy-start.4
  161.5 6.1 %collective-permute-start.13 = (bf16[200,128]{1,0:T(8,128)(2,1)S(1)}, bf16[200,128]{1,0:T(8,128)(2,1)S(1)}, u32[]{:S(2)}, u32[]{:S(2)}) collective-permute-start(bf16[200,128]{1,0:T(8,128)(2,1)S(1)} %get-tuple-element.6), channel_id=1, source_target_pairs={{0,3},{1,0},{2,1},{3,2},{4,7},{5,4},{6,5},{7,6},{8,11},{9,8},{10,9... | collective-permute-start | bytes 153608 | tf_op jit(solution)/shard_map/ppermute | solution.py:58
  165.1 8.0 %collective-permute-start.11 = (bf16[200,128]{1,0:T(8,128)(2,1)S(1)}, bf16[200,128]{1,0:T(8,128)(2,1)S(1)}, u32[]{:S(2)}, u32[]{:S(2)}) collective-permute-start(bf16[200,128]{1,0:T(8,128)(2,1)S(1)} %get-tuple-element.8), channel_id=1, source_target_pairs={{0,2},{1,3},{2,0},{3,1},{4,6},{5,7},{6,4},{7,5},{8,10},{9,11},{10,... | collective-permute-start | bytes 153608 | tf_op jit(solution)/shard_map/ppermute | solution.py:58
  166.9 7.0 %collective-permute-start.12 = (bf16[200,128]{1,0:T(8,128)(2,1)S(1)}, bf16[200,128]{1,0:T(8,128)(2,1)S(1)}, u32[]{:S(2)}, u32[]{:S(2)}) collective-permute-start(bf16[200,128]{1,0:T(8,128)(2,1)S(1)} %get-tuple-element.9), channel_id=1, source_target_pairs={{0,1},{1,2},{2,3},{3,0},{4,5},{5,6},{6,7},{7,4},{8,9},{9,10},{10,1... | collective-permute-start | bytes 153608 | tf_op jit(solution)/shard_map/ppermute | solution.py:58

commit v10 on v9

--- a/solution.py
+++ b/solution.py
@@ -135,10 +135,9 @@
 
 
 def label_kernel(unit_ref, h0, h1, h2, h3, b0, b1, b2, b3, out_ref, head, back, total, sums, sems):
-    step = pl.program_id(0)
     labels = head.shape[1] // PARTS
-    count = out_ref.shape[0]
-    block = unit_ref.shape[0] // count
+    count = out_ref.shape[0] // STEPS
+    block = unit_ref.shape[0] // out_ref.shape[0]
     narrow = back.shape[1] // PARTS
     pieces = ((h0, h1, h2, h3), (b0, b1, b2, b3))
 
@@ -153,12 +152,18 @@
                 target = back.at[span, q * narrow : (q + 1) * narrow]
             yield pltpu.make_async_copy(source, target, sems.at[kind, part, q])
 
-    @pl.when(step == 0)
-    def _():
-        for part in range(PARTS):
-            for kind in range(2):
-                for copy in copies(kind, part):
-                    copy.start()
+    for part in range(PARTS):
+        for kind in range(2):
+            for copy in copies(kind, part):
+                copy.start()
+
+    @pl.loop(0, STEPS)
+    def _(step):
+        label_step(step, count, block, labels, copies, unit_ref, out_ref, head, back, total, sums)
+
+
+def label_step(step, count, block, labels, copies, unit_ref, out_ref, head, back, total, sums):
+    frames = pl.ds(pl.multiple_of(step * (count * block), 128), count * block)
 
     def arrive(kind, part):
         @pl.when(step == 0)
@@ -169,7 +174,7 @@
     def logits(part):
         arrive(0, part)
         span = slice(part * labels, (part + 1) * labels)
-        return jnp.dot(unit_ref[...], head[:, span], preferred_element_type=F32)
+        return jnp.dot(unit_ref[frames, :], head[:, span], preferred_element_type=F32)
 
     ahead = logits(0)
     lanes = None
@@ -195,13 +200,13 @@
     for s in range(count):
         for j in range(total.shape[1] // 128):
             tile = total[s * block : (s + 1) * block, j * 128 : (j + 1) * 128]
-            out_ref[s, j * block : (j + 1) * block, :] = tile.astype(BF)
+            out_ref[step * count + s, j * block : (j + 1) * block, :] = tile.astype(BF)
         flat = jnp.sum(sums[s * block : s * block + 128, :].T, axis=0, keepdims=True)
         high = flat.astype(BF).astype(F32)
         mid = (flat - high).astype(BF).astype(F32)
         low = flat - high - mid
         split = jnp.where(row == 0, high, jnp.where(row == 1, mid, jnp.where(row == 2, low, 0.0)))
-        out_ref[s, 8 * block :, :] = split.astype(BF)
+        out_ref[step * count + s, 8 * block :, :] = split.astype(BF)
 
 
 def label_sums(unit, head_parts, back_parts):
@@ -213,10 +218,9 @@
     rows = 8 * block + 8
     return pl.pallas_call(
         label_kernel,
-        grid=(STEPS,),
-        in_specs=[pl.BlockSpec((count * block, width), lambda i: (i, 0))]
+        in_specs=[pl.BlockSpec(memory_space=pltpu.VMEM)]
         + [pl.BlockSpec(memory_space=pltpu.HBM)] * 8,
-        out_specs=pl.BlockSpec((count, rows, 128), lambda i: (i, 0, 0)),
+        out_specs=pl.BlockSpec(memory_space=pltpu.VMEM),
         out_shape=jax.ShapeDtypeStruct((slots, rows, 128), BF),
         scratch_shapes=[
             pltpu.VMEM((width, labels), BF),

time: 176 us -> 175 us (level)
  no operation moved by 1% of the time
where the time goes in v10:
time: 175 us
  waiting for transfers between devices  61.9 us (35%)
  blocking collectives  47 us (27%)
  starting transfers between devices  30 us (17%)
  Pallas kernels  28.4 us (16%)
  local copies, waits for them, and re-layouts  5.3 us (3%)
    all_to_all x1, blocking collectives, body(): summed = jnp.sum(lax.all_to_all(sent, PLANE, 0, 0).astype(F32), axis=0)  47 us
    ppermute x6, waiting for transfers between devices, swapped(): return lax.ppermute(block, axis, [(0, 1), (1, 0)])  44.4 us
    pallas_call x1, Pallas kernels, label_sums(): pl.pallas_call(label_kernel, in_specs=[pl.BlockSpec(memory_space=pltpu.VM...  19.7 us
    ppermute x6, starting transfers between devices, turned(): lax.ppermute(block, COL, [(i, (i + distance) % size) for i in range(size)])  15.4 us
    ppermute x6, waiting for transfers between devices, turned(): lax.ppermute(block, COL, [(i, (i + distance) % size) for i in range(size)])  11.5 us
    ppermute x2, starting transfers between devices, passed_along(): return lax.ppermute(block, axes, route)  8.29 us
    pallas_call x1, Pallas kernels, attended(): pl.pallas_call(attention_kernel, in_specs=[pl.BlockSpec(memory_space=pltp...  7.85 us
    ppermute x2, waiting for transfers between devices, passed_along(): return lax.ppermute(block, axes, route)  5.94 us
  transfers between devices with their start and end apart: 15, of which 7 were waited for; matrix products, arithmetic and copies ran while one was open for 0% of the time, Pallas kernels for 0%

profile of v10, /device:TPU:32, one launch (start us, length us, event | category | flops | bytes accessed | tf_op | source)
XLA Modules:
  0.0 175.2 jit_solution(15678537827344945032)
XLA Ops:
  0.6 5.5 %collective-permute-start.1 = (bf16[24,1024]{1,0:T(8,128)(2,1)}, bf16[24,1024]{1,0:T(8,128)(2,1)S(1)}, u32[]{:S(2)}, u32[]{:S(2)}) collective-permute-start(bf16[24,1024]{1,0:T(8,128)(2,1)} %param.5), channel_id=1, source_target_pairs={{0,3},{1,0},{2,1},{3,2},{4,7},{5,4},{6,5},{7,6},{8,11},{9,8},{10,9... | collective-permute-start | bytes 147464 | tf_op jit(solution)/shard_map/ppermute | solution.py:58
  6.1 3.8 %collective-permute-start.2 = (bf16[24,1024]{1,0:T(8,128)(2,1)}, bf16[24,1024]{1,0:T(8,128)(2,1)S(1)}, u32[]{:S(2)}, u32[]{:S(2)}) collective-permute-start(bf16[24,1024]{1,0:T(8,128)(2,1)} %param.5), channel_id=1, source_target_pairs={{0,2},{1,3},{2,0},{3,1},{4,6},{5,7},{6,4},{7,5},{8,10},{9,11},{10,... | collective-permute-start | bytes 147464 | tf_op jit(solution)/shard_map/ppermute | solution.py:58
  9.9 5.2 %collective-permute-done = bf16[24,1024]{1,0:T(8,128)(2,1)S(1)} collective-permute-done((bf16[24,1024]{1,0:T(8,128)(2,1)}, bf16[24,1024]{1,0:T(8,128)(2,1)S(1)}, u32[]{:S(2)}, u32[]{:S(2)}) %collective-permute-start) | collective-permute-done | bytes 49184 | tf_op jit(solution)/shard_map/ppermute | solution.py:58
  15.2 0.8 broadcast_select_fusion.13
  16.0 3.5 %collective-permute-start.4 = (bf16[96,1024]{1,0:T(8,128)(2,1)S(1)}, bf16[96,1024]{1,0:T(8,128)(2,1)S(1)}, u32[]{:S(2)}, u32[]{:S(2)}) collective-permute-start(bf16[96,1024]{1,0:T(8,128)(2,1)S(1)} %pad_maximum_fusion.own_ref), channel_id=1, source_target_pairs={{0,4},{4,8},{8,12},{12,16},{16,20},{20,24},{24,28},{28,32},{32,36}... | collective-permute-start | bytes 589832 | tf_op jit(solution)/shard_map/ppermute | solution.py:33
  19.5 4.8 %collective-permute-start.3 = (bf16[32,1024]{1,0:T(8,128)(2,1)S(1)}, bf16[32,1024]{1,0:T(8,128)(2,1)S(1)}, u32[]{:S(2)}, u32[]{:S(2)}) collective-permute-start(bf16[32,1024]{1,0:T(8,128)(2,1)S(1)} %pad_maximum_fusion.3), channel_id=1, source_target_pairs={{0,8},{4,12},{8,16},{12,20},{16,24},{20,28},{24,32},{28,36},{32,40... | collective-permute-start | bytes 196616 | tf_op jit(solution)/shard_map/ppermute | solution.py:33
  24.3 5.9 %collective-permute-done.3.far_ref = bf16[32,1024]{1,0:T(8,128)(2,1)S(1)} collective-permute-done((bf16[32,1024]{1,0:T(8,128)(2,1)S(1)}, bf16[32,1024]{1,0:T(8,128)(2,1)S(1)}, u32[]{:S(2)}, u32[]{:S(2)}) %collective-permute-start.3) | collective-permute-done | bytes 65568 | tf_op jit(solution)/shard_map/ppermute | solution.py:33
  30.3 7.8 %qkv.1 = bf16[96,1024]{1,0:T(8,128)(2,1)S(1)} custom-call(s32[1]{0:T(128)} %bitcast.1.first_ref, bf16[32,1024]{1,0:T(8,128)(2,1)S(1)} %collective-permute-done.3.far_ref, bf16[96,1024]{1,0:T(8,128)(2,1)S(1)} %collective-permute-done.4.near_ref, bf16[96,1024]{1,0:T(8,128)(2,1)S(1)} %pad_maximum_fusion.own_ref, bf16[1024,3072]{1,0:T(8,128)(2,1)} %qkv_ref.1, ...), custom_call_target="tpu_custom_call" | custom-call | flops 1879048192 | bytes 9437184 | tf_op jit(solution)/shard_map/qkv/pallas_call | solution.py:294
  38.5 2.0 %broadcast_in_dim.5 = bf16[16,96,1024]{2,1,0:T(8,128)(2,1)} broadcast(bf16[96,1024]{1,0:T(8,128)(2,1)S(1)} %pad_maximum_fusion.2), dimensions={1,2} | broadcast | bytes 3342336 | tf_op jit(solution)/shard_map/broadcast_in_dim | solution.py:25
  40.5 3.7 %all-to-all-start = ((bf16[16,96,1024]{2,1,0:T(8,128)(2,1)}), bf16[16,96,1024]{2,1,0:T(8,128)(2,1)S(1)}, u32[]{:S(2)}, u32[]{:S(2)}) async-start(bf16[16,96,1024]{2,1,0:T(8,128)(2,1)} %broadcast_in_dim.5), calls=%async_computation | async-start | bytes 6291456 | tf_op jit(solution)/shard_map/all_to_all | solution.py:26
  44.5 1.9 %collective-permute-start.9 = (bf16[2048,256]{1,0:T(8,128)(2,1)}, bf16[2048,256]{1,0:T(8,128)(2,1)S(1)}, u32[]{:S(2)}, u32[]{:S(2)}) collective-permute-start(bf16[2048,256]{1,0:T(8,128)(2,1)} %b0.1), channel_id=1, source_target_pairs={{0,128},{128,0},{1,129},{129,1},{2,130},{130,2},{3,131},{131,3},{4... | collective-permute-start | bytes 3145736 | tf_op jit(solution)/shard_map/ppermute | solution.py:37
  46.9 23.7 %collective-permute-done.6.h2 = bf16[256,2048]{1,0:T(8,128)(2,1)S(1)} collective-permute-done((bf16[256,2048]{1,0:T(8,128)(2,1)}, bf16[256,2048]{1,0:T(8,128)(2,1)S(1)}, u32[]{:S(2)}, u32[]{:S(2)}) %collective-permute-start.6) | collective-permute-done | bytes 1048608 | tf_op jit(solution)/shard_map/ppermute | solution.py:37
  70.6 20.6 %collective-permute-done.9.b2 = bf16[2048,256]{1,0:T(8,128)(2,1)S(1)} collective-permute-done((bf16[2048,256]{1,0:T(8,128)(2,1)}, bf16[2048,256]{1,0:T(8,128)(2,1)S(1)}, u32[]{:S(2)}, u32[]{:S(2)}) %collective-permute-start.9) | collective-permute-done | bytes 1048608 | tf_op jit(solution)/shard_map/ppermute | solution.py:37
  91.3 1.0 copy-done.1
  92.9 1.0 copy-done.4
  94.0 19.7 %shard_map.68 = bf16[16,776,128]{2,1,0:T(8,128)(2,1)S(1)} custom-call(bf16[1536,1024]{1,0:T(8,128)(2,1)S(1)} %bitcast.19, bf16[256,2048]{1,0:T(8,128)(2,1)} %h0.1, bf16[256,2048]{1,0:T(8,128)(2,1)} %copy-done.2, bf16[256,2048]{1,0:T(8,128)(2,1)} %copy-done, bf16[256,2048]{1,0:T(8,128)(2,1)} %copy-done.4, bf16[2048,256]{1,0:T(8,128)(2,1)} %b0.1, ...), custom_call_target="tpu_custom_call" | custom-call | flops 12884901888 | bytes 16777216 | tf_op jit(solution)/shard_map/pallas_call | solution.py:219
  113.7 47.0 %all_to_all.10 = bf16[16,776,128]{2,1,0:T(8,128)(2,1)S(1)} all-to-all(bf16[16,776,128]{2,1,0:T(8,128)(2,1)S(1)} %shard_map.68), channel_id=1, replica_groups=mesh['zl'=2,'c'=2,'x'=4,'y'=4,'zh'=4] {'x','y'}, dimensions={0} | all-to-all | bytes 6356992 | tf_op jit(solution)/shard_map/all_to_all | solution.py:335
  161.4 3.6 %collective-permute-start.13 = (bf16[200,128]{1,0:T(8,128)(2,1)S(1)}, bf16[200,128]{1,0:T(8,128)(2,1)S(1)}, u32[]{:S(2)}, u32[]{:S(2)}) collective-permute-start(bf16[200,128]{1,0:T(8,128)(2,1)S(1)} %get-tuple-element.6), channel_id=1, source_target_pairs={{0,3},{1,0},{2,1},{3,2},{4,7},{5,4},{6,5},{7,6},{8,11},{9,8},{10,9... | collective-permute-start | bytes 153608 | tf_op jit(solution)/shard_map/ppermute | solution.py:58
  165.0 1.7 collective-permute-start.11
  166.7 0.7 collective-permute-start.12
  167.4 5.6 %collective-permute-done.11.p1 = bf16[200,128]{1,0:T(8,128)(2,1)S(1)} collective-permute-done((bf16[200,128]{1,0:T(8,128)(2,1)S(1)}, bf16[200,128]{1,0:T(8,128)(2,1)S(1)}, u32[]{:S(2)}, u32[]{:S(2)}) %collective-permute-start.11) | collective-permute-done | bytes 51232 | tf_op jit(solution)/shard_map/ppermute | solution.py:58
  173.0 0.8 collective-permute-done.12.p2
  173.8 0.9 shard_map.69
  174.7 0.5 slice_bitcast_fusion
  (41 shorter events, 2.5 us)
Async XLA Ops:
  0.6 9.3 %collective-permute-start.1 = (bf16[24,1024]{1,0:T(8,128)(2,1)}, bf16[24,1024]{1,0:T(8,128)(2,1)S(1)}, u32[]{:S(2)}, u32[]{:S(2)}) collective-permute-start(bf16[24,1024]{1,0:T(8,128)(2,1)} %param.5), channel_id=1, source_target_pairs={{0,3},{1,0},{2,1},{3,2},{4,7},{5,4},{6,5},{7,6},{8,11},{9,8},{10,9... | collective-permute-start | bytes 147464 | tf_op jit(solution)/shard_map/ppermute | solution.py:58
  6.1 9.0 %collective-permute-start = (bf16[24,1024]{1,0:T(8,128)(2,1)}, bf16[24,1024]{1,0:T(8,128)(2,1)S(1)}, u32[]{:S(2)}, u32[]{:S(2)}) collective-permute-start(bf16[24,1024]{1,0:T(8,128)(2,1)} %param.5), channel_id=1, source_target_pairs={{0,1},{1,2},{2,3},{3,0},{4,5},{5,6},{6,7},{7,4},{8,9},{9,10},{10,1... | collective-permute-start | bytes 147464 | tf_op jit(solution)/shard_map/ppermute | solution.py:58
  6.1 9.0 %collective-permute-start.2 = (bf16[24,1024]{1,0:T(8,128)(2,1)}, bf16[24,1024]{1,0:T(8,128)(2,1)S(1)}, u32[]{:S(2)}, u32[]{:S(2)}) collective-permute-start(bf16[24,1024]{1,0:T(8,128)(2,1)} %param.5), channel_id=1, source_target_pairs={{0,2},{1,3},{2,0},{3,1},{4,6},{5,7},{6,4},{7,5},{8,10},{9,11},{10,... | collective-permute-start | bytes 147464 | tf_op jit(solution)/shard_map/ppermute | solution.py:58
  16.0 14.3 %collective-permute-start.4 = (bf16[96,1024]{1,0:T(8,128)(2,1)S(1)}, bf16[96,1024]{1,0:T(8,128)(2,1)S(1)}, u32[]{:S(2)}, u32[]{:S(2)}) collective-permute-start(bf16[96,1024]{1,0:T(8,128)(2,1)S(1)} %pad_maximum_fusion.own_ref), channel_id=1, source_target_pairs={{0,4},{4,8},{8,12},{12,16},{16,20},{20,24},{24,28},{28,32},{32,36}... | collective-permute-start | bytes 589832 | tf_op jit(solution)/shard_map/ppermute | solution.py:33
  19.5 10.8 %collective-permute-start.3 = (bf16[32,1024]{1,0:T(8,128)(2,1)S(1)}, bf16[32,1024]{1,0:T(8,128)(2,1)S(1)}, u32[]{:S(2)}, u32[]{:S(2)}) collective-permute-start(bf16[32,1024]{1,0:T(8,128)(2,1)S(1)} %pad_maximum_fusion.3), channel_id=1, source_target_pairs={{0,8},{4,12},{8,16},{12,20},{16,24},{20,28},{24,32},{28,36},{32,40... | collective-permute-start | bytes 196616 | tf_op jit(solution)/shard_map/ppermute | solution.py:33
  40.5 53.5 %all-to-all-start = ((bf16[16,96,1024]{2,1,0:T(8,128)(2,1)}), bf16[16,96,1024]{2,1,0:T(8,128)(2,1)S(1)}, u32[]{:S(2)}, u32[]{:S(2)}) async-start(bf16[16,96,1024]{2,1,0:T(8,128)(2,1)} %broadcast_in_dim.5), calls=%async_computation | async-start | bytes 6291456 | tf_op jit(solution)/shard_map/all_to_all | solution.py:26
  44.3 26.3 %collective-permute-start.6 = (bf16[256,2048]{1,0:T(8,128)(2,1)}, bf16[256,2048]{1,0:T(8,128)(2,1)S(1)}, u32[]{:S(2)}, u32[]{:S(2)}) collective-permute-start(bf16[256,2048]{1,0:T(8,128)(2,1)} %h0.1), channel_id=1, source_target_pairs={{0,128},{128,0},{1,129},{129,1},{2,130},{130,2},{3,131},{131,3},{4... | collective-permute-start | bytes 3145736 | tf_op jit(solution)/shard_map/ppermute | solution.py:37
  44.5 46.7 %collective-permute-start.9 = (bf16[2048,256]{1,0:T(8,128)(2,1)}, bf16[2048,256]{1,0:T(8,128)(2,1)S(1)}, u32[]{:S(2)}, u32[]{:S(2)}) collective-permute-start(bf16[2048,256]{1,0:T(8,128)(2,1)} %b0.1), channel_id=1, source_target_pairs={{0,128},{128,0},{1,129},{129,1},{2,130},{130,2},{3,131},{131,3},{4... | collective-permute-start | bytes 3145736 | tf_op jit(solution)/shard_map/ppermute | solution.py:37
  46.4 44.8 %collective-permute-start.5 = (bf16[256,2048]{1,0:T(8,128)(2,1)}, bf16[256,2048]{1,0:T(8,128)(2,1)S(1)}, u32[]{:S(2)}, u32[]{:S(2)}) collective-permute-start(bf16[256,2048]{1,0:T(8,128)(2,1)} %h0.1), channel_id=1, source_target_pairs={{0,64},{64,0},{1,65},{65,1},{2,66},{66,2},{3,67},{67,3},{4,68},{68... | collective-permute-start | bytes 3145736 | tf_op jit(solution)/shard_map/ppermute | solution.py:37
  46.4 44.9 %collective-permute-start.8 = (bf16[2048,256]{1,0:T(8,128)(2,1)}, bf16[2048,256]{1,0:T(8,128)(2,1)S(1)}, u32[]{:S(2)}, u32[]{:S(2)}) collective-permute-start(bf16[2048,256]{1,0:T(8,128)(2,1)} %b0.1), channel_id=1, source_target_pairs={{0,64},{64,0},{1,65},{65,1},{2,66},{66,2},{3,67},{67,3},{4,68},{68... | collective-permute-start | bytes 3145736 | tf_op jit(solution)/shard_map/ppermute | solution.py:37
  70.6 20.7 %copy-start = (bf16[256,2048]{1,0:T(8,128)(2,1)}, bf16[256,2048]{1,0:T(8,128)(2,1)S(1)}, u32[]{:S(2)}) copy-start(bf16[256,2048]{1,0:T(8,128)(2,1)S(1)} %collective-permute-done.6.h2) | copy-start | bytes 3145732
  70.6 20.7 %collective-permute-start.7 = (bf16[256,2048]{1,0:T(8,128)(2,1)S(1)}, bf16[256,2048]{1,0:T(8,128)(2,1)S(1)}, u32[]{:S(2)}, u32[]{:S(2)}) collective-permute-start(bf16[256,2048]{1,0:T(8,128)(2,1)S(1)} %collective-permute-done.6.h2), channel_id=1, source_target_pairs={{0,64},{64,0},{1,65},{65,1},{2,66},{66,2},{3,67},{67,3},{4,68},{68... | collective-permute-start | bytes 3145736 | tf_op jit(solution)/shard_map/ppermute | solution.py:37
  91.2 1.0 copy-start.1
  91.2 2.8 %collective-permute-start.10 = (bf16[2048,256]{1,0:T(8,128)(2,1)S(1)}, bf16[2048,256]{1,0:T(8,128)(2,1)}, u32[]{:S(2)}, u32[]{:S(2)}) collective-permute-start(bf16[2048,256]{1,0:T(8,128)(2,1)S(1)} %collective-permute-done.9.b2), channel_id=1, source_target_pairs={{0,64},{64,0},{1,65},{65,1},{2,66},{66,2},{3,67},{67,3},{4,68},{68... | collective-permute-start | bytes 3145736 | tf_op jit(solution)/shard_map/ppermute | solution.py:37
  91.2 1.3 copy-start.2
  91.2 1.6 copy-start.3
  92.9 1.0 copy-start.4
  161.4 6.1 %collective-permute-start.13 = (bf16[200,128]{1,0:T(8,128)(2,1)S(1)}, bf16[200,128]{1,0:T(8,128)(2,1)S(1)}, u32[]{:S(2)}, u32[]{:S(2)}) collective-permute-start(bf16[200,128]{1,0:T(8,128)(2,1)S(1)} %get-tuple-element.6), channel_id=1, source_target_pairs={{0,3},{1,0},{2,1},{3,2},{4,7},{5,4},{6,5},{7,6},{8,11},{9,8},{10,9... | collective-permute-start | bytes 153608 | tf_op jit(solution)/shard_map/ppermute | solution.py:58
  165.0 8.0 %collective-permute-start.11 = (bf16[200,128]{1,0:T(8,128)(2,1)S(1)}, bf16[200,128]{1,0:T(8,128)(2,1)S(1)}, u32[]{:S(2)}, u32[]{:S(2)}) collective-permute-start(bf16[200,128]{1,0:T(8,128)(2,1)S(1)} %get-tuple-element.8), channel_id=1, source_target_pairs={{0,2},{1,3},{2,0},{3,1},{4,6},{5,7},{6,4},{7,5},{8,10},{9,11},{10,... | collective-permute-start | bytes 153608 | tf_op jit(solution)/shard_map/ppermute | solution.py:58
  166.7 7.0 %collective-permute-start.12 = (bf16[200,128]{1,0:T(8,128)(2,1)S(1)}, bf16[200,128]{1,0:T(8,128)(2,1)S(1)}, u32[]{:S(2)}, u32[]{:S(2)}) collective-permute-start(bf16[200,128]{1,0:T(8,128)(2,1)S(1)} %get-tuple-element.9), channel_id=1, source_target_pairs={{0,1},{1,2},{2,3},{3,0},{4,5},{5,6},{6,7},{7,4},{8,9},{9,10},{10,1... | collective-permute-start | bytes 153608 | tf_op jit(solution)/shard_map/ppermute | solution.py:58
